TPU v7x, 512 devices: a whole 4x8x8 slice. The times are simulated.
512 devices in a mesh: dp: 16 (over y_lo, x, core), expert: 4 (over y_hi), tensor: 8 (over z).
Axes of the slice: x: 4, y: 8 (y_hi: 4, y_lo: 2; y = y_hi * 2 + y_lo), z: 8, core: 2. Of those that a mesh axis runs over, the one named last changes fastest.
Arguments:
- tokens: bfloat16 [1792, 4096], P(('dp', 'expert'), 'tensor'), may hold values from -6 to 6
- route_ids: int32 [1792, 2], P(('dp', 'expert')), may hold values from 0 to 3, all different within a row; in each aligned block of 28 rows (0 to 27, 28 to 55, ...) at most 17 rows name the same one
- route_gates: float32 [1792, 2], P(('dp', 'expert')), may hold values from 0.2 to 1
- d_out: bfloat16 [1792, 4096], P(('dp', 'expert'), 'tensor'), may hold values from -6 to 6
- gate_saved: bfloat16 [4, 4096, 8192], P(None, 'tensor', ('dp', 'expert')), may hold values from -0.09375 to 0.09375
- up_saved: bfloat16 [4, 4096, 8192], P(None, 'tensor', ('dp', 'expert')), may hold values from -0.09375 to 0.09375
- down_saved: bfloat16 [4, 4096, 8192], P(None, 'tensor', ('dp', 'expert')), may hold values from -0.0625 to 0.0625
Outputs:
- out: bfloat16 [1792, 4096], P(('dp', 'expert'), 'tensor')
- d_tokens: bfloat16 [1792, 4096], P(('dp', 'expert'), 'tensor')
- grad_gate: bfloat16 [4, 4096, 8192], P('expert', 'tensor', 'dp')
- grad_up: bfloat16 [4, 4096, 8192], P('expert', 'tensor', 'dp')
- grad_down: bfloat16 [4, 4096, 8192], P('expert', 'tensor', 'dp')
Inputs may be any that keep to these rules, and one draw needn't show every extreme that they name: `route_ids`: each token names two different experts. Among the 28 tokens of one aligned block of the token dimension no expert is named more than 17 times, and in some block one expert is named exactly 17 times.
All inputs are finite; a program needn't handle non-finite values.
Results may differ from a plain program's by a relative error of at most 0.028.
Values may be sent and summed in bfloat16 or wider, within the bound.
No kernel may reach another device: no remote copies, remote signals or barrier semaphores. Data moves between devices by JAX's collectives and lax.ppermute only.
A program may use at most 64 MiB of HBM per device.

v0:
```python
import jax
import jax.numpy as jnp
from jax import lax
from jax.sharding import PartitionSpec as P


def sent_together(arrays, axis, split_dim, concat_dim, along):
    ends, at = ([], 0)
    for a in arrays[:-1]:
        at += a.shape[along]
        ends.append(at)
    both = jnp.concatenate(arrays, axis=along)
    return tuple(
        jnp.split(
            lax.all_to_all(both, axis, split_axis=split_dim, concat_axis=concat_dim, tiled=True),
            ends,
            axis=along,
        )
    )


def side_by_side(arrays, axis, dim, along):
    widths = [a.shape[along] for a in arrays]
    both = jnp.concatenate(arrays, axis=along)
    filled = lax.all_gather(both, axis, axis=dim, tiled=True)
    return tuple(jnp.split(filled, [sum(widths[:k]) for k in range(1, len(widths))], axis=along))


def in_one_piece(arrays, axis, dim, along):
    ends, at = ([], 0)
    for a in arrays[:-1]:
        at += a.shape[along]
        ends.append(at)
    both = jnp.concatenate(arrays, axis=along)
    return tuple(
        jnp.split(lax.psum_scatter(both, axis, scatter_dimension=dim, tiled=True), ends, axis=along)
    )


def cut_along(x, dim, size):
    lengths = x.shape
    tiles = x.reshape(*lengths[:dim], size, lengths[dim] // size, *lengths[dim + 1 :])
    return jnp.moveaxis(tiles, dim, 0)


def summed_on_arrival(x, axis, dim):
    tiles = cut_along(x, dim, lax.axis_size(axis))
    arrived = lax.all_to_all(tiles, axis, split_axis=0, concat_axis=0, tiled=True)
    return arrived.astype(jnp.float32).sum(axis=0)


def side_by_side_2(arrays, axis, dim, along):
    ends, at = ([], 0)
    for a in arrays[:-1]:
        at += a.shape[along]
        ends.append(at)
    both = jnp.concatenate(arrays, axis=along)
    return tuple(jnp.split(summed_on_arrival(both, axis, dim), ends, axis=along))


def swiglu_pair(gate_sum, up_sum, back_sum):
    sigmoid_gate = jax.nn.sigmoid(gate_sum)
    silu_gate = gate_sum * sigmoid_gate
    hidden = (silu_gate * up_sum).astype(jnp.bfloat16)
    d_up = (back_sum * silu_gate).astype(jnp.bfloat16)
    d_gate = (back_sum * up_sum * sigmoid_gate * (1.0 + gate_sum * (1.0 - sigmoid_gate))).astype(
        jnp.bfloat16
    )
    return (hidden, d_gate, d_up)


def contract_rows(left_side, right_side):
    return lax.dot_general(
        left_side, right_side, (((0,), (0,)), ((), ())), preferred_element_type=jnp.float32
    )


def contract_last(left_side, right_side):
    return lax.dot_general(
        left_side, right_side, (((1,), (1,)), ((), ())), preferred_element_type=jnp.float32
    )


def spread_back(weights, values):
    return lax.dot_general(
        weights,
        values,
        (((0,), (0,)), ((), ())),
        precision=lax.Precision.HIGHEST,
        preferred_element_type=jnp.float32,
    )


def local(tokens, route_ids, route_gates, d_out, gate_saved, up_saved, down_saved):
    relaid = sent_together((gate_saved, up_saved, down_saved), "expert", 0, 2, 1)
    w_gate = relaid[0][0]
    w_up = relaid[1][0]
    w_down = relaid[2][0]
    experts = lax.axis_size("expert")
    tok_count = tokens.shape[0]
    capacity = 5 * tok_count // 8
    feature_width = tokens.shape[1]
    onehot = (route_ids[:, :, None] == jnp.arange(experts, dtype=jnp.int32)).astype(jnp.int32)
    flat_hits = onehot.reshape(tok_count * 2, experts)
    before = jnp.cumsum(flat_hits, axis=0) - flat_hits
    slot_index = jnp.sum(before * flat_hits, axis=1).reshape(tok_count, 2)
    target = route_ids * capacity + slot_index
    matches = jnp.arange(experts * capacity, dtype=jnp.int32)[:, None, None] == target[None]
    placer = jnp.sum(matches.astype(jnp.float32), axis=2)
    weighted = jnp.sum(jnp.where(matches, route_gates[None], 0.0), axis=2)
    send_rows = jnp.dot(placer.astype(jnp.bfloat16), tokens, preferred_element_type=jnp.float32)
    send_rows = send_rows.astype(jnp.bfloat16).reshape(experts, capacity, feature_width)
    send_grads = jnp.dot(
        weighted,
        d_out.astype(jnp.float32),
        precision=lax.Precision.HIGHEST,
        preferred_element_type=jnp.float32,
    )
    send_grads = send_grads.astype(jnp.bfloat16).reshape(experts, capacity, feature_width)
    arrived = sent_together((send_rows, send_grads), "expert", 0, 0, 1)
    collected = side_by_side((arrived[0], arrived[1]), "dp", 0, 1)
    rows_x = collected[0].reshape(-1, feature_width)
    rows_dy = collected[1].reshape(-1, feature_width)
    gate_part = jnp.dot(rows_x, w_gate, preferred_element_type=jnp.float32)
    up_part = jnp.dot(rows_x, w_up, preferred_element_type=jnp.float32)
    back_part = jnp.dot(rows_dy, w_down, preferred_element_type=jnp.float32)
    shares = tuple(
        (
            part.astype(jnp.float32)
            for part in in_one_piece(
                (
                    gate_part.astype(jnp.bfloat16),
                    up_part.astype(jnp.bfloat16),
                    back_part.astype(jnp.bfloat16),
                ),
                "tensor",
                0,
                1,
            )
        )
    )
    pieces = swiglu_pair(shares[0], shares[1], shares[2])
    joined = side_by_side((pieces[0], pieces[1], pieces[2]), "tensor", 0, 1)
    hidden = joined[0]
    d_gate = joined[1]
    d_up = joined[2]
    out_part = contract_last(hidden, w_down)
    dx_part = contract_last(d_gate, w_gate) + contract_last(d_up, w_up)
    own_sums = side_by_side_2(
        (out_part.astype(jnp.bfloat16), dx_part.astype(jnp.bfloat16)), "dp", 0, 1
    )
    grad_gate = contract_rows(rows_x, d_gate).astype(jnp.bfloat16)[None]
    grad_up = contract_rows(rows_x, d_up).astype(jnp.bfloat16)[None]
    grad_down = contract_rows(rows_dy, hidden).astype(jnp.bfloat16)[None]
    back_rows = own_sums[0].astype(jnp.bfloat16).reshape(experts, capacity, feature_width)
    back_grads = own_sums[1].astype(jnp.bfloat16).reshape(experts, capacity, feature_width)
    returned = sent_together((back_rows, back_grads), "expert", 0, 0, 1)
    result_rows = returned[0].reshape(experts * capacity, feature_width).astype(jnp.float32)
    result_grads = returned[1].reshape(experts * capacity, feature_width).astype(jnp.float32)
    out = spread_back(weighted, result_rows).astype(jnp.bfloat16)
    d_tokens = spread_back(placer, result_grads).astype(jnp.bfloat16)
    return (out, d_tokens, grad_gate, grad_up, grad_down)


def solution(mesh):
    in_specs = (
        P(("dp", "expert"), "tensor"),
        P(("dp", "expert"), None),
        P(("dp", "expert"), None),
        P(("dp", "expert"), "tensor"),
        P(None, "tensor", ("dp", "expert")),
        P(None, "tensor", ("dp", "expert")),
        P(None, "tensor", ("dp", "expert")),
    )
    out_specs = (
        P(("dp", "expert"), "tensor"),
        P(("dp", "expert"), "tensor"),
        P("expert", "tensor", "dp"),
        P("expert", "tensor", "dp"),
        P("expert", "tensor", "dp"),
    )
    return jax.shard_map(local, mesh=mesh, in_specs=in_specs, out_specs=out_specs, check_vma=False)
```

profile of v0, /device:TPU:6, one launch (start us, length us, event | category | flops | bytes accessed | tf_op | source)
XLA Modules:
  0.0 274.8 jit_solution(13261205111525313573)
XLA Ops:
  7.2 0.9 copy.37
  8.1 0.1 eq.30
  8.3 0.1 reduce_window_sum.11
  8.4 0.2 select_reduce_fusion.1
  8.5 0.1 reshape.46
  8.7 0.1 copy.38
  8.7 0.7 multiply_add_fusion
  9.4 0.1 copy.39
  9.5 0.8 copy.40
  10.3 0.1 convert_reduce_fusion
  10.5 0.3 convolution_convert_fusion.7
  10.8 0.9 convolution_convert_fusion.8
  11.8 16.6 %all_to_all.33 = bf16[4,34,512]{2,1,0:T(8,128)(2,1)} all-to-all(bf16[4,34,512]{2,1,0:T(8,128)(2,1)S(1)} %pad_maximum_fusion.4), channel_id=1, replica_groups=mesh['dp'=16,'expert'=4,'tensor'=8] {'expert'}, dimensions={0} | all-to-all | bytes 278528 | tf_op jit(solution)/shard_map/all_to_all | solution.py:15
  28.5 0.2 copy.43
  28.7 0.2 copy.42
  29.0 0.2 copy.41
  29.2 1.3 pad_maximum_fusion.2
  30.5 4.3 %all-to-all-start.1 = ((bf16[4,1536,128]{1,2,0:T(8,128)(2,1)}), bf16[4,1536,128]{1,2,0:T(8,128)(2,1)}, u32[]{:S(2)}, u32[]{:S(2)}) async-start(bf16[4,1536,128]{1,2,0:T(8,128)(2,1)} %pad_maximum_fusion.2), calls=%async_computation.1 | async-start | bytes 3145728 | tf_op jit(solution)/shard_map/all_to_all | solution.py:15
  34.8 47.3 %all-gather.3.cloned.1.call-done = bf16[64,34,512]{2,1,0:T(8,128)(2,1)} async-done(((bf16[4,34,512]{2,1,0:T(8,128)(2,1)}), bf16[64,34,512]{2,1,0:T(8,128)(2,1)}) %all-gather.3.cloned.1.call-update) | async-done | bytes 2228240 | tf_op jit(solution)/shard_map/all_gather | solution.py:25
  82.1 2.7 fusion.22
  84.8 1.2 reshape.49
  86.1 2.2 convolution_convert_fusion.2
  88.3 2.8 %convolution_convert_fusion.3 = bf16[1088,512]{1,0:T(8,128)(2,1)} fusion(bf16[1088,512]{1,0:T(8,128)(2,1)S(1)} %copy-done.4, bf16[1,1536,512]{1,2,0:T(8,128)(2,1)} %bitcast.2), kind=kOutput, calls=%fused_computation.6 | convolution fusion | flops 570982400 | bytes 2752512 | tf_op jit(solution)/shard_map/dot_general | solution.py:124
  91.1 1.2 reshape.50
  92.4 2.2 convolution_convert_fusion.1
  94.6 1.8 pad_maximum_fusion
  96.5 53.1 %reduce-scatter.2.cloned.1.call-done = bf16[136,1536]{1,0:T(8,128)(2,1)} async-done(((bf16[1088,1536]{1,0:T(8,128)(2,1)}), bf16[136,1536]{1,0:T(8,128)(2,1)}) %reduce-scatter.2.cloned.1.call-update) | async-done | bytes 417808 | tf_op jit(solution)/shard_map/reduce_scatter | solution.py:36
  149.6 1.2 fusion.11
  150.8 0.8 pad_maximum_fusion.3
  151.6 49.6 %all-gather.5.cloned.1.call-done = bf16[1088,1536]{1,0:T(8,128)(2,1)} async-done(((bf16[136,1536]{1,0:T(8,128)(2,1)}), bf16[1088,1536]{1,0:T(8,128)(2,1)}) %all-gather.5.cloned.1.call-update) | async-done | bytes 3342352 | tf_op jit(solution)/shard_map/all_gather | solution.py:25
  201.2 2.3 fusion.7
  203.5 0.2 copy-done.1
  203.7 1.8 convolution_convert_fusion
  205.5 1.8 fusion
  207.2 0.3 pad_maximum_fusion.1
  207.5 2.1 reshape.51
  209.6 5.9 %all-to-all-start.2 = ((bf16[16,68,1024]{2,1,0:T(8,128)(2,1)}), bf16[16,68,1024]{2,1,0:T(8,128)(2,1)S(1)}, u32[]{:S(2)}, u32[]{:S(2)}) async-start(bf16[16,68,1024]{2,1,0:T(8,128)(2,1)} %reshape.51), calls=%async_computation.3 | async-start | bytes 4718592 | tf_op jit(solution)/shard_map/all_to_all | solution.py:48
  215.5 2.9 %fusion.1 = bf16[1,512,512]{2,1,0:T(8,128)(2,1)} fusion(bf16[1088,512]{1,0:T(8,128)(2,1)S(1)} %copy-done.5, bf16[1088,1536]{1,0:T(8,128)(2,1)} %all-gather.5.cloned.1.call-done), kind=kOutput, calls=%fused_computation.12 | convolution fusion | flops 570687488 | bytes 2752512 | tf_op jit(solution)/shard_map/dot_general | solution.py:73
  218.4 2.9 %fusion.2 = bf16[1,512,512]{2,1,0:T(8,128)(2,1)} fusion(bf16[1088,512]{1,0:T(8,128)(2,1)S(1)} %copy-done.5, bf16[1088,1536]{1,0:T(8,128)(2,1)} %all-gather.5.cloned.1.call-done), kind=kOutput, calls=%fused_computation.13 | convolution fusion | flops 570687488 | bytes 2752512 | tf_op jit(solution)/shard_map/dot_general | solution.py:73
  221.3 26.9 %all-to-all-done.2 = bf16[16,68,1024]{2,1,0:T(8,128)(2,1)S(1)} async-done(((bf16[16,68,1024]{2,1,0:T(8,128)(2,1)}), bf16[16,68,1024]{2,1,0:T(8,128)(2,1)S(1)}, u32[]{:S(2)}, u32[]{:S(2)}) %all-to-all-start.2) | async-done | bytes 2228256 | tf_op jit(solution)/shard_map/all_to_all | solution.py:48
  248.2 1.2 reduce
  249.4 0.9 fusion.24
  250.4 0.7 pad_maximum_fusion.5
  251.1 5.8 %all-to-all-start.3 = ((bf16[4,34,512]{2,1,0:T(8,128)(2,1)}), bf16[4,34,512]{2,1,0:T(8,128)(2,1)S(1)}, u32[]{:S(2)}, u32[]{:S(2)}) async-start(bf16[4,34,512]{2,1,0:T(8,128)(2,1)} %pad_maximum_fusion.5), calls=%async_computation.4 | async-start | bytes 327680 | tf_op jit(solution)/shard_map/all_to_all | solution.py:15
  256.9 2.9 %fusion.3 = bf16[1,512,512]{2,1,0:T(8,128)(2,1)} fusion(bf16[1088,512]{1,0:T(8,128)(2,1)S(1)} %copy-done.3, bf16[1088,1536]{1,0:T(8,128)(2,1)} %all-gather.5.cloned.1.call-done), kind=kOutput, calls=%fused_computation.14 | convolution fusion | flops 570687488 | bytes 2752512 | tf_op jit(solution)/shard_map/dot_general | solution.py:73
  259.8 6.7 %all-to-all-done.3 = bf16[4,34,512]{2,1,0:T(8,128)(2,1)S(1)} async-done(((bf16[4,34,512]{2,1,0:T(8,128)(2,1)}), bf16[4,34,512]{2,1,0:T(8,128)(2,1)S(1)}, u32[]{:S(2)}, u32[]{:S(2)}) %all-to-all-start.3) | async-done | bytes 139296 | tf_op jit(solution)/shard_map/all_to_all | solution.py:15
  266.7 0.8 convolution_convert_fusion.10
  267.5 0.8 convolution_convert_fusion.9
  (33 shorter events, 0.5 us)
Async XLA Ops:
  7.2 3.3 %copy-start = (bf16[28,512]{1,0:T(8,128)(2,1)S(1)}, bf16[28,512]{1,0:T(8,128)(2,1)}, u32[]{:S(2)}) copy-start(bf16[28,512]{1,0:T(8,128)(2,1)} %param.10) | copy-start | bytes 86020
  7.2 21.3 %copy-start.6 = (bf16[4,512,128]{2,1,0:T(8,128)(2,1)S(1)}, bf16[4,512,128]{2,1,0:T(8,128)(2,1)}, u32[]{:S(2)}) copy-start(bf16[4,512,128]{2,1,0:T(8,128)(2,1)} %param.13) | copy-start | bytes 1572868
  7.2 21.5 %copy-start.7 = (bf16[4,512,128]{2,1,0:T(8,128)(2,1)S(1)}, bf16[4,512,128]{2,1,0:T(8,128)(2,1)}, u32[]{:S(2)}) copy-start(bf16[4,512,128]{2,1,0:T(8,128)(2,1)} %param.12) | copy-start | bytes 1572868
  7.2 74.9 %all-gather.3.cloned.1.call-start = ((), (), s32[]{:S(2)}) async-start(), calls=%async_computation.5 | async-start | bytes 2785280 | tf_op jit(solution)/shard_map/all_gather | solution.py:25
  11.7 17.2 %copy-start.8 = (bf16[4,512,128]{2,1,0:T(8,128)(2,1)S(1)}, bf16[4,512,128]{2,1,0:T(8,128)(2,1)}, u32[]{:S(2)}) copy-start(bf16[4,512,128]{2,1,0:T(8,128)(2,1)} %param.11) | copy-start | bytes 1572868
  30.5 55.6 %all-to-all-start.1 = ((bf16[4,1536,128]{1,2,0:T(8,128)(2,1)}), bf16[4,1536,128]{1,2,0:T(8,128)(2,1)}, u32[]{:S(2)}, u32[]{:S(2)}) async-start(bf16[4,1536,128]{1,2,0:T(8,128)(2,1)} %pad_maximum_fusion.2), calls=%async_computation.1 | async-start | bytes 3145728 | tf_op jit(solution)/shard_map/all_to_all | solution.py:15
  34.8 114.8 %reduce-scatter.2.cloned.1.call-start = ((), (), s32[]{:S(2)}) async-start(), calls=%async_computation.6 | async-start | bytes 3760128 | tf_op jit(solution)/shard_map/reduce_scatter | solution.py:36
  86.0 2.3 copy-start.4
  92.4 2.3 copy-start.2
  96.5 104.7 %all-gather.5.cloned.1.call-start = ((), (), s32[]{:S(2)}) async-start(), calls=%async_computation.7 | async-start | bytes 3760128 | tf_op jit(solution)/shard_map/all_gather | solution.py:25
  201.2 2.5 copy-start.1
  209.6 5.9 %copy-start.5 = (bf16[1088,512]{1,0:T(8,128)(2,1)S(1)}, bf16[1088,512]{1,0:T(8,128)(2,1)}, u32[]{:S(2)}) copy-start(bf16[1088,512]{1,0:T(8,128)(2,1)} %reshape.49) | copy-start | bytes 3342340
  209.6 38.6 %all-to-all-start.2 = ((bf16[16,68,1024]{2,1,0:T(8,128)(2,1)}), bf16[16,68,1024]{2,1,0:T(8,128)(2,1)S(1)}, u32[]{:S(2)}, u32[]{:S(2)}) async-start(bf16[16,68,1024]{2,1,0:T(8,128)(2,1)} %reshape.51), calls=%async_computation.3 | async-start | bytes 4718592 | tf_op jit(solution)/shard_map/all_to_all | solution.py:48
  221.3 35.6 %copy-start.3 = (bf16[1088,512]{1,0:T(8,128)(2,1)S(1)}, bf16[1088,512]{1,0:T(8,128)(2,1)}, u32[]{:S(2)}) copy-start(bf16[1088,512]{1,0:T(8,128)(2,1)} %reshape.50) | copy-start | bytes 3342340
  251.1 15.5 %all-to-all-start.3 = ((bf16[4,34,512]{2,1,0:T(8,128)(2,1)}), bf16[4,34,512]{2,1,0:T(8,128)(2,1)S(1)}, u32[]{:S(2)}, u32[]{:S(2)}) async-start(bf16[4,34,512]{2,1,0:T(8,128)(2,1)} %pad_maximum_fusion.5), calls=%async_computation.4 | async-start | bytes 327680 | tf_op jit(solution)/shard_map/all_to_all | solution.py:15
Sparse Core Ops, SparseCore 0:
  28.6 53.4 all-gather.2
  96.6 52.9 reduce-scatter.1
  152.3 48.9 all-gather.4
where the time goes:
time: 276 us; the launch traced here: 275 us
  waiting for transfers between devices  184 us (67%)
  matrix products  24.6 us (9%)
  blocking collectives  16.6 us (6%)
  starting transfers between devices  16.2 us (6%)
  between operations  14 us (5%)
  local copies, waits for them, and re-layouts  11.3 us (4%)
  other arithmetic  8.46 us (3%)
    all_gather x2, waiting for transfers between devices, side_by_side(): filled = lax.all_gather(both, axis, axis=dim, tiled=True)  96.9 us
    reduce_scatter x1, waiting for transfers between devices, in_one_piece(): lax.psum_scatter(both, axis, scatter_dimension=dim, tiled=True)  53.1 us
    all_to_all x1, waiting for transfers between devices, summed_on_arrival(): lax.all_to_all(tiles, axis, split_axis=0, concat_axis=0, tiled=True)  26.9 us
    all_to_all x1, blocking collectives, sent_together(): lax.all_to_all(both, axis, split_axis=split_dim, concat_axis=concat_dim,...  16.6 us
    all_to_all x2, starting transfers between devices, sent_together(): lax.all_to_all(both, axis, split_axis=split_dim, concat_axis=concat_dim,...  10.2 us
    dot_general x3, matrix products, contract_rows(): lax.dot_general(left_side, right_side, (((0,), (0,)), ((), ())), preferre...  8.73 us
    all_to_all x2, waiting for transfers between devices, sent_together(): lax.all_to_all(both, axis, split_axis=split_dim, concat_axis=concat_dim,...  6.75 us
    all_to_all x1, starting transfers between devices, summed_on_arrival(): lax.all_to_all(tiles, axis, split_axis=0, concat_axis=0, tiled=True)  5.87 us
  transfers between devices with their start and end apart: 6, of which 5 were waited for; matrix products, arithmetic and copies ran while one was open for 5% of the time, Pallas kernels for 0%

commit v1 on v0

v1 whole, which is shorter than its diff:
```python
import functools

import jax
import jax.numpy as jnp
from jax import lax
from jax.experimental import pallas as pl
from jax.experimental.pallas import tpu as pltpu
from jax.sharding import Mesh, PartitionSpec as P


CHIPS = ("ylo", "x")
BF16 = jnp.bfloat16
F32 = jnp.float32


def place_of(ids_row, expert, slots):
    tokens = ids_row.shape[1]
    hits = jnp.sum((ids_row == expert).astype(F32), axis=0, keepdims=True)
    earlier = (
        lax.broadcasted_iota(jnp.int32, (tokens, tokens), 0)
        < lax.broadcasted_iota(jnp.int32, (tokens, tokens), 1)
    ).astype(F32)
    before = jnp.dot(
        jnp.broadcast_to(hits, (8, tokens)), earlier, preferred_element_type=F32
    )[:1].astype(jnp.int32)
    slot = lax.broadcasted_iota(jnp.int32, (slots, tokens), 0)
    return jnp.where((slot == before) & (hits > 0.5), 1.0, 0.0).astype(F32)


def send_kernel(ids_ref, gates_ref, tok_ref, dout_ref, out_ref):
    experts, slots = out_ref.shape[0] // 2, out_ref.shape[1]
    ids, gates = ids_ref[...], gates_ref[...]
    for e in range(experts):
        place = place_of(ids, e, slots)
        gate_row = jnp.sum(jnp.where(ids == e, gates, 0.0), axis=0, keepdims=True)
        gate_slot = jnp.sum(place * gate_row, axis=1, keepdims=True)
        pick = place.astype(BF16)
        out_ref[e] = jnp.dot(pick, tok_ref[...], preferred_element_type=F32).astype(BF16)
        grads = jnp.dot(pick, dout_ref[...], preferred_element_type=F32)
        out_ref[experts + e] = (gate_slot * grads).astype(BF16)


def finish_kernel(ids_ref, gates_ref, back_ref, out_ref, dtok_ref):
    experts, slots = back_ref.shape[0] // 2, back_ref.shape[1]
    ids, gates = ids_ref[...], gates_ref[...]
    tokens = ids.shape[1]
    eye = lax.broadcasted_iota(jnp.int32, (tokens, tokens), 0) == lax.broadcasted_iota(
        jnp.int32, (tokens, tokens), 1
    )
    out = jnp.zeros(out_ref.shape, F32)
    dtok = jnp.zeros(dtok_ref.shape, F32)
    for e in range(experts):
        pick = place_of(ids, e, slots).astype(BF16)
        gate_row = jnp.sum(jnp.where(ids == e, gates, 0.0), axis=0, keepdims=True)
        gate_col = jnp.sum(jnp.where(eye, gate_row, 0.0), axis=1, keepdims=True)
        spread = functools.partial(
            lax.dot_general,
            pick,
            dimension_numbers=(((0,), (0,)), ((), ())),
            preferred_element_type=F32,
        )
        out += gate_col * spread(back_ref[e])
        dtok += spread(back_ref[experts + e])
    out_ref[...] = out.astype(BF16)
    dtok_ref[...] = dtok.astype(BF16)


def pack_kernel(expert_ref, *refs):
    saved, outs = refs[:3], refs[3:]
    width = saved[0].shape[2]
    for r, out in enumerate(outs):

        @pl.when(pl.program_id(0) == r)
        def _():
            for a in range(3):
                out[:, a * width : (a + 1) * width] = saved[a][0]


def pack(expert, saved):
    n, depth, width = saved[0].shape
    return pl.pallas_call(
        pack_kernel,
        grid_spec=pltpu.PrefetchScalarGridSpec(
            num_scalar_prefetch=1,
            grid=(n,),
            in_specs=[pl.BlockSpec((1, depth, width), lambda i, e: ((e[0] + i) & (n - 1), 0, 0))] * 3,
            out_specs=[pl.BlockSpec((depth, 3 * width), lambda i, e: (0, 0))] * n,
        ),
        out_shape=[jax.ShapeDtypeStruct((depth, 3 * width), BF16)] * n,
        cost_estimate=pl.CostEstimate(
            flops=0, bytes_accessed=12 * n * depth * width, transcendentals=0
        ),
    )(expert.astype(jnp.int32).reshape(1), *saved)


def place_kernel(expert_ref, *refs):
    pieces, out = refs[:-1], refs[-1]
    width = out.shape[2]
    for r, piece in enumerate(pieces):

        @pl.when(pl.program_id(0) == r)
        def _():
            for a in range(3):
                out[a] = piece[:, a * width : (a + 1) * width]


def place(expert, pieces):
    n, (depth, width3) = len(pieces), pieces[0].shape
    width = width3 // 3
    return pl.pallas_call(
        place_kernel,
        grid_spec=pltpu.PrefetchScalarGridSpec(
            num_scalar_prefetch=1,
            grid=(n,),
            in_specs=[pl.BlockSpec((depth, width3), lambda i, e: (0, 0))] * n,
            out_specs=pl.BlockSpec((3, depth, width), lambda i, e: (0, 0, (e[0] - i) & (n - 1))),
        ),
        out_shape=jax.ShapeDtypeStruct((3, depth, n * width), BF16),
        cost_estimate=pl.CostEstimate(
            flops=0, bytes_accessed=12 * n * depth * width, transcendentals=0
        ),
    )(expert.astype(jnp.int32).reshape(1), *pieces)


def part_kernel(n, order_ref, mine_x_ref, other_x_ref, w_ref, *out_refs):
    width = w_ref.shape[2]
    first = order_ref[1] == 0
    mine, other = mine_x_ref[0], other_x_ref[0]
    x, dy = jnp.where(first, mine, other), jnp.where(first, other, mine)

    def fill(outs):
        for a, rows in enumerate((x, x, dy)):
            s = slice(a * width, (a + 1) * width)
            product = jnp.dot(rows, w_ref[a], preferred_element_type=F32).astype(BF16)
            lower = 0
            for out in outs:
                out[:, s] = product[lower : lower + out.shape[0]]
                lower += out.shape[0]

    if n == 1:
        fill(out_refs)
        return
    for i, out in enumerate(out_refs):
        pl.when(pl.program_id(0) == i)(functools.partial(fill, (out,)))


def stepper(steps, ring):
    first, jump = steps[0], steps[-1] - steps[0]
    return lambda i, o: (o[0] + first + jump * i) & (ring - 1)


def parts(where, steps, mine, other, w, heights=None):
    ring, height, depth = mine.shape
    width = w.shape[2]
    n = len(steps)
    chunk = stepper(steps, ring)
    heights = heights or (height,) * n
    return pl.pallas_call(
        functools.partial(part_kernel, n),
        grid_spec=pltpu.PrefetchScalarGridSpec(
            num_scalar_prefetch=1,
            grid=(n,),
            in_specs=[
                pl.BlockSpec((1, height, depth), lambda i, o: (chunk(i, o), 0, 0)),
                pl.BlockSpec((1, height, depth), lambda i, o: (chunk(i, o), 0, 0)),
                pl.BlockSpec(w.shape, lambda i, o: (0, 0, 0)),
            ],
            out_specs=[pl.BlockSpec((h, 3 * width), lambda i, o: (0, 0)) for h in heights],
        ),
        out_shape=[jax.ShapeDtypeStruct((h, 3 * width), BF16) for h in heights],
        cost_estimate=pl.CostEstimate(
            flops=n * height * depth * width * 6,
            bytes_accessed=2 * (n * height * (2 * depth + 3 * width) + 3 * depth * width),
            transcendentals=0,
        ),
    )(where, mine, other, w)


def act_kernel(a_ref, b_ref, c_ref, out_ref):
    width = a_ref.shape[1] // 3

    def total(k):
        s = slice(k * width, (k + 1) * width)
        return a_ref[:, s].astype(F32) + b_ref[:, s].astype(F32) + c_ref[:, s].astype(F32)

    gate, up, back = total(0), total(1), total(2)
    sig = jax.nn.sigmoid(gate)
    silu = gate * sig
    out_ref[:, :width] = (back * up * sig * (1.0 + gate * (1.0 - sig))).astype(BF16)
    out_ref[:, width : 2 * width] = (back * silu).astype(BF16)
    out_ref[:, 2 * width :] = (silu * up).astype(BF16)


def contract_last(left, right):
    return lax.dot_general(
        left, right, (((1,), (1,)), ((), ())), preferred_element_type=F32
    )


def back_rows(acts, first, w_ref, keep_ref, send_ref, all_ref, lower, upper):
    width = w_ref.shape[2]
    d_gate, d_up, hidden = (acts[:, k * width : (k + 1) * width] for k in range(3))
    out = contract_last(hidden, w_ref[2])
    d_x = contract_last(d_gate, w_ref[0]) + contract_last(d_up, w_ref[1])
    keep_ref[0, lower:upper] = jnp.where(first, out, d_x).astype(BF16)
    send_ref[0, lower:upper] = jnp.where(first, d_x, out).astype(BF16)
    all_ref[0, lower:upper] = acts


def back_kernel(n, halves, order_ref, *refs):
    chunks, w_ref = refs[:n], refs[n]
    outs = refs[-3:]
    first = order_ref[1] == 0
    if halves:
        lower = 0
        for c in chunks:
            back_rows(c[...], first, w_ref, *outs, lower, lower + c.shape[0])
            lower += c.shape[0]
        return
    for i, c in enumerate(chunks):

        @pl.when(pl.program_id(0) == i)
        def _():
            back_rows(c[...], first, w_ref, *outs, 0, c.shape[0])


def back(where, steps, chunks, w, held, n_chunks, halves=False):
    n = len(chunks)
    chunk = stepper(steps, n_chunks)
    height = sum(c.shape[0] for c in chunks) if halves else chunks[0].shape[0]
    width3 = chunks[0].shape[1]
    depth = w.shape[1]
    grid = len(steps)
    in_specs = [pl.BlockSpec(c.shape, lambda i, o: (0, 0)) for c in chunks]
    in_specs.append(pl.BlockSpec(w.shape, lambda i, o: (0, 0, 0)))
    aliases = {}
    extra = ()
    if held is not None:
        in_specs += [pl.BlockSpec(memory_space=pl.ANY)] * 3
        aliases = {n + 2: 0, n + 3: 1, n + 4: 2}
        extra = held
    return pl.pallas_call(
        functools.partial(back_kernel, n, halves),
        grid_spec=pltpu.PrefetchScalarGridSpec(
            num_scalar_prefetch=1,
            grid=(grid,),
            in_specs=in_specs,
            out_specs=[
                pl.BlockSpec((1, height, depth), lambda i, o: (chunk(i, o), 0, 0)),
                pl.BlockSpec((1, height, depth), lambda i, o: (chunk(i, o), 0, 0)),
                pl.BlockSpec((1, height, width3), lambda i, o: (chunk(i, o), 0, 0)),
            ],
        ),
        out_shape=[
            jax.ShapeDtypeStruct((n_chunks, height, depth), BF16),
            jax.ShapeDtypeStruct((n_chunks, height, depth), BF16),
            jax.ShapeDtypeStruct((n_chunks, height, width3), BF16),
        ],
        input_output_aliases=aliases,
        cost_estimate=pl.CostEstimate(
            flops=grid * height * depth * width3 * 2,
            bytes_accessed=2 * (grid * height * (2 * width3 + 2 * depth) + depth * width3),
            transcendentals=0,
        ),
    )(where, *chunks, w, *extra)


def contract_rows(left, right):
    return lax.dot_general(
        left, right, (((0,), (0,)), ((), ())), preferred_element_type=F32
    )


def step(tokens, route_ids, route_gates, d_out, gate_saved, up_saved, down_saved):
    experts = lax.axis_size("expert")
    ring = lax.axis_size("tensor")
    n_chips = lax.axis_size("ylo") * lax.axis_size("x")
    tok_count, depth = tokens.shape
    slots = 5 * tok_count // 8
    part = gate_saved.shape[2]
    width = experts * part
    core = lax.axis_index("core")

    ids_row, gates_row = route_ids.T, route_gates.T
    sent = pl.pallas_call(
        send_kernel,
        out_shape=jax.ShapeDtypeStruct((2 * experts, slots, depth), BF16),
    )(ids_row, gates_row, tokens, d_out)
    own = lax.all_to_all(sent, ("core", "expert"), 0, 0, tiled=True)
    height = 2 * experts * slots
    own = own.reshape(height, depth)
    expert = lax.axis_index("expert")
    pieces = pack(expert, (gate_saved, up_saved, down_saved))
    pieces = [pieces[0]] + [
        lax.ppermute(pieces[r], "expert", [(i, (i + r) % experts) for i in range(experts)])
        for r in range(1, experts)
    ]
    w = place(expert, pieces)
    mine = lax.all_to_all(
        jnp.broadcast_to(own[None], (n_chips, height, depth)), CHIPS, 0, 0, tiled=True
    )
    swap = [(0, 1), (1, 0)]
    other = lax.ppermute(mine, "core", swap)

    right = [(i, (i + 1) % ring) for i in range(ring)]
    left = [(i, (i - 1) % ring) for i in range(ring)]
    here = lax.axis_index("tensor")

    def both(to_right, to_left):
        return (lax.ppermute(to_right, "tensor", right), lax.ppermute(to_left, "tensor", left))

    where = jnp.stack([here, core]).astype(jnp.int32)

    half = height // 16 * 8
    got = both(*parts(where, (4,), mine, other, w, (half, height - half)))
    own_r, own_l = parts(where, (3, -3,), mine, other, w)
    to_right = jnp.concatenate((own_r[:half] + got[0], own_r[half:]), axis=0)
    to_left = jnp.concatenate((own_l[:half], own_l[half:] + got[1]), axis=0)
    for k in (2, 1):
        got = both(to_right, to_left)
        own_r, own_l = parts(where, (k, -k,), mine, other, w)
        to_right, to_left = got[0] + own_r, got[1] + own_l
    got = both(to_right, to_left)
    (own_0,) = parts(where, (0,), mine, other, w)
    acts = pl.pallas_call(
        act_kernel, out_shape=jax.ShapeDtypeStruct((height, 3 * width), BF16)
    )(own_0, *got)

    got = both(acts, acts)
    held = back(where, (0,), (acts,), w, None, ring)
    for k in (1, 2, 3):
        now = got
        if k < 3:
            got = both(*now)
        else:
            got = both(now[0][:half], now[1][half:])
        held = back(where, (-k, k,), now, w, held, ring)
    keep, send, acts = back(where, (4,), got, w, held, ring, halves=True)

    got = lax.ppermute(send, "core", swap)
    sums = (keep.astype(F32) + got.astype(F32)).astype(BF16)
    sums = lax.all_to_all(sums, CHIPS, 0, 0, tiled=True)
    own = jnp.sum(sums.astype(F32), axis=0).astype(BF16)
    own = own.reshape(2 * experts, slots, depth)
    returned = lax.all_to_all(own, ("core", "expert"), 0, 0, tiled=True)
    out, d_tokens = pl.pallas_call(
        finish_kernel,
        out_shape=[jax.ShapeDtypeStruct(tokens.shape, BF16)] * 2,
    )(ids_row, gates_row, returned)

    acts = acts.reshape(ring * height, 3 * width)
    x = jnp.where(core == 0, mine, other).reshape(n_chips * height, depth)
    dy = jnp.where(core == 0, other, mine).reshape(n_chips * height, depth)
    grads = [
        contract_rows(x if a < 2 else dy, acts[:, a * width : (a + 1) * width]).astype(BF16)[None]
        for a in range(3)
    ]
    return (out, d_tokens, *grads)


def solution(mesh):
    fine = Mesh(
        mesh.devices.reshape(2, 4, 2, 4, 8), ("ylo", "x", "core", "expert", "tensor")
    )
    dp = ("ylo", "x", "core")
    tok = P((*dp, "expert"), "tensor")
    route = P((*dp, "expert"), None)
    saved = P(None, "tensor", (*dp, "expert"))
    grad = P("expert", "tensor", dp)
    return jax.shard_map(
        step,
        mesh=fine,
        in_specs=(tok, route, route, tok, saved, saved, saved),
        out_specs=(tok, tok, grad, grad, grad),
        check_vma=False,
    )
```

time: 276 us -> 281 us (1.018)
  the two profiles are of different devices: /device:TPU:6 before, /device:TPU:1 now
where the time goes in v1:
time: 281 us; the launch traced here: 279 us
  starting transfers between devices  91.1 us (32%)
  waiting for transfers between devices  71.1 us (25%)
  Pallas kernels  54.5 us (19%)
  blocking collectives  38.6 us (14%)
  other arithmetic  8.05 us (3%)
  local copies, waits for them, and re-layouts  8.02 us (3%)
  matrix products  6.23 us (2%)
    ppermute x8, starting transfers between devices, both(): lax.ppermute(to_left, 'tensor', left)  42.9 us
    ppermute x3, waiting for transfers between devices, step(): lax.ppermute(pieces[r], 'expert', [(i, (i + r) % experts) for i in range(...  33.9 us
    pallas_call x5, Pallas kernels, back(): pl.pallas_call(functools.partial(back_kernel, n, halves), grid_spec=pltpu...  21.9 us
    all_to_all x1, blocking collectives, step(): lax.all_to_all(jnp.broadcast_to(own[None], (n_chips, height, depth)), CHI...  19.5 us
    all_to_all x1, blocking collectives, step(): own = lax.all_to_all(sent, ('core', 'expert'), 0, 0, tiled=True)  19.2 us
    pallas_call x5, Pallas kernels, parts(): pl.pallas_call(functools.partial(part_kernel, n), grid_spec=pltpu.Prefetc...  18.8 us
    ppermute x8, starting transfers between devices, both(): lax.ppermute(to_right, 'tensor', right)  17.4 us
    ppermute x8, waiting for transfers between devices, both(): lax.ppermute(to_left, 'tensor', left)  10.9 us
  transfers between devices with their start and end apart: 23, of which 13 were waited for; matrix products, arithmetic and copies ran while one was open for 5% of the time, Pallas kernels for 14%

profile of v1, /device:TPU:1, one launch (start us, length us, event | category | flops | bytes accessed | tf_op | source)
XLA Modules:
  0.0 278.7 jit_solution(5844117357569450386)
XLA Ops:
  0.6 2.2 shard_map.110
  2.8 19.2 %all_to_all.20 = bf16[8,17,512]{2,1,0:T(8,128)(2,1)S(1)} all-to-all(bf16[8,17,512]{2,1,0:T(8,128)(2,1)} %shard_map.110), channel_id=1, replica_groups=mesh['ylo'=2,'x'=4,'core'=2,'expert'=4,'tensor'=8] {'core','expert'}, dimensions={0} | all-to-all | bytes 278528 | tf_op jit(solution)/shard_map/all_to_all | solution.py:289
  22.1 19.5 %all_to_all.21.mine_x_ref = bf16[8,136,512]{2,1,0:T(8,128)(2,1)S(1)} all-to-all(bf16[8,136,512]{2,1,0:T(8,128)(2,1)S(1)} %broadcast_in_dim.17), channel_id=1, replica_groups=mesh['ylo'=2,'x'=4,'core'=2,'expert'=4,'tensor'=8] {'ylo','x'}, dimensions={0} | all-to-all | bytes 2228224 | tf_op jit(solution)/shard_map/all_to_all | solution.py:299
  41.6 3.2 %collective-permute-start = (bf16[8,136,512]{2,1,0:T(8,128)(2,1)S(1)}, bf16[8,136,512]{2,1,0:T(8,128)(2,1)S(1)}, u32[]{:S(2)}, u32[]{:S(2)}) collective-permute-start(bf16[8,136,512]{2,1,0:T(8,128)(2,1)S(1)} %all_to_all.21.mine_x_ref), channel_id=1, source_target_pairs={{0,32},{32,0},{1,33},{33,1},{2,34},{34,2},{3,35},{35,3},{4,36},{36... | collective-permute-start | bytes 3342344 | tf_op jit(solution)/shard_map/ppermute | solution.py:303
  44.8 3.6 %shard_map.111 = (bf16[512,384]{1,0:T(8,128)(2,1)}, bf16[512,384]{1,0:T(8,128)(2,1)}, bf16[512,384]{1,0:T(8,128)(2,1)}, bf16[512,384]{1,0:T(8,128)(2,1)}) custom-call(s32[1]{0:T(128)} %bitcast.4.expert_ref, bf16[4,512,128]{2,1,0:T(8,128)(2,1)} %refs_0_.1, bf16[4,512,128]{2,1,0:T(8,128)(2,1)} %refs_1_.1, bf16[4,512,128]{2,1,0:T(8,128)(2,1)} %refs_2_.1), custom_call_target="tpu_custom_call" | custom-call | bytes 3145728 | tf_op jit(solution)/shard_map/pallas_call | solution.py:81
  48.4 2.8 collective-permute-start.1
  51.2 2.9 %collective-permute-start.2 = (bf16[512,384]{1,0:T(8,128)(2,1)}, bf16[512,384]{1,0:T(8,128)(2,1)S(1)}, u32[]{:S(2)}, u32[]{:S(2)}) collective-permute-start(bf16[512,384]{1,0:T(8,128)(2,1)} %get-tuple-element.36), channel_id=1, source_target_pairs={{0,16},{8,24},{16,0},{24,8},{1,17},{9,25},{17,1},{25,9},{2,18},{10... | collective-permute-start | bytes 1179656 | tf_op jit(solution)/shard_map/ppermute | solution.py:295
  54.1 4.5 %collective-permute-start.3 = (bf16[512,384]{1,0:T(8,128)(2,1)}, bf16[512,384]{1,0:T(8,128)(2,1)S(1)}, u32[]{:S(2)}, u32[]{:S(2)}) collective-permute-start(bf16[512,384]{1,0:T(8,128)(2,1)} %get-tuple-element.37), channel_id=1, source_target_pairs={{0,24},{8,0},{16,8},{24,16},{1,25},{9,1},{17,9},{25,17},{2,26},{10... | collective-permute-start | bytes 1179656 | tf_op jit(solution)/shard_map/ppermute | solution.py:295
  59.2 13.9 %collective-permute-done.1.refs_1_ = bf16[512,384]{1,0:T(8,128)(2,1)S(1)} collective-permute-done((bf16[512,384]{1,0:T(8,128)(2,1)}, bf16[512,384]{1,0:T(8,128)(2,1)S(1)}, u32[]{:S(2)}, u32[]{:S(2)}) %collective-permute-start.1) | collective-permute-done | bytes 393248 | tf_op jit(solution)/shard_map/ppermute | solution.py:295
  73.2 8.4 %collective-permute-done.2.refs_2_ = bf16[512,384]{1,0:T(8,128)(2,1)S(1)} collective-permute-done((bf16[512,384]{1,0:T(8,128)(2,1)}, bf16[512,384]{1,0:T(8,128)(2,1)S(1)}, u32[]{:S(2)}, u32[]{:S(2)}) %collective-permute-start.2) | collective-permute-done | bytes 393248 | tf_op jit(solution)/shard_map/ppermute | solution.py:295
  81.5 11.6 %collective-permute-done.3.refs_3_ = bf16[512,384]{1,0:T(8,128)(2,1)S(1)} collective-permute-done((bf16[512,384]{1,0:T(8,128)(2,1)}, bf16[512,384]{1,0:T(8,128)(2,1)S(1)}, u32[]{:S(2)}, u32[]{:S(2)}) %collective-permute-start.3) | collective-permute-done | bytes 393248 | tf_op jit(solution)/shard_map/ppermute | solution.py:295
  93.9 3.2 %shard_map.112.w_ref.refs_1_.refs_2_ = bf16[3,512,512]{2,1,0:T(8,128)(2,1)} custom-call(s32[1]{0:T(128)} %bitcast.4.expert_ref, bf16[512,384]{1,0:T(8,128)(2,1)} %get-tuple-element.34.refs_0_, bf16[512,384]{1,0:T(8,128)(2,1)} %copy-done.18, bf16[512,384]{1,0:T(8,128)(2,1)} %copy-done.19, bf16[512,384]{1,0:T(8,128)(2,1)} %copy-done.20), custom_call_target="tpu_custom_call" | custom-call | bytes 3145728 | tf_op jit(solution)/shard_map/pallas_call | solution.py:110
  98.1 3.4 %shard_map.115 = (bf16[64,1536]{1,0:T(8,128)(2,1)}, bf16[72,1536]{1,0:T(8,128)(2,1)}) custom-call(s32[2]{0:T(128)} %pad_add_fusion.order_ref, bf16[8,136,512]{2,1,0:T(8,128)(2,1)} %copy-done, bf16[8,136,512]{2,1,0:T(8,128)(2,1)} %copy-done.3, bf16[3,512,512]{2,1,0:T(8,128)(2,1)} %shard_map.112.w_ref.refs_1_.refs_2_), custom_call_target="tpu_custom_call" | custom-call | flops 213909504 | bytes 2269184 | tf_op jit(solution)/shard_map/pallas_call | solution.py:158
  101.5 4.0 %collective-permute-start.4 = (bf16[64,1536]{1,0:T(8,128)(2,1)}, bf16[64,1536]{1,0:T(8,128)(2,1)S(1)}, u32[]{:S(2)}, u32[]{:S(2)}) collective-permute-start(bf16[64,1536]{1,0:T(8,128)(2,1)} %get-tuple-element.39), channel_id=1, source_target_pairs={{0,1},{1,2},{2,3},{3,4},{4,5},{5,6},{6,7},{7,0},{8,9},{9,10},{10,1... | collective-permute-start | bytes 589832 | tf_op jit(solution)/shard_map/ppermute | solution.py:310
  105.5 8.6 %collective-permute-start.8 = (bf16[72,1536]{1,0:T(8,128)(2,1)}, bf16[72,1536]{1,0:T(8,128)(2,1)S(1)}, u32[]{:S(2)}, u32[]{:S(2)}) collective-permute-start(bf16[72,1536]{1,0:T(8,128)(2,1)} %get-tuple-element.43), channel_id=1, source_target_pairs={{0,7},{1,0},{2,1},{3,2},{4,3},{5,4},{6,5},{7,6},{8,15},{9,8},{10,9... | collective-permute-start | bytes 663560 | tf_op jit(solution)/shard_map/ppermute | solution.py:310
  114.1 4.0 %shard_map.114 = (bf16[136,1536]{1,0:T(8,128)(2,1)}, bf16[136,1536]{1,0:T(8,128)(2,1)}) custom-call(s32[2]{0:T(128)} %pad_add_fusion.order_ref, bf16[8,136,512]{2,1,0:T(8,128)(2,1)} %copy-done, bf16[8,136,512]{2,1,0:T(8,128)(2,1)} %copy-done.3, bf16[3,512,512]{2,1,0:T(8,128)(2,1)} %shard_map.112.w_ref.refs_1_.refs_2_), custom_call_target="tpu_custom_call" | custom-call | flops 427819008 | bytes 2965504 | tf_op jit(solution)/shard_map/pallas_call | solution.py:158
  121.1 1.9 collective-permute-start.5
  123.1 4.6 %collective-permute-start.9 = (bf16[136,1536]{1,0:T(8,128)(2,1)S(1)}, bf16[136,1536]{1,0:T(8,128)(2,1)S(1)}, u32[]{:S(2)}, u32[]{:S(2)}) collective-permute-start(bf16[136,1536]{1,0:T(8,128)(2,1)S(1)} %pad_maximum_fusion.1), channel_id=1, source_target_pairs={{0,7},{1,0},{2,1},{3,2},{4,3},{5,4},{6,5},{7,6},{8,15},{9,8},{10,9... | collective-permute-start | bytes 1253384 | tf_op jit(solution)/shard_map/ppermute | solution.py:310
  127.7 4.0 %shard_map.116 = (bf16[136,1536]{1,0:T(8,128)(2,1)}, bf16[136,1536]{1,0:T(8,128)(2,1)}) custom-call(s32[2]{0:T(128)} %pad_add_fusion.order_ref, bf16[8,136,512]{2,1,0:T(8,128)(2,1)} %copy-done, bf16[8,136,512]{2,1,0:T(8,128)(2,1)} %copy-done.3, bf16[3,512,512]{2,1,0:T(8,128)(2,1)} %shard_map.112.w_ref.refs_1_.refs_2_), custom_call_target="tpu_custom_call" | custom-call | flops 427819008 | bytes 2965504 | tf_op jit(solution)/shard_map/pallas_call | solution.py:158
  131.7 2.9 %collective-permute-done.5 = bf16[136,1536]{1,0:T(8,128)(2,1)S(1)} collective-permute-done((bf16[136,1536]{1,0:T(8,128)(2,1)S(1)}, bf16[136,1536]{1,0:T(8,128)(2,1)S(1)}, u32[]{:S(2)}, u32[]{:S(2)}) %collective-permute-start.5) | collective-permute-done | bytes 417824 | tf_op jit(solution)/shard_map/ppermute | solution.py:310
  137.8 4.6 %collective-permute-start.10 = (bf16[136,1536]{1,0:T(8,128)(2,1)S(1)}, bf16[136,1536]{1,0:T(8,128)(2,1)S(1)}, u32[]{:S(2)}, u32[]{:S(2)}) collective-permute-start(bf16[136,1536]{1,0:T(8,128)(2,1)S(1)} %add.25), channel_id=1, source_target_pairs={{0,7},{1,0},{2,1},{3,2},{4,3},{5,4},{6,5},{7,6},{8,15},{9,8},{10,9... | collective-permute-start | bytes 1253384 | tf_op jit(solution)/shard_map/ppermute | solution.py:310
  142.4 4.0 %shard_map.117 = (bf16[136,1536]{1,0:T(8,128)(2,1)}, bf16[136,1536]{1,0:T(8,128)(2,1)}) custom-call(s32[2]{0:T(128)} %pad_add_fusion.order_ref, bf16[8,136,512]{2,1,0:T(8,128)(2,1)} %copy-done, bf16[8,136,512]{2,1,0:T(8,128)(2,1)} %copy-done.3, bf16[3,512,512]{2,1,0:T(8,128)(2,1)} %shard_map.112.w_ref.refs_1_.refs_2_), custom_call_target="tpu_custom_call" | custom-call | flops 427819008 | bytes 2965504 | tf_op jit(solution)/shard_map/pallas_call | solution.py:158
  146.4 2.0 collective-permute-done.6
  149.6 1.9 collective-permute-start.7
  151.6 4.6 %collective-permute-start.11 = (bf16[136,1536]{1,0:T(8,128)(2,1)S(1)}, bf16[136,1536]{1,0:T(8,128)(2,1)S(1)}, u32[]{:S(2)}, u32[]{:S(2)}) collective-permute-start(bf16[136,1536]{1,0:T(8,128)(2,1)S(1)} %add.26), channel_id=1, source_target_pairs={{0,7},{1,0},{2,1},{3,2},{4,3},{5,4},{6,5},{7,6},{8,15},{9,8},{10,9... | collective-permute-start | bytes 1253384 | tf_op jit(solution)/shard_map/ppermute | solution.py:310
  156.2 3.4 %shard_map.113.a_ref = bf16[136,1536]{1,0:T(8,128)(2,1)} custom-call(s32[2]{0:T(128)} %pad_add_fusion.order_ref, bf16[8,136,512]{2,1,0:T(8,128)(2,1)} %copy-done, bf16[8,136,512]{2,1,0:T(8,128)(2,1)} %copy-done.3, bf16[3,512,512]{2,1,0:T(8,128)(2,1)} %shard_map.112.w_ref.refs_1_.refs_2_), custom_call_target="tpu_custom_call" | custom-call | flops 213909504 | bytes 2269184 | tf_op jit(solution)/shard_map/pallas_call | solution.py:158
  163.2 2.3 shard_map.118.refs_0_
  165.5 5.3 %collective-permute-start.16 = (bf16[136,1536]{1,0:T(8,128)(2,1)}, bf16[136,1536]{1,0:T(8,128)(2,1)S(1)}, u32[]{:S(2)}, u32[]{:S(2)}) collective-permute-start(bf16[136,1536]{1,0:T(8,128)(2,1)} %shard_map.118.refs_0_), channel_id=1, source_target_pairs={{0,7},{1,0},{2,1},{3,2},{4,3},{5,4},{6,5},{7,6},{8,15},{9,8},{10,9... | collective-permute-start | bytes 1253384 | tf_op jit(solution)/shard_map/ppermute | solution.py:310
  172.7 3.8 %collective-permute-done.16.refs_1_ = bf16[136,1536]{1,0:T(8,128)(2,1)S(1)} collective-permute-done((bf16[136,1536]{1,0:T(8,128)(2,1)}, bf16[136,1536]{1,0:T(8,128)(2,1)S(1)}, u32[]{:S(2)}, u32[]{:S(2)}) %collective-permute-start.16) | collective-permute-done | bytes 417824 | tf_op jit(solution)/shard_map/ppermute | solution.py:310
  176.5 5.2 %collective-permute-start.17 = (bf16[136,1536]{1,0:T(8,128)(2,1)S(1)}, bf16[136,1536]{1,0:T(8,128)(2,1)S(1)}, u32[]{:S(2)}, u32[]{:S(2)}) collective-permute-start(bf16[136,1536]{1,0:T(8,128)(2,1)S(1)} %collective-permute-done.16.refs_1_), channel_id=1, source_target_pairs={{0,7},{1,0},{2,1},{3,2},{4,3},{5,4},{6,5},{7,6},{8,15},{9,8},{10,9... | collective-permute-start | bytes 1253384 | tf_op jit(solution)/shard_map/ppermute | solution.py:310
  183.7 3.0 %collective-permute-done.17.refs_1_ = bf16[136,1536]{1,0:T(8,128)(2,1)S(1)} collective-permute-done((bf16[136,1536]{1,0:T(8,128)(2,1)S(1)}, bf16[136,1536]{1,0:T(8,128)(2,1)S(1)}, u32[]{:S(2)}, u32[]{:S(2)}) %collective-permute-start.17) | collective-permute-done | bytes 417824 | tf_op jit(solution)/shard_map/ppermute | solution.py:310
  186.7 5.0 %collective-permute-start.18 = (bf16[136,1536]{1,0:T(8,128)(2,1)S(1)}, bf16[136,1536]{1,0:T(8,128)(2,1)S(1)}, u32[]{:S(2)}, u32[]{:S(2)}) collective-permute-start(bf16[136,1536]{1,0:T(8,128)(2,1)S(1)} %collective-permute-done.17.refs_1_), channel_id=1, source_target_pairs={{0,7},{1,0},{2,1},{3,2},{4,3},{5,4},{6,5},{7,6},{8,15},{9,8},{10,9... | collective-permute-start | bytes 1253384 | tf_op jit(solution)/shard_map/ppermute | solution.py:310
  193.6 3.0 %collective-permute-done.18.refs_1_ = bf16[136,1536]{1,0:T(8,128)(2,1)S(1)} collective-permute-done((bf16[136,1536]{1,0:T(8,128)(2,1)S(1)}, bf16[136,1536]{1,0:T(8,128)(2,1)S(1)}, u32[]{:S(2)}, u32[]{:S(2)}) %collective-permute-start.18) | collective-permute-done | bytes 417824 | tf_op jit(solution)/shard_map/ppermute | solution.py:310
  196.7 5.0 %collective-permute-start.19 = (bf16[72,1536]{1,0:T(8,128)(2,1)S(1)}, bf16[72,1536]{1,0:T(8,128)(2,1)S(1)}, u32[]{:S(2)}, u32[]{:S(2)}) collective-permute-start(bf16[72,1536]{1,0:T(8,128)(2,1)S(1)} %slice.37), channel_id=1, source_target_pairs={{0,7},{1,0},{2,1},{3,2},{4,3},{5,4},{6,5},{7,6},{8,15},{9,8},{10,9... | collective-permute-start | bytes 663560 | tf_op jit(solution)/shard_map/ppermute | solution.py:310
  203.7 3.7 %shard_map.119 = (bf16[8,136,512]{2,1,0:T(8,128)(2,1)}, bf16[8,136,512]{2,1,0:T(8,128)(2,1)}, bf16[8,136,1536]{2,1,0:T(8,128)(2,1)}) custom-call(s32[2]{0:T(128)} %pad_add_fusion.order_ref, bf16[136,1536]{1,0:T(8,128)(2,1)} %shard_map.118.refs_0_, bf16[3,512,512]{2,1,0:T(8,128)(2,1)} %shard_map.112.w_ref.refs_1_.refs_2_), custom_call_target="tpu_custom_call" | custom-call | flops 213909504 | bytes 2686976 | tf_op jit(solution)/shard_map/pallas_call | solution.py:242
  207.5 4.6 %shard_map.120 = (bf16[8,136,512]{2,1,0:T(8,128)(2,1)}, bf16[8,136,512]{2,1,0:T(8,128)(2,1)}, bf16[8,136,1536]{2,1,0:T(8,128)(2,1)}) custom-call(s32[2]{0:T(128)} %pad_add_fusion.order_ref, bf16[136,1536]{1,0:T(8,128)(2,1)} %copy-done.16, bf16[136,1536]{1,0:T(8,128)(2,1)} %copy-done.14, ...), custom_call_target="tpu_custom_call", output_to_operand_aliasing={{0}: (4, {}), {1}: (5, {}), {2}: (6, {})} | custom-call | flops 427819008 | bytes 3801088 | tf_op jit(solution)/shard_map/pallas_call | solution.py:242
  212.1 4.6 %shard_map.121 = (bf16[8,136,512]{2,1,0:T(8,128)(2,1)}, bf16[8,136,512]{2,1,0:T(8,128)(2,1)}, bf16[8,136,1536]{2,1,0:T(8,128)(2,1)}) custom-call(s32[2]{0:T(128)} %pad_add_fusion.order_ref, bf16[136,1536]{1,0:T(8,128)(2,1)} %copy-done.17, bf16[136,1536]{1,0:T(8,128)(2,1)} %copy-done.15, ...), custom_call_target="tpu_custom_call", output_to_operand_aliasing={{0}: (4, {}), {1}: (5, {}), {2}: (6, {})} | custom-call | flops 427819008 | bytes 3801088 | tf_op jit(solution)/shard_map/pallas_call | solution.py:242
  216.7 4.6 %shard_map.122 = (bf16[8,136,512]{2,1,0:T(8,128)(2,1)}, bf16[8,136,512]{2,1,0:T(8,128)(2,1)}, bf16[8,136,1536]{2,1,0:T(8,128)(2,1)}) custom-call(s32[2]{0:T(128)} %pad_add_fusion.order_ref, bf16[136,1536]{1,0:T(8,128)(2,1)} %copy-done.7, bf16[136,1536]{1,0:T(8,128)(2,1)} %copy-done.6, ...), custom_call_target="tpu_custom_call", output_to_operand_aliasing={{0}: (4, {}), {1}: (5, {}), {2}: (6, {})} | custom-call | flops 427819008 | bytes 3801088 | tf_op jit(solution)/shard_map/pallas_call | solution.py:242
  222.1 4.3 %shard_map.123 = (bf16[8,136,512]{2,1,0:T(8,128)(2,1)}, bf16[8,136,512]{2,1,0:T(8,128)(2,1)}, bf16[8,136,1536]{2,1,0:T(8,128)(2,1)}) custom-call(s32[2]{0:T(128)} %pad_add_fusion.order_ref, bf16[64,1536]{1,0:T(8,128)(2,1)} %copy-done.22, bf16[72,1536]{1,0:T(8,128)(2,1)} %copy-done.21, ...), custom_call_target="tpu_custom_call", output_to_operand_aliasing={{0}: (4, {}), {1}: (5, {}), {2}: (6, {})} | custom-call | flops 213909504 | bytes 2686976 | tf_op jit(solution)/shard_map/pallas_call | solution.py:242
  226.4 9.7 %collective-permute-start.20 = (bf16[8,136,512]{2,1,0:T(8,128)(2,1)}, bf16[8,136,512]{2,1,0:T(8,128)(2,1)S(1)}, u32[]{:S(2)}, u32[]{:S(2)}) collective-permute-start(bf16[8,136,512]{2,1,0:T(8,128)(2,1)} %get-tuple-element.59), channel_id=1, source_target_pairs={{0,32},{32,0},{1,33},{33,1},{2,34},{34,2},{3,35},{35,3},{4,36},{36... | collective-permute-start | bytes 3342344 | tf_op jit(solution)/shard_map/ppermute | solution.py:340
  236.1 2.6 collective-permute-done.20
  238.6 2.5 add_convert_fusion
  241.2 3.7 %all-to-all-start.2 = ((bf16[8,136,512]{2,1,0:T(8,128)(2,1)}), bf16[8,136,512]{2,1,0:T(8,128)(2,1)S(1)}, u32[]{:S(2)}, u32[]{:S(2)}) async-start(bf16[8,136,512]{2,1,0:T(8,128)(2,1)} %add_convert_fusion), calls=%async_computation.2 | async-start | bytes 2228224 | tf_op jit(solution)/shard_map/all_to_all | solution.py:342
  250.6 9.9 %all-to-all-done.2 = bf16[8,136,512]{2,1,0:T(8,128)(2,1)S(1)} async-done(((bf16[8,136,512]{2,1,0:T(8,128)(2,1)}), bf16[8,136,512]{2,1,0:T(8,128)(2,1)S(1)}, u32[]{:S(2)}, u32[]{:S(2)}) %all-to-all-start.2) | async-done | bytes 1114144 | tf_op jit(solution)/shard_map/all_to_all | solution.py:342
  261.4 4.1 %all-to-all-start.3 = ((bf16[8,17,512]{2,1,0:T(8,128)(2,1)}), bf16[8,17,512]{2,1,0:T(8,128)(2,1)S(1)}, u32[]{:S(2)}, u32[]{:S(2)}) async-start(bf16[8,17,512]{2,1,0:T(8,128)(2,1)} %reshape.28), calls=%async_computation.3 | async-start | bytes 393216 | tf_op jit(solution)/shard_map/all_to_all | solution.py:345
  265.5 2.9 %fusion.2 = bf16[1,512,512]{2,1,0:T(8,128)(2,1)} fusion(bf16[1088,512]{1,0:T(8,128)(2,1)S(1)} %bitcast.20, bf16[1088,1536]{1,0:T(8,128)(2,1)} %bitcast.17), kind=kOutput, calls=%fused_computation.6 | convolution fusion | flops 570687488 | bytes 2752512 | tf_op jit(solution)/shard_map/dot_general | solution.py:269
  268.4 7.1 %all-to-all-done.3.back_ref = bf16[8,17,512]{2,1,0:T(8,128)(2,1)S(1)} async-done(((bf16[8,17,512]{2,1,0:T(8,128)(2,1)}), bf16[8,17,512]{2,1,0:T(8,128)(2,1)S(1)}, u32[]{:S(2)}, u32[]{:S(2)}) %all-to-all-start.3) | async-done | bytes 139296 | tf_op jit(solution)/shard_map/all_to_all | solution.py:345
  276.2 2.5 shard_map.124
  (83 shorter events, 29.3 us)
Async XLA Ops:
  41.6 55.5 %copy-start = (bf16[8,136,512]{2,1,0:T(8,128)(2,1)}, bf16[8,136,512]{2,1,0:T(8,128)(2,1)S(1)}, u32[]{:S(2)}) copy-start(bf16[8,136,512]{2,1,0:T(8,128)(2,1)S(1)} %all_to_all.21.mine_x_ref) | copy-start | bytes 3342340
  41.6 55.5 %collective-permute-start = (bf16[8,136,512]{2,1,0:T(8,128)(2,1)S(1)}, bf16[8,136,512]{2,1,0:T(8,128)(2,1)S(1)}, u32[]{:S(2)}, u32[]{:S(2)}) collective-permute-start(bf16[8,136,512]{2,1,0:T(8,128)(2,1)S(1)} %all_to_all.21.mine_x_ref), channel_id=1, source_target_pairs={{0,32},{32,0},{1,33},{33,1},{2,34},{34,2},{3,35},{35,3},{4,36},{36... | collective-permute-start | bytes 3342344 | tf_op jit(solution)/shard_map/ppermute | solution.py:303
  48.4 24.8 %collective-permute-start.1 = (bf16[512,384]{1,0:T(8,128)(2,1)}, bf16[512,384]{1,0:T(8,128)(2,1)S(1)}, u32[]{:S(2)}, u32[]{:S(2)}) collective-permute-start(bf16[512,384]{1,0:T(8,128)(2,1)} %get-tuple-element.35), channel_id=1, source_target_pairs={{0,8},{8,16},{16,24},{24,0},{1,9},{9,17},{17,25},{25,1},{2,10},{10... | collective-permute-start | bytes 1179656 | tf_op jit(solution)/shard_map/ppermute | solution.py:295
  51.2 30.4 %collective-permute-start.2 = (bf16[512,384]{1,0:T(8,128)(2,1)}, bf16[512,384]{1,0:T(8,128)(2,1)S(1)}, u32[]{:S(2)}, u32[]{:S(2)}) collective-permute-start(bf16[512,384]{1,0:T(8,128)(2,1)} %get-tuple-element.36), channel_id=1, source_target_pairs={{0,16},{8,24},{16,0},{24,8},{1,17},{9,25},{17,1},{25,9},{2,18},{10... | collective-permute-start | bytes 1179656 | tf_op jit(solution)/shard_map/ppermute | solution.py:295
  54.1 39.0 %collective-permute-start.3 = (bf16[512,384]{1,0:T(8,128)(2,1)}, bf16[512,384]{1,0:T(8,128)(2,1)S(1)}, u32[]{:S(2)}, u32[]{:S(2)}) collective-permute-start(bf16[512,384]{1,0:T(8,128)(2,1)} %get-tuple-element.37), channel_id=1, source_target_pairs={{0,24},{8,0},{16,8},{24,16},{1,25},{9,1},{17,9},{25,17},{2,26},{10... | collective-permute-start | bytes 1179656 | tf_op jit(solution)/shard_map/ppermute | solution.py:295
  73.2 20.0 %copy-start.18 = (bf16[512,384]{1,0:T(8,128)(2,1)}, bf16[512,384]{1,0:T(8,128)(2,1)S(1)}, u32[]{:S(2)}) copy-start(bf16[512,384]{1,0:T(8,128)(2,1)S(1)} %collective-permute-done.1.refs_1_) | copy-start | bytes 1179652
  81.5 11.6 %copy-start.19 = (bf16[512,384]{1,0:T(8,128)(2,1)}, bf16[512,384]{1,0:T(8,128)(2,1)S(1)}, u32[]{:S(2)}) copy-start(bf16[512,384]{1,0:T(8,128)(2,1)S(1)} %collective-permute-done.2.refs_2_) | copy-start | bytes 1179652
  93.1 0.8 copy-start.20
  97.1 1.0 copy-start.3
  101.5 18.6 %collective-permute-start.4 = (bf16[64,1536]{1,0:T(8,128)(2,1)}, bf16[64,1536]{1,0:T(8,128)(2,1)S(1)}, u32[]{:S(2)}, u32[]{:S(2)}) collective-permute-start(bf16[64,1536]{1,0:T(8,128)(2,1)} %get-tuple-element.39), channel_id=1, source_target_pairs={{0,1},{1,2},{2,3},{3,4},{4,5},{5,6},{6,7},{7,0},{8,9},{9,10},{10,1... | collective-permute-start | bytes 589832 | tf_op jit(solution)/shard_map/ppermute | solution.py:310
  105.5 17.5 %collective-permute-start.8 = (bf16[72,1536]{1,0:T(8,128)(2,1)}, bf16[72,1536]{1,0:T(8,128)(2,1)S(1)}, u32[]{:S(2)}, u32[]{:S(2)}) collective-permute-start(bf16[72,1536]{1,0:T(8,128)(2,1)} %get-tuple-element.43), channel_id=1, source_target_pairs={{0,7},{1,0},{2,1},{3,2},{4,3},{5,4},{6,5},{7,6},{8,15},{9,8},{10,9... | collective-permute-start | bytes 663560 | tf_op jit(solution)/shard_map/ppermute | solution.py:310
  118.1 4.9 %copy-start.13 = (bf16[136,1536]{1,0:T(8,128)(2,1)S(1)}, bf16[136,1536]{1,0:T(8,128)(2,1)}, u32[]{:S(2)}) copy-start(bf16[136,1536]{1,0:T(8,128)(2,1)} %get-tuple-element.42) | copy-start | bytes 1253380
  121.1 13.6 %collective-permute-start.5 = (bf16[136,1536]{1,0:T(8,128)(2,1)S(1)}, bf16[136,1536]{1,0:T(8,128)(2,1)S(1)}, u32[]{:S(2)}, u32[]{:S(2)}) collective-permute-start(bf16[136,1536]{1,0:T(8,128)(2,1)S(1)} %pad_maximum_fusion), channel_id=1, source_target_pairs={{0,1},{1,2},{2,3},{3,4},{4,5},{5,6},{6,7},{7,0},{8,9},{9,10},{10,1... | collective-permute-start | bytes 1253384 | tf_op jit(solution)/shard_map/ppermute | solution.py:310
  123.1 14.6 %collective-permute-start.9 = (bf16[136,1536]{1,0:T(8,128)(2,1)S(1)}, bf16[136,1536]{1,0:T(8,128)(2,1)S(1)}, u32[]{:S(2)}, u32[]{:S(2)}) collective-permute-start(bf16[136,1536]{1,0:T(8,128)(2,1)S(1)} %pad_maximum_fusion.1), channel_id=1, source_target_pairs={{0,7},{1,0},{2,1},{3,2},{4,3},{5,4},{6,5},{7,6},{8,15},{9,8},{10,9... | collective-permute-start | bytes 1253384 | tf_op jit(solution)/shard_map/ppermute | solution.py:310
  131.7 6.0 %copy-start.10 = (bf16[136,1536]{1,0:T(8,128)(2,1)S(1)}, bf16[136,1536]{1,0:T(8,128)(2,1)}, u32[]{:S(2)}) copy-start(bf16[136,1536]{1,0:T(8,128)(2,1)} %get-tuple-element.44) | copy-start | bytes 1253380
  135.8 12.7 %collective-permute-start.6 = (bf16[136,1536]{1,0:T(8,128)(2,1)S(1)}, bf16[136,1536]{1,0:T(8,128)(2,1)S(1)}, u32[]{:S(2)}, u32[]{:S(2)}) collective-permute-start(bf16[136,1536]{1,0:T(8,128)(2,1)S(1)} %add.22), channel_id=1, source_target_pairs={{0,1},{1,2},{2,3},{3,4},{4,5},{5,6},{6,7},{7,0},{8,9},{9,10},{10,1... | collective-permute-start | bytes 1253384 | tf_op jit(solution)/shard_map/ppermute | solution.py:310
  137.8 13.7 %collective-permute-start.10 = (bf16[136,1536]{1,0:T(8,128)(2,1)S(1)}, bf16[136,1536]{1,0:T(8,128)(2,1)S(1)}, u32[]{:S(2)}, u32[]{:S(2)}) collective-permute-start(bf16[136,1536]{1,0:T(8,128)(2,1)S(1)} %add.25), channel_id=1, source_target_pairs={{0,7},{1,0},{2,1},{3,2},{4,3},{5,4},{6,5},{7,6},{8,15},{9,8},{10,9... | collective-permute-start | bytes 1253384 | tf_op jit(solution)/shard_map/ppermute | solution.py:310
  146.4 5.1 %copy-start.11 = (bf16[136,1536]{1,0:T(8,128)(2,1)S(1)}, bf16[136,1536]{1,0:T(8,128)(2,1)}, u32[]{:S(2)}) copy-start(bf16[136,1536]{1,0:T(8,128)(2,1)} %get-tuple-element.45) | copy-start | bytes 1253380
  149.6 11.8 %collective-permute-start.7 = (bf16[136,1536]{1,0:T(8,128)(2,1)S(1)}, bf16[136,1536]{1,0:T(8,128)(2,1)S(1)}, u32[]{:S(2)}, u32[]{:S(2)}) collective-permute-start(bf16[136,1536]{1,0:T(8,128)(2,1)S(1)} %add.23), channel_id=1, source_target_pairs={{0,1},{1,2},{2,3},{3,4},{4,5},{5,6},{6,7},{7,0},{8,9},{9,10},{10,1... | collective-permute-start | bytes 1253384 | tf_op jit(solution)/shard_map/ppermute | solution.py:310
  151.6 10.8 %collective-permute-start.11 = (bf16[136,1536]{1,0:T(8,128)(2,1)S(1)}, bf16[136,1536]{1,0:T(8,128)(2,1)S(1)}, u32[]{:S(2)}, u32[]{:S(2)}) collective-permute-start(bf16[136,1536]{1,0:T(8,128)(2,1)S(1)} %add.26), channel_id=1, source_target_pairs={{0,7},{1,0},{2,1},{3,2},{4,3},{5,4},{6,5},{7,6},{8,15},{9,8},{10,9... | collective-permute-start | bytes 1253384 | tf_op jit(solution)/shard_map/ppermute | solution.py:310
  161.4 1.1 copy-start.9
  162.5 0.8 copy-start.12
  165.5 11.0 %collective-permute-start.16 = (bf16[136,1536]{1,0:T(8,128)(2,1)}, bf16[136,1536]{1,0:T(8,128)(2,1)S(1)}, u32[]{:S(2)}, u32[]{:S(2)}) collective-permute-start(bf16[136,1536]{1,0:T(8,128)(2,1)} %shard_map.118.refs_0_), channel_id=1, source_target_pairs={{0,7},{1,0},{2,1},{3,2},{4,3},{5,4},{6,5},{7,6},{8,15},{9,8},{10,9... | collective-permute-start | bytes 1253384 | tf_op jit(solution)/shard_map/ppermute | solution.py:310
  170.8 10.9 %collective-permute-start.12 = (bf16[136,1536]{1,0:T(8,128)(2,1)}, bf16[136,1536]{1,0:T(8,128)(2,1)S(1)}, u32[]{:S(2)}, u32[]{:S(2)}) collective-permute-start(bf16[136,1536]{1,0:T(8,128)(2,1)} %shard_map.118.refs_0_), channel_id=1, source_target_pairs={{0,1},{1,2},{2,3},{3,4},{4,5},{5,6},{6,7},{7,0},{8,9},{9,10},{10,1... | collective-permute-start | bytes 1253384 | tf_op jit(solution)/shard_map/ppermute | solution.py:310
  176.5 30.9 %copy-start.14 = (bf16[136,1536]{1,0:T(8,128)(2,1)}, bf16[136,1536]{1,0:T(8,128)(2,1)S(1)}, u32[]{:S(2)}) copy-start(bf16[136,1536]{1,0:T(8,128)(2,1)S(1)} %collective-permute-done.16.refs_1_) | copy-start | bytes 1253380
  176.5 10.2 %collective-permute-start.17 = (bf16[136,1536]{1,0:T(8,128)(2,1)S(1)}, bf16[136,1536]{1,0:T(8,128)(2,1)S(1)}, u32[]{:S(2)}, u32[]{:S(2)}) collective-permute-start(bf16[136,1536]{1,0:T(8,128)(2,1)S(1)} %collective-permute-done.16.refs_1_), channel_id=1, source_target_pairs={{0,7},{1,0},{2,1},{3,2},{4,3},{5,4},{6,5},{7,6},{8,15},{9,8},{10,9... | collective-permute-start | bytes 1253384 | tf_op jit(solution)/shard_map/ppermute | solution.py:310
  181.7 25.7 %copy-start.16 = (bf16[136,1536]{1,0:T(8,128)(2,1)}, bf16[136,1536]{1,0:T(8,128)(2,1)S(1)}, u32[]{:S(2)}) copy-start(bf16[136,1536]{1,0:T(8,128)(2,1)S(1)} %collective-permute-done.12.refs_0_) | copy-start | bytes 1253380
  181.7 10.0 %collective-permute-start.13 = (bf16[136,1536]{1,0:T(8,128)(2,1)S(1)}, bf16[136,1536]{1,0:T(8,128)(2,1)S(1)}, u32[]{:S(2)}, u32[]{:S(2)}) collective-permute-start(bf16[136,1536]{1,0:T(8,128)(2,1)S(1)} %collective-permute-done.12.refs_0_), channel_id=1, source_target_pairs={{0,1},{1,2},{2,3},{3,4},{4,5},{5,6},{6,7},{7,0},{8,9},{9,10},{10,1... | collective-permute-start | bytes 1253384 | tf_op jit(solution)/shard_map/ppermute | solution.py:310
  186.7 20.7 %copy-start.15 = (bf16[136,1536]{1,0:T(8,128)(2,1)}, bf16[136,1536]{1,0:T(8,128)(2,1)S(1)}, u32[]{:S(2)}) copy-start(bf16[136,1536]{1,0:T(8,128)(2,1)S(1)} %collective-permute-done.17.refs_1_) | copy-start | bytes 1253380
  186.7 10.0 %collective-permute-start.18 = (bf16[136,1536]{1,0:T(8,128)(2,1)S(1)}, bf16[136,1536]{1,0:T(8,128)(2,1)S(1)}, u32[]{:S(2)}, u32[]{:S(2)}) collective-permute-start(bf16[136,1536]{1,0:T(8,128)(2,1)S(1)} %collective-permute-done.17.refs_1_), channel_id=1, source_target_pairs={{0,7},{1,0},{2,1},{3,2},{4,3},{5,4},{6,5},{7,6},{8,15},{9,8},{10,9... | collective-permute-start | bytes 1253384 | tf_op jit(solution)/shard_map/ppermute | solution.py:310
  191.7 15.7 %copy-start.17 = (bf16[136,1536]{1,0:T(8,128)(2,1)}, bf16[136,1536]{1,0:T(8,128)(2,1)S(1)}, u32[]{:S(2)}) copy-start(bf16[136,1536]{1,0:T(8,128)(2,1)S(1)} %collective-permute-done.13.refs_0_) | copy-start | bytes 1253380
  191.7 10.0 %collective-permute-start.14 = (bf16[136,1536]{1,0:T(8,128)(2,1)S(1)}, bf16[136,1536]{1,0:T(8,128)(2,1)S(1)}, u32[]{:S(2)}, u32[]{:S(2)}) collective-permute-start(bf16[136,1536]{1,0:T(8,128)(2,1)S(1)} %collective-permute-done.13.refs_0_), channel_id=1, source_target_pairs={{0,1},{1,2},{2,3},{3,4},{4,5},{5,6},{6,7},{7,0},{8,9},{9,10},{10,1... | collective-permute-start | bytes 1253384 | tf_op jit(solution)/shard_map/ppermute | solution.py:310
  196.7 10.8 %copy-start.6 = (bf16[136,1536]{1,0:T(8,128)(2,1)}, bf16[136,1536]{1,0:T(8,128)(2,1)S(1)}, u32[]{:S(2)}) copy-start(bf16[136,1536]{1,0:T(8,128)(2,1)S(1)} %collective-permute-done.18.refs_1_) | copy-start | bytes 1253380
  196.7 24.7 %collective-permute-start.19 = (bf16[72,1536]{1,0:T(8,128)(2,1)S(1)}, bf16[72,1536]{1,0:T(8,128)(2,1)S(1)}, u32[]{:S(2)}, u32[]{:S(2)}) collective-permute-start(bf16[72,1536]{1,0:T(8,128)(2,1)S(1)} %slice.37), channel_id=1, source_target_pairs={{0,7},{1,0},{2,1},{3,2},{4,3},{5,4},{6,5},{7,6},{8,15},{9,8},{10,9... | collective-permute-start | bytes 663560 | tf_op jit(solution)/shard_map/ppermute | solution.py:310
  201.7 5.7 %copy-start.7 = (bf16[136,1536]{1,0:T(8,128)(2,1)}, bf16[136,1536]{1,0:T(8,128)(2,1)S(1)}, u32[]{:S(2)}) copy-start(bf16[136,1536]{1,0:T(8,128)(2,1)S(1)} %collective-permute-done.14.refs_0_) | copy-start | bytes 1253380
  201.8 19.6 %collective-permute-start.15 = (bf16[64,1536]{1,0:T(8,128)(2,1)S(1)}, bf16[64,1536]{1,0:T(8,128)(2,1)S(1)}, u32[]{:S(2)}, u32[]{:S(2)}) collective-permute-start(bf16[64,1536]{1,0:T(8,128)(2,1)S(1)} %slice.36), channel_id=1, source_target_pairs={{0,1},{1,2},{2,3},{3,4},{4,5},{5,6},{6,7},{7,0},{8,9},{9,10},{10,1... | collective-permute-start | bytes 589832 | tf_op jit(solution)/shard_map/ppermute | solution.py:310
  221.3 0.7 copy-start.22
  221.3 0.7 copy-start.21
  226.4 12.3 %collective-permute-start.20 = (bf16[8,136,512]{2,1,0:T(8,128)(2,1)}, bf16[8,136,512]{2,1,0:T(8,128)(2,1)S(1)}, u32[]{:S(2)}, u32[]{:S(2)}) collective-permute-start(bf16[8,136,512]{2,1,0:T(8,128)(2,1)} %get-tuple-element.59), channel_id=1, source_target_pairs={{0,32},{32,0},{1,33},{33,1},{2,34},{34,2},{3,35},{35,3},{4,36},{36... | collective-permute-start | bytes 3342344 | tf_op jit(solution)/shard_map/ppermute | solution.py:340
  241.2 3.7 %copy-start.1 = (bf16[8,136,512]{2,1,0:T(8,128)(2,1)S(1)}, bf16[8,136,512]{2,1,0:T(8,128)(2,1)}, u32[]{:S(2)}) copy-start(bf16[8,136,512]{2,1,0:T(8,128)(2,1)} %copy-done) | copy-start | bytes 3342340
  241.2 3.7 %copy-start.4 = (bf16[8,136,512]{2,1,0:T(8,128)(2,1)S(1)}, bf16[8,136,512]{2,1,0:T(8,128)(2,1)}, u32[]{:S(2)}) copy-start(bf16[8,136,512]{2,1,0:T(8,128)(2,1)} %copy-done.3) | copy-start | bytes 3342340
  241.2 19.3 %all-to-all-start.2 = ((bf16[8,136,512]{2,1,0:T(8,128)(2,1)}), bf16[8,136,512]{2,1,0:T(8,128)(2,1)S(1)}, u32[]{:S(2)}, u32[]{:S(2)}) async-start(bf16[8,136,512]{2,1,0:T(8,128)(2,1)} %add_convert_fusion), calls=%async_computation.2 | async-start | bytes 2228224 | tf_op jit(solution)/shard_map/all_to_all | solution.py:342
  244.9 2.3 copy-start.2
  250.6 14.9 %copy-start.5 = (bf16[8,136,512]{2,1,0:T(8,128)(2,1)S(1)}, bf16[8,136,512]{2,1,0:T(8,128)(2,1)}, u32[]{:S(2)}) copy-start(bf16[8,136,512]{2,1,0:T(8,128)(2,1)} %get-tuple-element.63) | copy-start | bytes 3342340
  261.4 14.1 %all-to-all-start.3 = ((bf16[8,17,512]{2,1,0:T(8,128)(2,1)}), bf16[8,17,512]{2,1,0:T(8,128)(2,1)S(1)}, u32[]{:S(2)}, u32[]{:S(2)}) async-start(bf16[8,17,512]{2,1,0:T(8,128)(2,1)} %reshape.28), calls=%async_computation.3 | async-start | bytes 393216 | tf_op jit(solution)/shard_map/all_to_all | solution.py:345
  275.5 0.7 copy-start.8

commit v2 on v1

--- a/solution.py
+++ b/solution.py
@@ -8,9 +8,12 @@
 from jax.sharding import Mesh, PartitionSpec as P
 
 
-CHIPS = ("ylo", "x")
+NEAR = ("ylo", "core", "expert")
 BF16 = jnp.bfloat16
 F32 = jnp.float32
+call = functools.partial(
+    pl.pallas_call, compiler_params=pltpu.CompilerParams(vmem_limit_bytes=14 << 20)
+)
 
 
 def place_of(ids_row, expert, slots):
@@ -28,22 +31,31 @@
 
 
 def send_kernel(ids_ref, gates_ref, tok_ref, dout_ref, out_ref):
-    experts, slots = out_ref.shape[0] // 2, out_ref.shape[1]
+    copies, both, slots, _ = out_ref.shape
+    experts = both // 2
     ids, gates = ids_ref[...], gates_ref[...]
     for e in range(experts):
         place = place_of(ids, e, slots)
         gate_row = jnp.sum(jnp.where(ids == e, gates, 0.0), axis=0, keepdims=True)
         gate_slot = jnp.sum(place * gate_row, axis=1, keepdims=True)
         pick = place.astype(BF16)
-        out_ref[e] = jnp.dot(pick, tok_ref[...], preferred_element_type=F32).astype(BF16)
+        rows = jnp.dot(pick, tok_ref[...], preferred_element_type=F32).astype(BF16)
         grads = jnp.dot(pick, dout_ref[...], preferred_element_type=F32)
-        out_ref[experts + e] = (gate_slot * grads).astype(BF16)
+        grads = (gate_slot * grads).astype(BF16)
+        for c in range(copies):
+            out_ref[c, e] = rows
+            out_ref[c, experts + e] = grads
 
 
 def finish_kernel(ids_ref, gates_ref, back_ref, out_ref, dtok_ref):
-    experts, slots = back_ref.shape[0] // 2, back_ref.shape[1]
+    copies, both, slots, _ = back_ref.shape
+    experts = both // 2
     ids, gates = ids_ref[...], gates_ref[...]
     tokens = ids.shape[1]
+
+    def returned(k):
+        return sum(back_ref[c, k].astype(F32) for c in range(copies)).astype(BF16)
+
     eye = lax.broadcasted_iota(jnp.int32, (tokens, tokens), 0) == lax.broadcasted_iota(
         jnp.int32, (tokens, tokens), 1
     )
@@ -59,8 +71,8 @@
             dimension_numbers=(((0,), (0,)), ((), ())),
             preferred_element_type=F32,
         )
-        out += gate_col * spread(back_ref[e])
-        dtok += spread(back_ref[experts + e])
+        out += gate_col * spread(returned(e))
+        dtok += spread(returned(experts + e))
     out_ref[...] = out.astype(BF16)
     dtok_ref[...] = dtok.astype(BF16)
 
@@ -78,7 +90,7 @@
 
 def pack(expert, saved):
     n, depth, width = saved[0].shape
-    return pl.pallas_call(
+    return call(
         pack_kernel,
         grid_spec=pltpu.PrefetchScalarGridSpec(
             num_scalar_prefetch=1,
@@ -107,7 +119,7 @@
 def place(expert, pieces):
     n, (depth, width3) = len(pieces), pieces[0].shape
     width = width3 // 3
-    return pl.pallas_call(
+    return call(
         place_kernel,
         grid_spec=pltpu.PrefetchScalarGridSpec(
             num_scalar_prefetch=1,
@@ -145,6 +157,8 @@
 
 
 def stepper(steps, ring):
+    if len(steps) > 2:
+        return lambda i, o: (o[0] + (steps[0] - (i >> 1)) * (1 - 2 * (i & 1))) & (ring - 1)
     first, jump = steps[0], steps[-1] - steps[0]
     return lambda i, o: (o[0] + first + jump * i) & (ring - 1)
 
@@ -155,7 +169,7 @@
     n = len(steps)
     chunk = stepper(steps, ring)
     heights = heights or (height,) * n
-    return pl.pallas_call(
+    return call(
         functools.partial(part_kernel, n),
         grid_spec=pltpu.PrefetchScalarGridSpec(
             num_scalar_prefetch=1,
@@ -174,6 +188,25 @@
             transcendentals=0,
         ),
     )(where, mine, other, w)
+
+
+def merge_kernel(lower, own_ref, got_ref, out_ref):
+    upper = lower + got_ref.shape[0]
+    if lower:
+        out_ref[:lower] = own_ref[:lower]
+    if upper < out_ref.shape[0]:
+        out_ref[upper:] = own_ref[upper:]
+    out_ref[lower:upper] = own_ref[lower:upper] + got_ref[...]
+
+
+def merge(own, got, lower):
+    return call(
+        functools.partial(merge_kernel, lower),
+        out_shape=jax.ShapeDtypeStruct(own.shape, BF16),
+        cost_estimate=pl.CostEstimate(
+            flops=own.size, bytes_accessed=6 * own.size, transcendentals=0
+        ),
+    )(own, got)
 
 
 def act_kernel(a_ref, b_ref, c_ref, out_ref):
@@ -239,7 +272,7 @@
         in_specs += [pl.BlockSpec(memory_space=pl.ANY)] * 3
         aliases = {n + 2: 0, n + 3: 1, n + 4: 2}
         extra = held
-    return pl.pallas_call(
+    return call(
         functools.partial(back_kernel, n, halves),
         grid_spec=pltpu.PrefetchScalarGridSpec(
             num_scalar_prefetch=1,
@@ -265,6 +298,13 @@
     )(where, *chunks, w, *extra)
 
 
+def split_kernel(sums_ref, out_ref):
+    slots = out_ref.shape[1]
+    total = sum(sums_ref[k].astype(F32) for k in range(sums_ref.shape[0])).astype(BF16)
+    for k in range(out_ref.shape[0]):
+        out_ref[k] = total[k * slots : (k + 1) * slots]
+
+
 def contract_rows(left, right):
     return lax.dot_general(
         left, right, (((0,), (0,)), ((), ())), preferred_element_type=F32
@@ -282,13 +322,15 @@
     core = lax.axis_index("core")
 
     ids_row, gates_row = route_ids.T, route_gates.T
+    lows = lax.axis_size("ylo")
     sent = pl.pallas_call(
         send_kernel,
-        out_shape=jax.ShapeDtypeStruct((2 * experts, slots, depth), BF16),
+        out_shape=jax.ShapeDtypeStruct((lows, 2 * experts, slots, depth), BF16),
     )(ids_row, gates_row, tokens, d_out)
-    own = lax.all_to_all(sent, ("core", "expert"), 0, 0, tiled=True)
     height = 2 * experts * slots
-    own = own.reshape(height, depth)
+    own = lax.all_to_all(
+        sent.reshape(lows * 2 * experts, slots, depth), NEAR, 0, 0, tiled=True
+    ).reshape(lows * height, depth)
     expert = lax.axis_index("expert")
     pieces = pack(expert, (gate_saved, up_saved, down_saved))
     pieces = [pieces[0]] + [
@@ -297,8 +339,8 @@
     ]
     w = place(expert, pieces)
     mine = lax.all_to_all(
-        jnp.broadcast_to(own[None], (n_chips, height, depth)), CHIPS, 0, 0, tiled=True
-    )
+        jnp.broadcast_to(own[None], (n_chips // lows, lows * height, depth)), "x", 0, 0, tiled=True
+    ).reshape(n_chips, height, depth)
     swap = [(0, 1), (1, 0)]
     other = lax.ppermute(mine, "core", swap)
 
@@ -312,19 +354,18 @@
     where = jnp.stack([here, core]).astype(jnp.int32)
 
     half = height // 16 * 8
-    got = both(*parts(where, (4,), mine, other, w, (half, height - half)))
-    own_r, own_l = parts(where, (3, -3,), mine, other, w)
-    to_right = jnp.concatenate((own_r[:half] + got[0], own_r[half:]), axis=0)
-    to_left = jnp.concatenate((own_l[:half], own_l[half:] + got[1]), axis=0)
-    for k in (2, 1):
-        got = both(to_right, to_left)
-        own_r, own_l = parts(where, (k, -k,), mine, other, w)
-        to_right, to_left = got[0] + own_r, got[1] + own_l
+    far = parts(where, (4,), mine, other, w, (half, height - half))
+    got = both(*far)
+    near = parts(where, (3, -3), mine, other, w)
+    to_right = merge(near[0], got[0], 0)
+    to_left = merge(near[1], got[1], half)
     got = both(to_right, to_left)
-    (own_0,) = parts(where, (0,), mine, other, w)
-    acts = pl.pallas_call(
+    near = parts(where, (2, -2, 1, -1, 0), mine, other, w)
+    got = both(got[0] + near[0], got[1] + near[1])
+    got = both(got[0] + near[2], got[1] + near[3])
+    acts = call(
         act_kernel, out_shape=jax.ShapeDtypeStruct((height, 3 * width), BF16)
-    )(own_0, *got)
+    )(near[4], *got)
 
     got = both(acts, acts)
     held = back(where, (0,), (acts,), w, None, ring)
@@ -339,11 +380,15 @@
 
     got = lax.ppermute(send, "core", swap)
     sums = (keep.astype(F32) + got.astype(F32)).astype(BF16)
-    sums = lax.all_to_all(sums, CHIPS, 0, 0, tiled=True)
-    own = jnp.sum(sums.astype(F32), axis=0).astype(BF16)
-    own = own.reshape(2 * experts, slots, depth)
-    returned = lax.all_to_all(own, ("core", "expert"), 0, 0, tiled=True)
-    out, d_tokens = pl.pallas_call(
+    sums = sums.reshape(n_chips // lows, lows * height, depth)
+    sums = lax.all_to_all(sums, "x", 0, 0, tiled=True)
+    own = call(
+        split_kernel,
+        out_shape=jax.ShapeDtypeStruct((lows * 2 * experts, slots, depth), BF16),
+    )(sums)
+    returned = lax.all_to_all(own, NEAR, 0, 0, tiled=True)
+    returned = returned.reshape(lows, 2 * experts, slots, depth)
+    out, d_tokens = call(
         finish_kernel,
         out_shape=[jax.ShapeDtypeStruct(tokens.shape, BF16)] * 2,
     )(ids_row, gates_row, returned)

time: 281 us -> 263 us (0.936)
  Pallas kernels: 54.5 us -> 22.3 us
  waiting for transfers between devices: 71.1 us -> 85.5 us
  starting transfers between devices: 91.1 us -> 95.1 us
  other arithmetic: 8.05 us -> 4.54 us
  local copies, waits for them, and re-layouts: 8.02 us -> 4.79 us
  blocking collectives: 38.6 us -> 41.8 us
    pallas_call x15 -> x16, Pallas kernels: 54.5 us -> 22.3 us  [the longest x5 8.55 us: back(): call(functools.partial(back_kernel, n, halves), grid_spec=pltpu.PrefetchS...]
    ppermute x8, waiting for transfers between devices: 6.8 us -> 19.4 us  [both(): lax.ppermute(to_right, 'tensor', right)]
    all_to_all x2, blocking collectives: 38.6 us -> 41.8 us  [the longest x1 24.5 us: step(): lax.all_to_all(sent.reshape(lows * 2 * experts, slots, depth), NEAR, 0, 0...]
    add x6 -> x4, other arithmetic: 3.44 us -> 0.45 us  [the longest x2 0.25 us: step(): got = both(got[0] + near[0], got[1] + near[1])]
    all_to_all x2, waiting for transfers between devices: 17 us -> 19.9 us  [the longest x1 10.2 us: step(): sums = lax.all_to_all(sums, 'x', 0, 0, tiled=True)]
  transfers between devices with their start and end apart: 23 -> 23, of which waited for: 13 -> 16; matrix products, arithmetic and copies ran while one was open for 5% -> 4% of each run, Pallas kernels for 14% -> 5%
where the time goes in v2:
time: 263 us; the launch traced here: 261 us
  starting transfers between devices  95.1 us (36%)
  waiting for transfers between devices  85.5 us (33%)
  blocking collectives  41.8 us (16%)
  Pallas kernels  22.3 us (8%)
  matrix products  6.33 us (2%)
  local copies, waits for them, and re-layouts  4.79 us (2%)
  other arithmetic  4.54 us (2%)
    ppermute x8, starting transfers between devices, both(): lax.ppermute(to_left, 'tensor', left)  44.5 us
    ppermute x3, waiting for transfers between devices, step(): lax.ppermute(pieces[r], 'expert', [(i, (i + r) % experts) for i in range(...  33.2 us
    all_to_all x1, blocking collectives, step(): lax.all_to_all(sent.reshape(lows * 2 * experts, slots, depth), NEAR, 0, 0...  24.5 us
    ppermute x8, waiting for transfers between devices, both(): lax.ppermute(to_right, 'tensor', right)  19.4 us
    all_to_all x1, blocking collectives, step(): lax.all_to_all(jnp.broadcast_to(own[None], (n_chips // lows, lows * heigh...  17.3 us
    ppermute x8, starting transfers between devices, both(): lax.ppermute(to_right, 'tensor', right)  15.4 us
    ppermute x3, starting transfers between devices, step(): lax.ppermute(pieces[r], 'expert', [(i, (i + r) % experts) for i in range(...  12.2 us
    ppermute x1, starting transfers between devices, step(): got = lax.ppermute(send, 'core', swap)  11.2 us
  transfers between devices with their start and end apart: 23, of which 16 were waited for; matrix products, arithmetic and copies ran while one was open for 4% of the time, Pallas kernels for 5%

profile of v2, /device:TPU:1, one launch (start us, length us, event | category | flops | bytes accessed | tf_op | source)
XLA Modules:
  0.0 261.5 jit_solution(14529169378669257407)
XLA Ops:
  0.6 2.3 shard_map.110
  2.9 24.5 %all_to_all.20 = bf16[16,17,512]{2,1,0:T(8,128)(2,1)S(1)} all-to-all(bf16[16,17,512]{2,1,0:T(8,128)(2,1)} %bitcast.34), channel_id=1, replica_groups=mesh['ylo'=2,'x'=4,'core'=2,'expert'=4,'tensor'=8] {'ylo','core','expert'}, dimensions={0} | all-to-all | bytes 557056 | tf_op jit(solution)/shard_map/all_to_all | solution.py:331
  27.6 17.3 %all_to_all.21 = bf16[4,272,512]{2,1,0:T(8,128)(2,1)S(1)} all-to-all(bf16[4,272,512]{2,1,0:T(8,128)(2,1)S(1)} %broadcast_in_dim.17), channel_id=1, replica_groups=mesh['ylo'=2,'x'=4,'core'=2,'expert'=4,'tensor'=8] {'x'}, dimensions={0} | all-to-all | bytes 2228224 | tf_op jit(solution)/shard_map/all_to_all | solution.py:341
  44.9 1.9 collective-permute-start
  50.0 4.0 %collective-permute-start.1 = (bf16[512,384]{1,0:T(8,128)(2,1)}, bf16[512,384]{1,0:T(8,128)(2,1)S(1)}, u32[]{:S(2)}, u32[]{:S(2)}) collective-permute-start(bf16[512,384]{1,0:T(8,128)(2,1)} %get-tuple-element.36), channel_id=1, source_target_pairs={{0,8},{8,16},{16,24},{24,0},{1,9},{9,17},{17,25},{25,1},{2,10},{10... | collective-permute-start | bytes 1179656 | tf_op jit(solution)/shard_map/ppermute | solution.py:337
  54.0 4.9 %collective-permute-start.2 = (bf16[512,384]{1,0:T(8,128)(2,1)}, bf16[512,384]{1,0:T(8,128)(2,1)S(1)}, u32[]{:S(2)}, u32[]{:S(2)}) collective-permute-start(bf16[512,384]{1,0:T(8,128)(2,1)} %get-tuple-element.37), channel_id=1, source_target_pairs={{0,16},{8,24},{16,0},{24,8},{1,17},{9,25},{17,1},{25,9},{2,18},{10... | collective-permute-start | bytes 1179656 | tf_op jit(solution)/shard_map/ppermute | solution.py:337
  58.9 3.3 %collective-permute-start.3 = (bf16[512,384]{1,0:T(8,128)(2,1)}, bf16[512,384]{1,0:T(8,128)(2,1)S(1)}, u32[]{:S(2)}, u32[]{:S(2)}) collective-permute-start(bf16[512,384]{1,0:T(8,128)(2,1)} %get-tuple-element.38), channel_id=1, source_target_pairs={{0,24},{8,0},{16,8},{24,16},{1,25},{9,1},{17,9},{25,17},{2,26},{10... | collective-permute-start | bytes 1179656 | tf_op jit(solution)/shard_map/ppermute | solution.py:337
  62.3 7.8 %collective-permute-done.1.refs_1_ = bf16[512,384]{1,0:T(8,128)(2,1)S(1)} collective-permute-done((bf16[512,384]{1,0:T(8,128)(2,1)}, bf16[512,384]{1,0:T(8,128)(2,1)S(1)}, u32[]{:S(2)}, u32[]{:S(2)}) %collective-permute-start.1) | collective-permute-done | bytes 393248 | tf_op jit(solution)/shard_map/ppermute | solution.py:337
  70.1 19.2 %collective-permute-done.2.refs_2_ = bf16[512,384]{1,0:T(8,128)(2,1)S(1)} collective-permute-done((bf16[512,384]{1,0:T(8,128)(2,1)}, bf16[512,384]{1,0:T(8,128)(2,1)S(1)}, u32[]{:S(2)}, u32[]{:S(2)}) %collective-permute-start.2) | collective-permute-done | bytes 393248 | tf_op jit(solution)/shard_map/ppermute | solution.py:337
  89.3 6.2 %collective-permute-done.3.refs_3_ = bf16[512,384]{1,0:T(8,128)(2,1)S(1)} collective-permute-done((bf16[512,384]{1,0:T(8,128)(2,1)}, bf16[512,384]{1,0:T(8,128)(2,1)S(1)}, u32[]{:S(2)}, u32[]{:S(2)}) %collective-permute-start.3) | collective-permute-done | bytes 393248 | tf_op jit(solution)/shard_map/ppermute | solution.py:337
  98.1 10.4 %collective-permute-start.8 = (bf16[72,1536]{1,0:T(8,128)(2,1)S(1)}, bf16[72,1536]{1,0:T(8,128)(2,1)S(1)}, u32[]{:S(2)}, u32[]{:S(2)}) collective-permute-start(bf16[72,1536]{1,0:T(8,128)(2,1)S(1)} %get-tuple-element.45), channel_id=1, source_target_pairs={{0,7},{1,0},{2,1},{3,2},{4,3},{5,4},{6,5},{7,6},{8,15},{9,8},{10,9... | collective-permute-start | bytes 663560 | tf_op jit(solution)/shard_map/ppermute | solution.py:352
  108.5 1.9 collective-permute-start.4
  111.9 5.4 %collective-permute-done.4.got_ref = bf16[64,1536]{1,0:T(8,128)(2,1)S(1)} collective-permute-done((bf16[64,1536]{1,0:T(8,128)(2,1)S(1)}, bf16[64,1536]{1,0:T(8,128)(2,1)S(1)}, u32[]{:S(2)}, u32[]{:S(2)}) %collective-permute-start.4) | collective-permute-done | bytes 196640 | tf_op jit(solution)/shard_map/ppermute | solution.py:352
  117.3 1.9 collective-permute-start.5
  119.3 4.6 %collective-permute-start.9 = (bf16[136,1536]{1,0:T(8,128)(2,1)S(1)}, bf16[136,1536]{1,0:T(8,128)(2,1)S(1)}, u32[]{:S(2)}, u32[]{:S(2)}) collective-permute-start(bf16[136,1536]{1,0:T(8,128)(2,1)S(1)} %shard_map.117), channel_id=1, source_target_pairs={{0,7},{1,0},{2,1},{3,2},{4,3},{5,4},{6,5},{7,6},{8,15},{9,8},{10,9... | collective-permute-start | bytes 1253384 | tf_op jit(solution)/shard_map/ppermute | solution.py:352
  123.9 2.8 %shard_map.113 = (bf16[136,1536]{1,0:T(8,128)(2,1)S(1)}, bf16[136,1536]{1,0:T(8,128)(2,1)S(1)}, bf16[136,1536]{1,0:T(8,128)(2,1)S(1)}, bf16[136,1536]{1,0:T(8,128)(2,1)S(1)}, bf16[136,1536]{1,0:T(8,128)(2,1)S(1)}) custom-call(s32[2]{0:T(128)S(1)} %pad_add_fusion.order_ref, bf16[8,136,512]{2,1,0:T(8,128)(2,1)S(1)} %bitcast.27, ...), custom_call_target="tpu_custom_call" | custom-call | flops 1069547520 | bytes 5054464 | tf_op jit(solution)/shard_map/pallas_call | solution.py:172
  126.7 3.3 %collective-permute-done.5 = bf16[136,1536]{1,0:T(8,128)(2,1)S(1)} collective-permute-done((bf16[136,1536]{1,0:T(8,128)(2,1)S(1)}, bf16[136,1536]{1,0:T(8,128)(2,1)S(1)}, u32[]{:S(2)}, u32[]{:S(2)}) %collective-permute-start.5) | collective-permute-done | bytes 417824 | tf_op jit(solution)/shard_map/ppermute | solution.py:352
  130.1 1.9 collective-permute-start.6
  132.2 4.6 %collective-permute-start.10 = (bf16[136,1536]{1,0:T(8,128)(2,1)S(1)}, bf16[136,1536]{1,0:T(8,128)(2,1)S(1)}, u32[]{:S(2)}, u32[]{:S(2)}) collective-permute-start(bf16[136,1536]{1,0:T(8,128)(2,1)S(1)} %add.17), channel_id=1, source_target_pairs={{0,7},{1,0},{2,1},{3,2},{4,3},{5,4},{6,5},{7,6},{8,15},{9,8},{10,9... | collective-permute-start | bytes 1253384 | tf_op jit(solution)/shard_map/ppermute | solution.py:352
  136.8 5.2 %collective-permute-done.6 = bf16[136,1536]{1,0:T(8,128)(2,1)S(1)} collective-permute-done((bf16[136,1536]{1,0:T(8,128)(2,1)S(1)}, bf16[136,1536]{1,0:T(8,128)(2,1)S(1)}, u32[]{:S(2)}, u32[]{:S(2)}) %collective-permute-start.6) | collective-permute-done | bytes 417824 | tf_op jit(solution)/shard_map/ppermute | solution.py:352
  142.0 1.9 collective-permute-start.7
  144.1 4.6 %collective-permute-start.11 = (bf16[136,1536]{1,0:T(8,128)(2,1)S(1)}, bf16[136,1536]{1,0:T(8,128)(2,1)S(1)}, u32[]{:S(2)}, u32[]{:S(2)}) collective-permute-start(bf16[136,1536]{1,0:T(8,128)(2,1)S(1)} %add.18), channel_id=1, source_target_pairs={{0,7},{1,0},{2,1},{3,2},{4,3},{5,4},{6,5},{7,6},{8,15},{9,8},{10,9... | collective-permute-start | bytes 1253384 | tf_op jit(solution)/shard_map/ppermute | solution.py:352
  148.7 4.3 %collective-permute-done.7.b_ref = bf16[136,1536]{1,0:T(8,128)(2,1)S(1)} collective-permute-done((bf16[136,1536]{1,0:T(8,128)(2,1)S(1)}, bf16[136,1536]{1,0:T(8,128)(2,1)S(1)}, u32[]{:S(2)}, u32[]{:S(2)}) %collective-permute-start.7) | collective-permute-done | bytes 417824 | tf_op jit(solution)/shard_map/ppermute | solution.py:352
  154.3 5.3 %collective-permute-start.16 = (bf16[136,1536]{1,0:T(8,128)(2,1)S(1)}, bf16[136,1536]{1,0:T(8,128)(2,1)S(1)}, u32[]{:S(2)}, u32[]{:S(2)}) collective-permute-start(bf16[136,1536]{1,0:T(8,128)(2,1)S(1)} %shard_map.118.refs_0_), channel_id=1, source_target_pairs={{0,7},{1,0},{2,1},{3,2},{4,3},{5,4},{6,5},{7,6},{8,15},{9,8},{10,9... | collective-permute-start | bytes 1253384 | tf_op jit(solution)/shard_map/ppermute | solution.py:352
  159.6 1.9 collective-permute-start.12
  161.6 3.0 %collective-permute-done.16.refs_1_ = bf16[136,1536]{1,0:T(8,128)(2,1)S(1)} collective-permute-done((bf16[136,1536]{1,0:T(8,128)(2,1)S(1)}, bf16[136,1536]{1,0:T(8,128)(2,1)S(1)}, u32[]{:S(2)}, u32[]{:S(2)}) %collective-permute-start.16) | collective-permute-done | bytes 417824 | tf_op jit(solution)/shard_map/ppermute | solution.py:352
  164.6 5.0 %collective-permute-start.17 = (bf16[136,1536]{1,0:T(8,128)(2,1)S(1)}, bf16[136,1536]{1,0:T(8,128)(2,1)S(1)}, u32[]{:S(2)}, u32[]{:S(2)}) collective-permute-start(bf16[136,1536]{1,0:T(8,128)(2,1)S(1)} %collective-permute-done.16.refs_1_), channel_id=1, source_target_pairs={{0,7},{1,0},{2,1},{3,2},{4,3},{5,4},{6,5},{7,6},{8,15},{9,8},{10,9... | collective-permute-start | bytes 1253384 | tf_op jit(solution)/shard_map/ppermute | solution.py:352
  169.6 1.9 collective-permute-start.13
  171.6 3.0 %collective-permute-done.17.refs_1_ = bf16[136,1536]{1,0:T(8,128)(2,1)S(1)} collective-permute-done((bf16[136,1536]{1,0:T(8,128)(2,1)S(1)}, bf16[136,1536]{1,0:T(8,128)(2,1)S(1)}, u32[]{:S(2)}, u32[]{:S(2)}) %collective-permute-start.17) | collective-permute-done | bytes 417824 | tf_op jit(solution)/shard_map/ppermute | solution.py:352
  174.6 5.0 %collective-permute-start.18 = (bf16[136,1536]{1,0:T(8,128)(2,1)S(1)}, bf16[136,1536]{1,0:T(8,128)(2,1)S(1)}, u32[]{:S(2)}, u32[]{:S(2)}) collective-permute-start(bf16[136,1536]{1,0:T(8,128)(2,1)S(1)} %collective-permute-done.17.refs_1_), channel_id=1, source_target_pairs={{0,7},{1,0},{2,1},{3,2},{4,3},{5,4},{6,5},{7,6},{8,15},{9,8},{10,9... | collective-permute-start | bytes 1253384 | tf_op jit(solution)/shard_map/ppermute | solution.py:352
  179.6 1.9 collective-permute-start.14
  181.5 3.6 %collective-permute-done.18.refs_1_ = bf16[136,1536]{1,0:T(8,128)(2,1)S(1)} collective-permute-done((bf16[136,1536]{1,0:T(8,128)(2,1)S(1)}, bf16[136,1536]{1,0:T(8,128)(2,1)S(1)}, u32[]{:S(2)}, u32[]{:S(2)}) %collective-permute-start.18) | collective-permute-done | bytes 417824 | tf_op jit(solution)/shard_map/ppermute | solution.py:352
  185.2 5.0 %collective-permute-start.19 = (bf16[72,1536]{1,0:T(8,128)(2,1)S(1)}, bf16[72,1536]{1,0:T(8,128)(2,1)S(1)}, u32[]{:S(2)}, u32[]{:S(2)}) collective-permute-start(bf16[72,1536]{1,0:T(8,128)(2,1)S(1)} %slice.21), channel_id=1, source_target_pairs={{0,7},{1,0},{2,1},{3,2},{4,3},{5,4},{6,5},{7,6},{8,15},{9,8},{10,9... | collective-permute-start | bytes 663560 | tf_op jit(solution)/shard_map/ppermute | solution.py:352
  190.5 1.9 collective-permute-start.15
  193.6 1.9 shard_map.120
  195.5 1.9 shard_map.121
  197.5 1.9 shard_map.122
  201.9 11.2 %collective-permute-start.20 = (bf16[8,136,512]{2,1,0:T(8,128)(2,1)S(1)}, bf16[8,136,512]{2,1,0:T(8,128)(2,1)S(1)}, u32[]{:S(2)}, u32[]{:S(2)}) collective-permute-start(bf16[8,136,512]{2,1,0:T(8,128)(2,1)S(1)} %get-tuple-element.61), channel_id=1, source_target_pairs={{0,32},{32,0},{1,33},{33,1},{2,34},{34,2},{3,35},{35,3},{4,36},{36... | collective-permute-start | bytes 3342344 | tf_op jit(solution)/shard_map/ppermute | solution.py:381
  213.1 2.4 collective-permute-done.20
  216.8 4.3 %all-to-all-start.2 = ((bf16[4,272,512]{2,1,0:T(8,128)(2,1)}), bf16[4,272,512]{2,1,0:T(8,128)(2,1)}, u32[]{:S(2)}, u32[]{:S(2)}) async-start(bf16[4,272,512]{2,1,0:T(8,128)(2,1)} %bitcast.33), calls=%async_computation.2 | async-start | bytes 2228224 | tf_op jit(solution)/shard_map/all_to_all | solution.py:384
  221.0 2.7 %broadcast_select_fusion = (bf16[8,136,512]{2,1,0:T(8,128)(2,1)}, bf16[8,136,512]{2,1,0:T(8,128)(2,1)S(1)}) fusion(bf16[8,136,512]{2,1,0:T(8,128)(2,1)} %copy-done.1, bf16[8,136,512]{2,1,0:T(8,128)(2,1)} %bitcast.28, pred[]{:T(512)S(6)} %eq.4), kind=kLoop, calls=%fused_computation.10 | loop fusion | flops 1114112 | bytes 4456449 | tf_op jit(solution)/shard_map/jit(_where)/select_n | solution.py:398
  224.8 1.7 fusion.1
  226.4 10.2 %all-to-all-done.2.sums_ref = bf16[4,272,512]{2,1,0:T(8,128)(2,1)} async-done(((bf16[4,272,512]{2,1,0:T(8,128)(2,1)}), bf16[4,272,512]{2,1,0:T(8,128)(2,1)}, u32[]{:S(2)}, u32[]{:S(2)}) %all-to-all-start.2) | async-done | bytes 1114144 | tf_op jit(solution)/shard_map/all_to_all | solution.py:384
  238.8 5.7 %all-to-all-start.3 = ((bf16[16,17,512]{2,1,0:T(8,128)(2,1)}), bf16[16,17,512]{2,1,0:T(8,128)(2,1)}, u32[]{:S(2)}, u32[]{:S(2)}) async-start(bf16[16,17,512]{2,1,0:T(8,128)(2,1)} %copy-done.2), calls=%async_computation.3 | async-start | bytes 786432 | tf_op jit(solution)/shard_map/all_to_all | solution.py:389
  244.5 3.0 %fusion = bf16[1,512,512]{2,1,0:T(8,128)(2,1)} fusion(bf16[1088,512]{1,0:T(8,128)(2,1)} %bitcast.37, bf16[1088,1536]{1,0:T(8,128)(2,1)S(1)} %bitcast.22), kind=kOutput, calls=%fused_computation.4 | convolution fusion | flops 570687488 | bytes 2752512 | tf_op jit(solution)/shard_map/dot_general | solution.py:309
  247.5 1.7 fusion.2
  249.2 9.7 %all-to-all-done.3 = bf16[16,17,512]{2,1,0:T(8,128)(2,1)} async-done(((bf16[16,17,512]{2,1,0:T(8,128)(2,1)}), bf16[16,17,512]{2,1,0:T(8,128)(2,1)}, u32[]{:S(2)}, u32[]{:S(2)}) %all-to-all-start.3) | async-done | bytes 278560 | tf_op jit(solution)/shard_map/all_to_all | solution.py:389
  258.9 2.5 shard_map.125
  (54 shorter events, 17.8 us)
Async XLA Ops:
  27.6 19.2 %copy-start.3 = (bf16[4,512,128]{2,1,0:T(8,128)(2,1)S(1)}, bf16[4,512,128]{2,1,0:T(8,128)(2,1)}, u32[]{:S(2)}) copy-start(bf16[4,512,128]{2,1,0:T(8,128)(2,1)} %refs_0_.1) | copy-start | bytes 1572868
  27.6 19.2 %copy-start.4 = (bf16[4,512,128]{2,1,0:T(8,128)(2,1)S(1)}, bf16[4,512,128]{2,1,0:T(8,128)(2,1)}, u32[]{:S(2)}) copy-start(bf16[4,512,128]{2,1,0:T(8,128)(2,1)} %refs_1_.1) | copy-start | bytes 1572868
  44.9 79.0 %copy-start = (bf16[4,272,512]{2,1,0:T(8,128)(2,1)}, bf16[4,272,512]{2,1,0:T(8,128)(2,1)S(1)}, u32[]{:S(2)}) copy-start(bf16[4,272,512]{2,1,0:T(8,128)(2,1)S(1)} %all_to_all.21) | copy-start | bytes 3342340
  44.9 52.2 %collective-permute-start = (bf16[8,136,512]{2,1,0:T(8,128)(2,1)S(1)}, bf16[8,136,512]{2,1,0:T(8,128)(2,1)S(1)}, u32[]{:S(2)}, u32[]{:S(2)}) collective-permute-start(bf16[8,136,512]{2,1,0:T(8,128)(2,1)S(1)} %bitcast.24), channel_id=1, source_target_pairs={{0,32},{32,0},{1,33},{33,1},{2,34},{34,2},{3,35},{35,3},{4,36},{36... | collective-permute-start | bytes 3342344 | tf_op jit(solution)/shard_map/ppermute | solution.py:345
  46.8 1.0 copy-start.5
  49.2 0.8 copy-start.6
  50.0 20.1 %collective-permute-start.1 = (bf16[512,384]{1,0:T(8,128)(2,1)}, bf16[512,384]{1,0:T(8,128)(2,1)S(1)}, u32[]{:S(2)}, u32[]{:S(2)}) collective-permute-start(bf16[512,384]{1,0:T(8,128)(2,1)} %get-tuple-element.36), channel_id=1, source_target_pairs={{0,8},{8,16},{16,24},{24,0},{1,9},{9,17},{17,25},{25,1},{2,10},{10... | collective-permute-start | bytes 1179656 | tf_op jit(solution)/shard_map/ppermute | solution.py:337
  54.0 35.2 %collective-permute-start.2 = (bf16[512,384]{1,0:T(8,128)(2,1)}, bf16[512,384]{1,0:T(8,128)(2,1)S(1)}, u32[]{:S(2)}, u32[]{:S(2)}) collective-permute-start(bf16[512,384]{1,0:T(8,128)(2,1)} %get-tuple-element.37), channel_id=1, source_target_pairs={{0,16},{8,24},{16,0},{24,8},{1,17},{9,25},{17,1},{25,9},{2,18},{10... | collective-permute-start | bytes 1179656 | tf_op jit(solution)/shard_map/ppermute | solution.py:337
  58.9 36.5 %collective-permute-start.3 = (bf16[512,384]{1,0:T(8,128)(2,1)}, bf16[512,384]{1,0:T(8,128)(2,1)S(1)}, u32[]{:S(2)}, u32[]{:S(2)}) collective-permute-start(bf16[512,384]{1,0:T(8,128)(2,1)} %get-tuple-element.38), channel_id=1, source_target_pairs={{0,24},{8,0},{16,8},{24,16},{1,25},{9,1},{17,9},{25,17},{2,26},{10... | collective-permute-start | bytes 1179656 | tf_op jit(solution)/shard_map/ppermute | solution.py:337
  95.4 1.0 copy-start.7
  97.1 26.8 %copy-start.1 = (bf16[8,136,512]{2,1,0:T(8,128)(2,1)}, bf16[8,136,512]{2,1,0:T(8,128)(2,1)S(1)}, u32[]{:S(2)}) copy-start(bf16[8,136,512]{2,1,0:T(8,128)(2,1)S(1)} %collective-permute-done.other_x_ref) | copy-start | bytes 3342340
  98.1 21.2 %collective-permute-start.8 = (bf16[72,1536]{1,0:T(8,128)(2,1)S(1)}, bf16[72,1536]{1,0:T(8,128)(2,1)S(1)}, u32[]{:S(2)}, u32[]{:S(2)}) collective-permute-start(bf16[72,1536]{1,0:T(8,128)(2,1)S(1)} %get-tuple-element.45), channel_id=1, source_target_pairs={{0,7},{1,0},{2,1},{3,2},{4,3},{5,4},{6,5},{7,6},{8,15},{9,8},{10,9... | collective-permute-start | bytes 663560 | tf_op jit(solution)/shard_map/ppermute | solution.py:352
  108.5 8.8 %collective-permute-start.4 = (bf16[64,1536]{1,0:T(8,128)(2,1)S(1)}, bf16[64,1536]{1,0:T(8,128)(2,1)S(1)}, u32[]{:S(2)}, u32[]{:S(2)}) collective-permute-start(bf16[64,1536]{1,0:T(8,128)(2,1)S(1)} %get-tuple-element.41), channel_id=1, source_target_pairs={{0,1},{1,2},{2,3},{3,4},{4,5},{5,6},{6,7},{7,0},{8,9},{9,10},{10,1... | collective-permute-start | bytes 589832 | tf_op jit(solution)/shard_map/ppermute | solution.py:352
  117.3 12.7 %collective-permute-start.5 = (bf16[136,1536]{1,0:T(8,128)(2,1)S(1)}, bf16[136,1536]{1,0:T(8,128)(2,1)S(1)}, u32[]{:S(2)}, u32[]{:S(2)}) collective-permute-start(bf16[136,1536]{1,0:T(8,128)(2,1)S(1)} %shard_map.116), channel_id=1, source_target_pairs={{0,1},{1,2},{2,3},{3,4},{4,5},{5,6},{6,7},{7,0},{8,9},{9,10},{10,1... | collective-permute-start | bytes 1253384 | tf_op jit(solution)/shard_map/ppermute | solution.py:352
  119.3 12.8 %collective-permute-start.9 = (bf16[136,1536]{1,0:T(8,128)(2,1)S(1)}, bf16[136,1536]{1,0:T(8,128)(2,1)S(1)}, u32[]{:S(2)}, u32[]{:S(2)}) collective-permute-start(bf16[136,1536]{1,0:T(8,128)(2,1)S(1)} %shard_map.117), channel_id=1, source_target_pairs={{0,7},{1,0},{2,1},{3,2},{4,3},{5,4},{6,5},{7,6},{8,15},{9,8},{10,9... | collective-permute-start | bytes 1253384 | tf_op jit(solution)/shard_map/ppermute | solution.py:352
  130.1 11.8 %collective-permute-start.6 = (bf16[136,1536]{1,0:T(8,128)(2,1)S(1)}, bf16[136,1536]{1,0:T(8,128)(2,1)S(1)}, u32[]{:S(2)}, u32[]{:S(2)}) collective-permute-start(bf16[136,1536]{1,0:T(8,128)(2,1)S(1)} %add.15), channel_id=1, source_target_pairs={{0,1},{1,2},{2,3},{3,4},{4,5},{5,6},{6,7},{7,0},{8,9},{9,10},{10,1... | collective-permute-start | bytes 1253384 | tf_op jit(solution)/shard_map/ppermute | solution.py:352
  132.2 11.8 %collective-permute-start.10 = (bf16[136,1536]{1,0:T(8,128)(2,1)S(1)}, bf16[136,1536]{1,0:T(8,128)(2,1)S(1)}, u32[]{:S(2)}, u32[]{:S(2)}) collective-permute-start(bf16[136,1536]{1,0:T(8,128)(2,1)S(1)} %add.17), channel_id=1, source_target_pairs={{0,7},{1,0},{2,1},{3,2},{4,3},{5,4},{6,5},{7,6},{8,15},{9,8},{10,9... | collective-permute-start | bytes 1253384 | tf_op jit(solution)/shard_map/ppermute | solution.py:352
  142.0 11.0 %collective-permute-start.7 = (bf16[136,1536]{1,0:T(8,128)(2,1)S(1)}, bf16[136,1536]{1,0:T(8,128)(2,1)S(1)}, u32[]{:S(2)}, u32[]{:S(2)}) collective-permute-start(bf16[136,1536]{1,0:T(8,128)(2,1)S(1)} %add.16), channel_id=1, source_target_pairs={{0,1},{1,2},{2,3},{3,4},{4,5},{5,6},{6,7},{7,0},{8,9},{9,10},{10,1... | collective-permute-start | bytes 1253384 | tf_op jit(solution)/shard_map/ppermute | solution.py:352
  144.1 9.9 %collective-permute-start.11 = (bf16[136,1536]{1,0:T(8,128)(2,1)S(1)}, bf16[136,1536]{1,0:T(8,128)(2,1)S(1)}, u32[]{:S(2)}, u32[]{:S(2)}) collective-permute-start(bf16[136,1536]{1,0:T(8,128)(2,1)S(1)} %add.18), channel_id=1, source_target_pairs={{0,7},{1,0},{2,1},{3,2},{4,3},{5,4},{6,5},{7,6},{8,15},{9,8},{10,9... | collective-permute-start | bytes 1253384 | tf_op jit(solution)/shard_map/ppermute | solution.py:352
  154.3 10.3 %collective-permute-start.16 = (bf16[136,1536]{1,0:T(8,128)(2,1)S(1)}, bf16[136,1536]{1,0:T(8,128)(2,1)S(1)}, u32[]{:S(2)}, u32[]{:S(2)}) collective-permute-start(bf16[136,1536]{1,0:T(8,128)(2,1)S(1)} %shard_map.118.refs_0_), channel_id=1, source_target_pairs={{0,7},{1,0},{2,1},{3,2},{4,3},{5,4},{6,5},{7,6},{8,15},{9,8},{10,9... | collective-permute-start | bytes 1253384 | tf_op jit(solution)/shard_map/ppermute | solution.py:352
  159.6 10.0 %collective-permute-start.12 = (bf16[136,1536]{1,0:T(8,128)(2,1)S(1)}, bf16[136,1536]{1,0:T(8,128)(2,1)S(1)}, u32[]{:S(2)}, u32[]{:S(2)}) collective-permute-start(bf16[136,1536]{1,0:T(8,128)(2,1)S(1)} %shard_map.118.refs_0_), channel_id=1, source_target_pairs={{0,1},{1,2},{2,3},{3,4},{4,5},{5,6},{6,7},{7,0},{8,9},{9,10},{10,1... | collective-permute-start | bytes 1253384 | tf_op jit(solution)/shard_map/ppermute | solution.py:352
  164.6 10.0 %collective-permute-start.17 = (bf16[136,1536]{1,0:T(8,128)(2,1)S(1)}, bf16[136,1536]{1,0:T(8,128)(2,1)S(1)}, u32[]{:S(2)}, u32[]{:S(2)}) collective-permute-start(bf16[136,1536]{1,0:T(8,128)(2,1)S(1)} %collective-permute-done.16.refs_1_), channel_id=1, source_target_pairs={{0,7},{1,0},{2,1},{3,2},{4,3},{5,4},{6,5},{7,6},{8,15},{9,8},{10,9... | collective-permute-start | bytes 1253384 | tf_op jit(solution)/shard_map/ppermute | solution.py:352
  169.6 10.0 %collective-permute-start.13 = (bf16[136,1536]{1,0:T(8,128)(2,1)S(1)}, bf16[136,1536]{1,0:T(8,128)(2,1)S(1)}, u32[]{:S(2)}, u32[]{:S(2)}) collective-permute-start(bf16[136,1536]{1,0:T(8,128)(2,1)S(1)} %collective-permute-done.12.refs_0_), channel_id=1, source_target_pairs={{0,1},{1,2},{2,3},{3,4},{4,5},{5,6},{6,7},{7,0},{8,9},{9,10},{10,1... | collective-permute-start | bytes 1253384 | tf_op jit(solution)/shard_map/ppermute | solution.py:352
  174.6 10.6 %collective-permute-start.18 = (bf16[136,1536]{1,0:T(8,128)(2,1)S(1)}, bf16[136,1536]{1,0:T(8,128)(2,1)S(1)}, u32[]{:S(2)}, u32[]{:S(2)}) collective-permute-start(bf16[136,1536]{1,0:T(8,128)(2,1)S(1)} %collective-permute-done.17.refs_1_), channel_id=1, source_target_pairs={{0,7},{1,0},{2,1},{3,2},{4,3},{5,4},{6,5},{7,6},{8,15},{9,8},{10,9... | collective-permute-start | bytes 1253384 | tf_op jit(solution)/shard_map/ppermute | solution.py:352
  179.6 10.8 %collective-permute-start.14 = (bf16[136,1536]{1,0:T(8,128)(2,1)S(1)}, bf16[136,1536]{1,0:T(8,128)(2,1)S(1)}, u32[]{:S(2)}, u32[]{:S(2)}) collective-permute-start(bf16[136,1536]{1,0:T(8,128)(2,1)S(1)} %collective-permute-done.13.refs_0_), channel_id=1, source_target_pairs={{0,1},{1,2},{2,3},{3,4},{4,5},{5,6},{6,7},{7,0},{8,9},{9,10},{10,1... | collective-permute-start | bytes 1253384 | tf_op jit(solution)/shard_map/ppermute | solution.py:352
  185.2 15.1 %collective-permute-start.19 = (bf16[72,1536]{1,0:T(8,128)(2,1)S(1)}, bf16[72,1536]{1,0:T(8,128)(2,1)S(1)}, u32[]{:S(2)}, u32[]{:S(2)}) collective-permute-start(bf16[72,1536]{1,0:T(8,128)(2,1)S(1)} %slice.21), channel_id=1, source_target_pairs={{0,7},{1,0},{2,1},{3,2},{4,3},{5,4},{6,5},{7,6},{8,15},{9,8},{10,9... | collective-permute-start | bytes 663560 | tf_op jit(solution)/shard_map/ppermute | solution.py:352
  190.5 9.8 %collective-permute-start.15 = (bf16[64,1536]{1,0:T(8,128)(2,1)S(1)}, bf16[64,1536]{1,0:T(8,128)(2,1)S(1)}, u32[]{:S(2)}, u32[]{:S(2)}) collective-permute-start(bf16[64,1536]{1,0:T(8,128)(2,1)S(1)} %slice.20), channel_id=1, source_target_pairs={{0,1},{1,2},{2,3},{3,4},{4,5},{5,6},{6,7},{7,0},{8,9},{9,10},{10,1... | collective-permute-start | bytes 589832 | tf_op jit(solution)/shard_map/ppermute | solution.py:352
  201.9 13.6 %collective-permute-start.20 = (bf16[8,136,512]{2,1,0:T(8,128)(2,1)S(1)}, bf16[8,136,512]{2,1,0:T(8,128)(2,1)S(1)}, u32[]{:S(2)}, u32[]{:S(2)}) collective-permute-start(bf16[8,136,512]{2,1,0:T(8,128)(2,1)S(1)} %get-tuple-element.61), channel_id=1, source_target_pairs={{0,32},{32,0},{1,33},{33,1},{2,34},{34,2},{3,35},{35,3},{4,36},{36... | collective-permute-start | bytes 3342344 | tf_op jit(solution)/shard_map/ppermute | solution.py:381
  216.8 19.9 %all-to-all-start.2 = ((bf16[4,272,512]{2,1,0:T(8,128)(2,1)}), bf16[4,272,512]{2,1,0:T(8,128)(2,1)}, u32[]{:S(2)}, u32[]{:S(2)}) async-start(bf16[4,272,512]{2,1,0:T(8,128)(2,1)} %bitcast.33), calls=%async_computation.2 | async-start | bytes 2228224 | tf_op jit(solution)/shard_map/all_to_all | solution.py:384
  223.8 1.0 copy-start.11
  238.1 0.7 copy-start.2
  238.8 20.1 %all-to-all-start.3 = ((bf16[16,17,512]{2,1,0:T(8,128)(2,1)}), bf16[16,17,512]{2,1,0:T(8,128)(2,1)}, u32[]{:S(2)}, u32[]{:S(2)}) async-start(bf16[16,17,512]{2,1,0:T(8,128)(2,1)} %copy-done.2), calls=%async_computation.3 | async-start | bytes 786432 | tf_op jit(solution)/shard_map/all_to_all | solution.py:389
  244.5 3.0 %copy-start.10 = (bf16[8,136,512]{2,1,0:T(8,128)(2,1)S(1)}, bf16[8,136,512]{2,1,0:T(8,128)(2,1)}, u32[]{:S(2)}) copy-start(bf16[8,136,512]{2,1,0:T(8,128)(2,1)} %get-tuple-element.65) | copy-start | bytes 3342340
  247.5 11.4 %copy-start.8 = (s32[28,2]{0,1:T(2,128)S(1)}, s32[28,2]{0,1:T(2,128)}, u32[]{:S(2)}) copy-start(s32[28,2]{0,1:T(2,128)} %param.8) | copy-start | bytes 676
  247.5 11.4 %copy-start.9 = (f32[28,2]{0,1:T(2,128)S(1)}, f32[28,2]{0,1:T(2,128)}, u32[]{:S(2)}) copy-start(f32[28,2]{0,1:T(2,128)} %param.9) | copy-start | bytes 676

commit v3 on v2

--- a/solution.py
+++ b/solution.py
@@ -48,14 +48,9 @@
 
 
 def finish_kernel(ids_ref, gates_ref, back_ref, out_ref, dtok_ref):
-    copies, both, slots, _ = back_ref.shape
-    experts = both // 2
+    experts, slots = back_ref.shape[0] // 2, back_ref.shape[1]
     ids, gates = ids_ref[...], gates_ref[...]
     tokens = ids.shape[1]
-
-    def returned(k):
-        return sum(back_ref[c, k].astype(F32) for c in range(copies)).astype(BF16)
-
     eye = lax.broadcasted_iota(jnp.int32, (tokens, tokens), 0) == lax.broadcasted_iota(
         jnp.int32, (tokens, tokens), 1
     )
@@ -71,8 +66,8 @@
             dimension_numbers=(((0,), (0,)), ((), ())),
             preferred_element_type=F32,
         )
-        out += gate_col * spread(returned(e))
-        dtok += spread(returned(experts + e))
+        out += gate_col * spread(back_ref[e])
+        dtok += spread(back_ref[experts + e])
     out_ref[...] = out.astype(BF16)
     dtok_ref[...] = dtok.astype(BF16)
 
@@ -267,11 +262,17 @@
     in_specs = [pl.BlockSpec(c.shape, lambda i, o: (0, 0)) for c in chunks]
     in_specs.append(pl.BlockSpec(w.shape, lambda i, o: (0, 0, 0)))
     aliases = {}
-    extra = ()
-    if held is not None:
-        in_specs += [pl.BlockSpec(memory_space=pl.ANY)] * 3
-        aliases = {n + 2: 0, n + 3: 1, n + 4: 2}
-        extra = held
+    extra = held or ()
+    if halves:
+        extra = held[2:]
+    if extra:
+        in_specs += [pl.BlockSpec(memory_space=pl.ANY)] * len(extra)
+        aliases = {n + 2 + i: 3 - len(extra) + i for i in range(len(extra))}
+
+    def sums(i, o):
+        return (0 if halves else chunk(i, o), 0, 0)
+
+    n_sums = 1 if halves else n_chunks
     return call(
         functools.partial(back_kernel, n, halves),
         grid_spec=pltpu.PrefetchScalarGridSpec(
@@ -279,14 +280,14 @@
             grid=(grid,),
             in_specs=in_specs,
             out_specs=[
-                pl.BlockSpec((1, height, depth), lambda i, o: (chunk(i, o), 0, 0)),
-                pl.BlockSpec((1, height, depth), lambda i, o: (chunk(i, o), 0, 0)),
+                pl.BlockSpec((1, height, depth), sums),
+                pl.BlockSpec((1, height, depth), sums),
                 pl.BlockSpec((1, height, width3), lambda i, o: (chunk(i, o), 0, 0)),
             ],
         ),
         out_shape=[
-            jax.ShapeDtypeStruct((n_chunks, height, depth), BF16),
-            jax.ShapeDtypeStruct((n_chunks, height, depth), BF16),
+            jax.ShapeDtypeStruct((n_sums, height, depth), BF16),
+            jax.ShapeDtypeStruct((n_sums, height, depth), BF16),
             jax.ShapeDtypeStruct((n_chunks, height, width3), BF16),
         ],
         input_output_aliases=aliases,
@@ -296,6 +297,43 @@
             transcendentals=0,
         ),
     )(where, *chunks, w, *extra)
+
+
+def join_kernel(keep_ref, got_ref, out_ref):
+    out_ref[...] = (keep_ref[...].astype(F32) + got_ref[...].astype(F32)).astype(BF16)
+
+
+def join_last_kernel(where_ref, keep_ref, got_ref, held_ref, out_ref):
+    join_kernel(keep_ref, got_ref, out_ref)
+
+
+def join(keep, got):
+    shape = keep.shape
+    block = pl.BlockSpec((shape[0] // 2, *shape[1:]), lambda i: (i, 0, 0))
+    return call(
+        join_kernel,
+        grid=(2,),
+        in_specs=[block, block],
+        out_specs=block,
+        out_shape=jax.ShapeDtypeStruct(shape, BF16),
+    )(keep, got)
+
+
+def join_last(where, steps, keep, got, held):
+    shape = keep.shape
+    chunk = stepper(steps, held.shape[0])
+    flat = pl.BlockSpec(shape, lambda i, o: (0, 0, 0))
+    return call(
+        join_last_kernel,
+        grid_spec=pltpu.PrefetchScalarGridSpec(
+            num_scalar_prefetch=1,
+            grid=(1,),
+            in_specs=[flat, flat, pl.BlockSpec(memory_space=pl.ANY)],
+            out_specs=pl.BlockSpec(shape, lambda i, o: (chunk(i, o), 0, 0)),
+        ),
+        out_shape=jax.ShapeDtypeStruct(held.shape, BF16),
+        input_output_aliases={3: 0},
+    )(where, keep, got, held)
 
 
 def split_kernel(sums_ref, out_ref):
@@ -376,18 +414,17 @@
         else:
             got = both(now[0][:half], now[1][half:])
         held = back(where, (-k, k,), now, w, held, ring)
+    early = lax.ppermute(held[1], "core", swap)
     keep, send, acts = back(where, (4,), got, w, held, ring, halves=True)
-
-    got = lax.ppermute(send, "core", swap)
-    sums = (keep.astype(F32) + got.astype(F32)).astype(BF16)
-    sums = sums.reshape(n_chips // lows, lows * height, depth)
-    sums = lax.all_to_all(sums, "x", 0, 0, tiled=True)
+    late = lax.ppermute(send, "core", swap)
+    sums = join(held[0], early)
+    sums = join_last(where, (4,), keep, late, sums)
+    sums = lax.all_to_all(sums, ("x", "ylo"), 0, 0, tiled=True)
     own = call(
         split_kernel,
-        out_shape=jax.ShapeDtypeStruct((lows * 2 * experts, slots, depth), BF16),
+        out_shape=jax.ShapeDtypeStruct((2 * experts, slots, depth), BF16),
     )(sums)
-    returned = lax.all_to_all(own, NEAR, 0, 0, tiled=True)
-    returned = returned.reshape(lows, 2 * experts, slots, depth)
+    returned = lax.all_to_all(own, ("core", "expert"), 0, 0, tiled=True)
     out, d_tokens = call(
         finish_kernel,
         out_shape=[jax.ShapeDtypeStruct(tokens.shape, BF16)] * 2,

time: 263 us -> 261 us (level)
  the two profiles are of different devices: /device:TPU:1 before, /device:TPU:6 now
where the time goes in v3:
time: 261 us; the launch traced here: 256 us
  starting transfers between devices  93.3 us (36%)
  waiting for transfers between devices  87.3 us (33%)
  blocking collectives  38 us (15%)
  Pallas kernels  22.9 us (9%)
  matrix products  6.25 us (2%)
  local copies, waits for them, and re-layouts  4.04 us (2%)
  other arithmetic  3.25 us (1%)
    ppermute x8, starting transfers between devices, both(): lax.ppermute(to_left, 'tensor', left)  47.8 us
    ppermute x8, waiting for transfers between devices, both(): lax.ppermute(to_right, 'tensor', right)  36.6 us
    ppermute x3, waiting for transfers between devices, step(): lax.ppermute(pieces[r], 'expert', [(i, (i + r) % experts) for i in range(...  32.8 us
    all_to_all x1, blocking collectives, step(): lax.all_to_all(sent.reshape(lows * 2 * experts, slots, depth), NEAR, 0, 0...  19.5 us
    all_to_all x1, blocking collectives, step(): lax.all_to_all(jnp.broadcast_to(own[None], (n_chips // lows, lows * heigh...  18.5 us
    ppermute x8, starting transfers between devices, both(): lax.ppermute(to_right, 'tensor', right)  15.3 us
    ppermute x3, starting transfers between devices, step(): lax.ppermute(pieces[r], 'expert', [(i, (i + r) % experts) for i in range(...  12.5 us
    all_to_all x1, waiting for transfers between devices, step(): sums = lax.all_to_all(sums, ('x', 'ylo'), 0, 0, tiled=True)  9.19 us
  transfers between devices with their start and end apart: 24, of which 15 were waited for; matrix products, arithmetic and copies ran while one was open for 4% of the time, Pallas kernels for 5%

profile of v3, /device:TPU:6, one launch (start us, length us, event | category | flops | bytes accessed | tf_op | source)
XLA Modules:
  0.0 256.1 jit_solution(16553413881696269975)
XLA Ops:
  0.6 2.3 shard_map.110
  2.9 19.5 %all_to_all.20 = bf16[16,17,512]{2,1,0:T(8,128)(2,1)S(1)} all-to-all(bf16[16,17,512]{2,1,0:T(8,128)(2,1)} %bitcast.31), channel_id=1, replica_groups=mesh['ylo'=2,'x'=4,'core'=2,'expert'=4,'tensor'=8] {'ylo','core','expert'}, dimensions={0} | all-to-all | bytes 557056 | tf_op jit(solution)/shard_map/all_to_all | solution.py:369
  22.6 18.5 %all_to_all.21 = bf16[4,272,512]{2,1,0:T(8,128)(2,1)S(1)} all-to-all(bf16[4,272,512]{2,1,0:T(8,128)(2,1)S(1)} %broadcast_in_dim.17), channel_id=1, replica_groups=mesh['ylo'=2,'x'=4,'core'=2,'expert'=4,'tensor'=8] {'x'}, dimensions={0} | all-to-all | bytes 2228224 | tf_op jit(solution)/shard_map/all_to_all | solution.py:379
  41.2 3.0 %collective-permute-start = (bf16[8,136,512]{2,1,0:T(8,128)(2,1)S(1)}, bf16[8,136,512]{2,1,0:T(8,128)(2,1)S(1)}, u32[]{:S(2)}, u32[]{:S(2)}) collective-permute-start(bf16[8,136,512]{2,1,0:T(8,128)(2,1)S(1)} %bitcast.22), channel_id=1, source_target_pairs={{0,32},{32,0},{1,33},{33,1},{2,34},{34,2},{3,35},{35,3},{4,36},{36... | collective-permute-start | bytes 3342344 | tf_op jit(solution)/shard_map/ppermute | solution.py:383
  47.4 3.8 %collective-permute-start.1 = (bf16[512,384]{1,0:T(8,128)(2,1)}, bf16[512,384]{1,0:T(8,128)(2,1)S(1)}, u32[]{:S(2)}, u32[]{:S(2)}) collective-permute-start(bf16[512,384]{1,0:T(8,128)(2,1)} %get-tuple-element.36), channel_id=1, source_target_pairs={{0,8},{8,16},{16,24},{24,0},{1,9},{9,17},{17,25},{25,1},{2,10},{10... | collective-permute-start | bytes 1179656 | tf_op jit(solution)/shard_map/ppermute | solution.py:375
  51.2 5.2 %collective-permute-start.2 = (bf16[512,384]{1,0:T(8,128)(2,1)}, bf16[512,384]{1,0:T(8,128)(2,1)S(1)}, u32[]{:S(2)}, u32[]{:S(2)}) collective-permute-start(bf16[512,384]{1,0:T(8,128)(2,1)} %get-tuple-element.37), channel_id=1, source_target_pairs={{0,16},{8,24},{16,0},{24,8},{1,17},{9,25},{17,1},{25,9},{2,18},{10... | collective-permute-start | bytes 1179656 | tf_op jit(solution)/shard_map/ppermute | solution.py:375
  56.4 3.5 %collective-permute-start.3 = (bf16[512,384]{1,0:T(8,128)(2,1)}, bf16[512,384]{1,0:T(8,128)(2,1)S(1)}, u32[]{:S(2)}, u32[]{:S(2)}) collective-permute-start(bf16[512,384]{1,0:T(8,128)(2,1)} %get-tuple-element.38), channel_id=1, source_target_pairs={{0,24},{8,0},{16,8},{24,16},{1,25},{9,1},{17,9},{25,17},{2,26},{10... | collective-permute-start | bytes 1179656 | tf_op jit(solution)/shard_map/ppermute | solution.py:375
  60.0 10.5 %collective-permute-done.1.refs_1_ = bf16[512,384]{1,0:T(8,128)(2,1)S(1)} collective-permute-done((bf16[512,384]{1,0:T(8,128)(2,1)}, bf16[512,384]{1,0:T(8,128)(2,1)S(1)}, u32[]{:S(2)}, u32[]{:S(2)}) %collective-permute-start.1) | collective-permute-done | bytes 393248 | tf_op jit(solution)/shard_map/ppermute | solution.py:375
  70.5 17.1 %collective-permute-done.2.refs_2_ = bf16[512,384]{1,0:T(8,128)(2,1)S(1)} collective-permute-done((bf16[512,384]{1,0:T(8,128)(2,1)}, bf16[512,384]{1,0:T(8,128)(2,1)S(1)}, u32[]{:S(2)}, u32[]{:S(2)}) %collective-permute-start.2) | collective-permute-done | bytes 393248 | tf_op jit(solution)/shard_map/ppermute | solution.py:375
  87.6 5.2 %collective-permute-done.3.refs_3_ = bf16[512,384]{1,0:T(8,128)(2,1)S(1)} collective-permute-done((bf16[512,384]{1,0:T(8,128)(2,1)}, bf16[512,384]{1,0:T(8,128)(2,1)S(1)}, u32[]{:S(2)}, u32[]{:S(2)}) %collective-permute-start.3) | collective-permute-done | bytes 393248 | tf_op jit(solution)/shard_map/ppermute | solution.py:375
  95.5 10.7 %collective-permute-start.8 = (bf16[72,1536]{1,0:T(8,128)(2,1)S(1)}, bf16[72,1536]{1,0:T(8,128)(2,1)S(1)}, u32[]{:S(2)}, u32[]{:S(2)}) collective-permute-start(bf16[72,1536]{1,0:T(8,128)(2,1)S(1)} %get-tuple-element.45), channel_id=1, source_target_pairs={{0,7},{1,0},{2,1},{3,2},{4,3},{5,4},{6,5},{7,6},{8,15},{9,8},{10,9... | collective-permute-start | bytes 663560 | tf_op jit(solution)/shard_map/ppermute | solution.py:390
  106.2 1.9 collective-permute-start.4
  109.6 6.3 %collective-permute-done.4.got_ref = bf16[64,1536]{1,0:T(8,128)(2,1)S(1)} collective-permute-done((bf16[64,1536]{1,0:T(8,128)(2,1)S(1)}, bf16[64,1536]{1,0:T(8,128)(2,1)S(1)}, u32[]{:S(2)}, u32[]{:S(2)}) %collective-permute-start.4) | collective-permute-done | bytes 196640 | tf_op jit(solution)/shard_map/ppermute | solution.py:390
  115.9 1.9 collective-permute-start.5
  117.9 5.1 %collective-permute-start.9 = (bf16[136,1536]{1,0:T(8,128)(2,1)S(1)}, bf16[136,1536]{1,0:T(8,128)(2,1)S(1)}, u32[]{:S(2)}, u32[]{:S(2)}) collective-permute-start(bf16[136,1536]{1,0:T(8,128)(2,1)S(1)} %shard_map.117), channel_id=1, source_target_pairs={{0,7},{1,0},{2,1},{3,2},{4,3},{5,4},{6,5},{7,6},{8,15},{9,8},{10,9... | collective-permute-start | bytes 1253384 | tf_op jit(solution)/shard_map/ppermute | solution.py:390
  123.0 2.8 %shard_map.113 = (bf16[136,1536]{1,0:T(8,128)(2,1)S(1)}, bf16[136,1536]{1,0:T(8,128)(2,1)S(1)}, bf16[136,1536]{1,0:T(8,128)(2,1)S(1)}, bf16[136,1536]{1,0:T(8,128)(2,1)S(1)}, bf16[136,1536]{1,0:T(8,128)(2,1)S(1)}) custom-call(s32[2]{0:T(128)S(1)} %pad_add_fusion.order_ref.where_ref, bf16[8,136,512]{2,1,0:T(8,128)(2,1)S(1)} %bitcast.25, ...), custom_call_target="tpu_custom_call" | custom-call | flops 1069547520 | bytes 5054464 | tf_op jit(solution)/shard_map/pallas_call | solution.py:167
  125.8 3.6 %collective-permute-done.5 = bf16[136,1536]{1,0:T(8,128)(2,1)S(1)} collective-permute-done((bf16[136,1536]{1,0:T(8,128)(2,1)S(1)}, bf16[136,1536]{1,0:T(8,128)(2,1)S(1)}, u32[]{:S(2)}, u32[]{:S(2)}) %collective-permute-start.5) | collective-permute-done | bytes 417824 | tf_op jit(solution)/shard_map/ppermute | solution.py:390
  129.5 1.9 collective-permute-start.6
  131.6 5.1 %collective-permute-start.10 = (bf16[136,1536]{1,0:T(8,128)(2,1)S(1)}, bf16[136,1536]{1,0:T(8,128)(2,1)S(1)}, u32[]{:S(2)}, u32[]{:S(2)}) collective-permute-start(bf16[136,1536]{1,0:T(8,128)(2,1)S(1)} %add.14), channel_id=1, source_target_pairs={{0,7},{1,0},{2,1},{3,2},{4,3},{5,4},{6,5},{7,6},{8,15},{9,8},{10,9... | collective-permute-start | bytes 1253384 | tf_op jit(solution)/shard_map/ppermute | solution.py:390
  136.7 5.5 %collective-permute-done.6 = bf16[136,1536]{1,0:T(8,128)(2,1)S(1)} collective-permute-done((bf16[136,1536]{1,0:T(8,128)(2,1)S(1)}, bf16[136,1536]{1,0:T(8,128)(2,1)S(1)}, u32[]{:S(2)}, u32[]{:S(2)}) %collective-permute-start.6) | collective-permute-done | bytes 417824 | tf_op jit(solution)/shard_map/ppermute | solution.py:390
  142.3 1.9 collective-permute-start.7
  144.3 5.1 %collective-permute-start.11 = (bf16[136,1536]{1,0:T(8,128)(2,1)S(1)}, bf16[136,1536]{1,0:T(8,128)(2,1)S(1)}, u32[]{:S(2)}, u32[]{:S(2)}) collective-permute-start(bf16[136,1536]{1,0:T(8,128)(2,1)S(1)} %add.15), channel_id=1, source_target_pairs={{0,7},{1,0},{2,1},{3,2},{4,3},{5,4},{6,5},{7,6},{8,15},{9,8},{10,9... | collective-permute-start | bytes 1253384 | tf_op jit(solution)/shard_map/ppermute | solution.py:390
  149.5 4.6 %collective-permute-done.7.b_ref = bf16[136,1536]{1,0:T(8,128)(2,1)S(1)} collective-permute-done((bf16[136,1536]{1,0:T(8,128)(2,1)S(1)}, bf16[136,1536]{1,0:T(8,128)(2,1)S(1)}, u32[]{:S(2)}, u32[]{:S(2)}) %collective-permute-start.7) | collective-permute-done | bytes 417824 | tf_op jit(solution)/shard_map/ppermute | solution.py:390
  155.7 1.9 collective-permute-start.12
  157.6 5.6 %collective-permute-start.16 = (bf16[136,1536]{1,0:T(8,128)(2,1)S(1)}, bf16[136,1536]{1,0:T(8,128)(2,1)S(1)}, u32[]{:S(2)}, u32[]{:S(2)}) collective-permute-start(bf16[136,1536]{1,0:T(8,128)(2,1)S(1)} %shard_map.118.refs_0_), channel_id=1, source_target_pairs={{0,7},{1,0},{2,1},{3,2},{4,3},{5,4},{6,5},{7,6},{8,15},{9,8},{10,9... | collective-permute-start | bytes 1253384 | tf_op jit(solution)/shard_map/ppermute | solution.py:390
  163.2 4.1 %collective-permute-done.12.refs_0_ = bf16[136,1536]{1,0:T(8,128)(2,1)S(1)} collective-permute-done((bf16[136,1536]{1,0:T(8,128)(2,1)S(1)}, bf16[136,1536]{1,0:T(8,128)(2,1)S(1)}, u32[]{:S(2)}, u32[]{:S(2)}) %collective-permute-start.12) | collective-permute-done | bytes 417824 | tf_op jit(solution)/shard_map/ppermute | solution.py:390
  167.3 1.9 collective-permute-start.13
  169.2 5.1 %collective-permute-start.17 = (bf16[136,1536]{1,0:T(8,128)(2,1)S(1)}, bf16[136,1536]{1,0:T(8,128)(2,1)S(1)}, u32[]{:S(2)}, u32[]{:S(2)}) collective-permute-start(bf16[136,1536]{1,0:T(8,128)(2,1)S(1)} %collective-permute-done.16.refs_1_), channel_id=1, source_target_pairs={{0,7},{1,0},{2,1},{3,2},{4,3},{5,4},{6,5},{7,6},{8,15},{9,8},{10,9... | collective-permute-start | bytes 1253384 | tf_op jit(solution)/shard_map/ppermute | solution.py:390
  174.4 4.4 %collective-permute-done.13.refs_0_ = bf16[136,1536]{1,0:T(8,128)(2,1)S(1)} collective-permute-done((bf16[136,1536]{1,0:T(8,128)(2,1)S(1)}, bf16[136,1536]{1,0:T(8,128)(2,1)S(1)}, u32[]{:S(2)}, u32[]{:S(2)}) %collective-permute-start.13) | collective-permute-done | bytes 417824 | tf_op jit(solution)/shard_map/ppermute | solution.py:390
  178.7 1.9 collective-permute-start.14
  180.7 5.4 %collective-permute-start.18 = (bf16[136,1536]{1,0:T(8,128)(2,1)S(1)}, bf16[136,1536]{1,0:T(8,128)(2,1)S(1)}, u32[]{:S(2)}, u32[]{:S(2)}) collective-permute-start(bf16[136,1536]{1,0:T(8,128)(2,1)S(1)} %collective-permute-done.17.refs_1_), channel_id=1, source_target_pairs={{0,7},{1,0},{2,1},{3,2},{4,3},{5,4},{6,5},{7,6},{8,15},{9,8},{10,9... | collective-permute-start | bytes 1253384 | tf_op jit(solution)/shard_map/ppermute | solution.py:390
  187.3 1.9 shard_map.120
  189.2 1.9 shard_map.121
  191.6 1.9 shard_map.122
  193.5 1.9 collective-permute-start.21
  195.5 5.6 %collective-permute-start.19 = (bf16[72,1536]{1,0:T(8,128)(2,1)S(1)}, bf16[72,1536]{1,0:T(8,128)(2,1)S(1)}, u32[]{:S(2)}, u32[]{:S(2)}) collective-permute-start(bf16[72,1536]{1,0:T(8,128)(2,1)S(1)} %slice.21), channel_id=1, source_target_pairs={{0,7},{1,0},{2,1},{3,2},{4,3},{5,4},{6,5},{7,6},{8,15},{9,8},{10,9... | collective-permute-start | bytes 663560 | tf_op jit(solution)/shard_map/ppermute | solution.py:390
  201.1 1.9 collective-permute-start.15
  203.0 8.2 %collective-permute-done.15.refs_0_ = bf16[64,1536]{1,0:T(8,128)(2,1)S(1)} collective-permute-done((bf16[64,1536]{1,0:T(8,128)(2,1)S(1)}, bf16[64,1536]{1,0:T(8,128)(2,1)S(1)}, u32[]{:S(2)}, u32[]{:S(2)}) %collective-permute-start.15) | collective-permute-done | bytes 196640 | tf_op jit(solution)/shard_map/ppermute | solution.py:390
  212.9 1.9 collective-permute-start.20
  217.7 6.2 %all-to-all-start.2 = ((bf16[8,136,512]{2,1,0:T(8,128)(2,1)}), bf16[8,136,512]{2,1,0:T(8,128)(2,1)}, u32[]{:S(2)}, u32[]{:S(2)}) async-start(bf16[8,136,512]{2,1,0:T(8,128)(2,1)} %copy-done.2), calls=%async_computation.2 | async-start | bytes 2228224 | tf_op jit(solution)/shard_map/all_to_all | solution.py:422
  223.9 2.7 %broadcast_select_fusion = (bf16[8,136,512]{2,1,0:T(8,128)(2,1)}, bf16[8,136,512]{2,1,0:T(8,128)(2,1)S(1)}) fusion(bf16[8,136,512]{2,1,0:T(8,128)(2,1)} %copy-done.1, bf16[8,136,512]{2,1,0:T(8,128)(2,1)} %bitcast.26, pred[]{:T(512)S(6)} %eq.4), kind=kLoop, calls=%fused_computation.9 | loop fusion | flops 1114112 | bytes 4456449 | tf_op jit(solution)/shard_map/jit(_where)/select_n | solution.py:435
  226.7 1.7 fusion.1
  228.3 1.7 fusion
  230.0 9.2 %all-to-all-done.2.sums_ref = bf16[8,136,512]{2,1,0:T(8,128)(2,1)} async-done(((bf16[8,136,512]{2,1,0:T(8,128)(2,1)}), bf16[8,136,512]{2,1,0:T(8,128)(2,1)}, u32[]{:S(2)}, u32[]{:S(2)}) %all-to-all-start.2) | async-done | bytes 1114144 | tf_op jit(solution)/shard_map/all_to_all | solution.py:422
  239.2 2.1 shard_map.126
  241.3 4.5 %all-to-all-start.3 = ((bf16[8,17,512]{2,1,0:T(8,128)(2,1)}), bf16[8,17,512]{2,1,0:T(8,128)(2,1)S(1)}, u32[]{:S(2)}, u32[]{:S(2)}) async-start(bf16[8,17,512]{2,1,0:T(8,128)(2,1)} %shard_map.126), calls=%async_computation.3 | async-start | bytes 393216 | tf_op jit(solution)/shard_map/all_to_all | solution.py:427
  245.7 2.9 %fusion.2 = bf16[1,512,512]{2,1,0:T(8,128)(2,1)} fusion(bf16[1088,512]{1,0:T(8,128)(2,1)} %bitcast.32, bf16[1088,1536]{1,0:T(8,128)(2,1)S(1)} %bitcast.21), kind=kOutput, calls=%fused_computation.5 | convolution fusion | flops 570687488 | bytes 2752512 | tf_op jit(solution)/shard_map/dot_general | solution.py:347
  248.7 5.9 %all-to-all-done.3.back_ref = bf16[8,17,512]{2,1,0:T(8,128)(2,1)S(1)} async-done(((bf16[8,17,512]{2,1,0:T(8,128)(2,1)}), bf16[8,17,512]{2,1,0:T(8,128)(2,1)S(1)}, u32[]{:S(2)}, u32[]{:S(2)}) %all-to-all-start.3) | async-done | bytes 139296 | tf_op jit(solution)/shard_map/all_to_all | solution.py:427
  (53 shorter events, 17.3 us)
Async XLA Ops:
  22.6 21.6 %copy-start.3 = (bf16[4,512,128]{2,1,0:T(8,128)(2,1)S(1)}, bf16[4,512,128]{2,1,0:T(8,128)(2,1)}, u32[]{:S(2)}) copy-start(bf16[4,512,128]{2,1,0:T(8,128)(2,1)} %refs_0_.1) | copy-start | bytes 1572868
  22.6 21.6 %copy-start.4 = (bf16[4,512,128]{2,1,0:T(8,128)(2,1)S(1)}, bf16[4,512,128]{2,1,0:T(8,128)(2,1)}, u32[]{:S(2)}) copy-start(bf16[4,512,128]{2,1,0:T(8,128)(2,1)} %refs_1_.1) | copy-start | bytes 1572868
  41.2 81.8 %copy-start = (bf16[4,272,512]{2,1,0:T(8,128)(2,1)}, bf16[4,272,512]{2,1,0:T(8,128)(2,1)S(1)}, u32[]{:S(2)}) copy-start(bf16[4,272,512]{2,1,0:T(8,128)(2,1)S(1)} %all_to_all.21) | copy-start | bytes 3342340
  41.2 53.4 %collective-permute-start = (bf16[8,136,512]{2,1,0:T(8,128)(2,1)S(1)}, bf16[8,136,512]{2,1,0:T(8,128)(2,1)S(1)}, u32[]{:S(2)}, u32[]{:S(2)}) collective-permute-start(bf16[8,136,512]{2,1,0:T(8,128)(2,1)S(1)} %bitcast.22), channel_id=1, source_target_pairs={{0,32},{32,0},{1,33},{33,1},{2,34},{34,2},{3,35},{35,3},{4,36},{36... | collective-permute-start | bytes 3342344 | tf_op jit(solution)/shard_map/ppermute | solution.py:383
  44.2 1.0 copy-start.5
  46.7 0.8 copy-start.6
  47.4 23.1 %collective-permute-start.1 = (bf16[512,384]{1,0:T(8,128)(2,1)}, bf16[512,384]{1,0:T(8,128)(2,1)S(1)}, u32[]{:S(2)}, u32[]{:S(2)}) collective-permute-start(bf16[512,384]{1,0:T(8,128)(2,1)} %get-tuple-element.36), channel_id=1, source_target_pairs={{0,8},{8,16},{16,24},{24,0},{1,9},{9,17},{17,25},{25,1},{2,10},{10... | collective-permute-start | bytes 1179656 | tf_op jit(solution)/shard_map/ppermute | solution.py:375
  51.2 36.4 %collective-permute-start.2 = (bf16[512,384]{1,0:T(8,128)(2,1)}, bf16[512,384]{1,0:T(8,128)(2,1)S(1)}, u32[]{:S(2)}, u32[]{:S(2)}) collective-permute-start(bf16[512,384]{1,0:T(8,128)(2,1)} %get-tuple-element.37), channel_id=1, source_target_pairs={{0,16},{8,24},{16,0},{24,8},{1,17},{9,25},{17,1},{25,9},{2,18},{10... | collective-permute-start | bytes 1179656 | tf_op jit(solution)/shard_map/ppermute | solution.py:375
  56.4 36.4 %collective-permute-start.3 = (bf16[512,384]{1,0:T(8,128)(2,1)}, bf16[512,384]{1,0:T(8,128)(2,1)S(1)}, u32[]{:S(2)}, u32[]{:S(2)}) collective-permute-start(bf16[512,384]{1,0:T(8,128)(2,1)} %get-tuple-element.38), channel_id=1, source_target_pairs={{0,24},{8,0},{16,8},{24,16},{1,25},{9,1},{17,9},{25,17},{2,26},{10... | collective-permute-start | bytes 1179656 | tf_op jit(solution)/shard_map/ppermute | solution.py:375
  92.9 1.0 copy-start.7
  94.5 28.5 %copy-start.1 = (bf16[8,136,512]{2,1,0:T(8,128)(2,1)}, bf16[8,136,512]{2,1,0:T(8,128)(2,1)S(1)}, u32[]{:S(2)}) copy-start(bf16[8,136,512]{2,1,0:T(8,128)(2,1)S(1)} %collective-permute-done.other_x_ref) | copy-start | bytes 3342340
  95.5 22.3 %collective-permute-start.8 = (bf16[72,1536]{1,0:T(8,128)(2,1)S(1)}, bf16[72,1536]{1,0:T(8,128)(2,1)S(1)}, u32[]{:S(2)}, u32[]{:S(2)}) collective-permute-start(bf16[72,1536]{1,0:T(8,128)(2,1)S(1)} %get-tuple-element.45), channel_id=1, source_target_pairs={{0,7},{1,0},{2,1},{3,2},{4,3},{5,4},{6,5},{7,6},{8,15},{9,8},{10,9... | collective-permute-start | bytes 663560 | tf_op jit(solution)/shard_map/ppermute | solution.py:390
  106.2 9.6 %collective-permute-start.4 = (bf16[64,1536]{1,0:T(8,128)(2,1)S(1)}, bf16[64,1536]{1,0:T(8,128)(2,1)S(1)}, u32[]{:S(2)}, u32[]{:S(2)}) collective-permute-start(bf16[64,1536]{1,0:T(8,128)(2,1)S(1)} %get-tuple-element.41), channel_id=1, source_target_pairs={{0,1},{1,2},{2,3},{3,4},{4,5},{5,6},{6,7},{7,0},{8,9},{9,10},{10,1... | collective-permute-start | bytes 589832 | tf_op jit(solution)/shard_map/ppermute | solution.py:390
  115.9 13.5 %collective-permute-start.5 = (bf16[136,1536]{1,0:T(8,128)(2,1)S(1)}, bf16[136,1536]{1,0:T(8,128)(2,1)S(1)}, u32[]{:S(2)}, u32[]{:S(2)}) collective-permute-start(bf16[136,1536]{1,0:T(8,128)(2,1)S(1)} %shard_map.116), channel_id=1, source_target_pairs={{0,1},{1,2},{2,3},{3,4},{4,5},{5,6},{6,7},{7,0},{8,9},{9,10},{10,1... | collective-permute-start | bytes 1253384 | tf_op jit(solution)/shard_map/ppermute | solution.py:390
  117.9 13.6 %collective-permute-start.9 = (bf16[136,1536]{1,0:T(8,128)(2,1)S(1)}, bf16[136,1536]{1,0:T(8,128)(2,1)S(1)}, u32[]{:S(2)}, u32[]{:S(2)}) collective-permute-start(bf16[136,1536]{1,0:T(8,128)(2,1)S(1)} %shard_map.117), channel_id=1, source_target_pairs={{0,7},{1,0},{2,1},{3,2},{4,3},{5,4},{6,5},{7,6},{8,15},{9,8},{10,9... | collective-permute-start | bytes 1253384 | tf_op jit(solution)/shard_map/ppermute | solution.py:390
  129.5 12.7 %collective-permute-start.6 = (bf16[136,1536]{1,0:T(8,128)(2,1)S(1)}, bf16[136,1536]{1,0:T(8,128)(2,1)S(1)}, u32[]{:S(2)}, u32[]{:S(2)}) collective-permute-start(bf16[136,1536]{1,0:T(8,128)(2,1)S(1)} %add.12), channel_id=1, source_target_pairs={{0,1},{1,2},{2,3},{3,4},{4,5},{5,6},{6,7},{7,0},{8,9},{9,10},{10,1... | collective-permute-start | bytes 1253384 | tf_op jit(solution)/shard_map/ppermute | solution.py:390
  131.6 12.6 %collective-permute-start.10 = (bf16[136,1536]{1,0:T(8,128)(2,1)S(1)}, bf16[136,1536]{1,0:T(8,128)(2,1)S(1)}, u32[]{:S(2)}, u32[]{:S(2)}) collective-permute-start(bf16[136,1536]{1,0:T(8,128)(2,1)S(1)} %add.14), channel_id=1, source_target_pairs={{0,7},{1,0},{2,1},{3,2},{4,3},{5,4},{6,5},{7,6},{8,15},{9,8},{10,9... | collective-permute-start | bytes 1253384 | tf_op jit(solution)/shard_map/ppermute | solution.py:390
  142.3 11.8 %collective-permute-start.7 = (bf16[136,1536]{1,0:T(8,128)(2,1)S(1)}, bf16[136,1536]{1,0:T(8,128)(2,1)S(1)}, u32[]{:S(2)}, u32[]{:S(2)}) collective-permute-start(bf16[136,1536]{1,0:T(8,128)(2,1)S(1)} %add.13), channel_id=1, source_target_pairs={{0,1},{1,2},{2,3},{3,4},{4,5},{5,6},{6,7},{7,0},{8,9},{9,10},{10,1... | collective-permute-start | bytes 1253384 | tf_op jit(solution)/shard_map/ppermute | solution.py:390
  144.3 11.1 %collective-permute-start.11 = (bf16[136,1536]{1,0:T(8,128)(2,1)S(1)}, bf16[136,1536]{1,0:T(8,128)(2,1)S(1)}, u32[]{:S(2)}, u32[]{:S(2)}) collective-permute-start(bf16[136,1536]{1,0:T(8,128)(2,1)S(1)} %add.15), channel_id=1, source_target_pairs={{0,7},{1,0},{2,1},{3,2},{4,3},{5,4},{6,5},{7,6},{8,15},{9,8},{10,9... | collective-permute-start | bytes 1253384 | tf_op jit(solution)/shard_map/ppermute | solution.py:390
  155.7 11.6 %collective-permute-start.12 = (bf16[136,1536]{1,0:T(8,128)(2,1)S(1)}, bf16[136,1536]{1,0:T(8,128)(2,1)S(1)}, u32[]{:S(2)}, u32[]{:S(2)}) collective-permute-start(bf16[136,1536]{1,0:T(8,128)(2,1)S(1)} %shard_map.118.refs_0_), channel_id=1, source_target_pairs={{0,1},{1,2},{2,3},{3,4},{4,5},{5,6},{6,7},{7,0},{8,9},{9,10},{10,1... | collective-permute-start | bytes 1253384 | tf_op jit(solution)/shard_map/ppermute | solution.py:390
  157.6 11.6 %collective-permute-start.16 = (bf16[136,1536]{1,0:T(8,128)(2,1)S(1)}, bf16[136,1536]{1,0:T(8,128)(2,1)S(1)}, u32[]{:S(2)}, u32[]{:S(2)}) collective-permute-start(bf16[136,1536]{1,0:T(8,128)(2,1)S(1)} %shard_map.118.refs_0_), channel_id=1, source_target_pairs={{0,7},{1,0},{2,1},{3,2},{4,3},{5,4},{6,5},{7,6},{8,15},{9,8},{10,9... | collective-permute-start | bytes 1253384 | tf_op jit(solution)/shard_map/ppermute | solution.py:390
  167.3 11.4 %collective-permute-start.13 = (bf16[136,1536]{1,0:T(8,128)(2,1)S(1)}, bf16[136,1536]{1,0:T(8,128)(2,1)S(1)}, u32[]{:S(2)}, u32[]{:S(2)}) collective-permute-start(bf16[136,1536]{1,0:T(8,128)(2,1)S(1)} %collective-permute-done.12.refs_0_), channel_id=1, source_target_pairs={{0,1},{1,2},{2,3},{3,4},{4,5},{5,6},{6,7},{7,0},{8,9},{9,10},{10,1... | collective-permute-start | bytes 1253384 | tf_op jit(solution)/shard_map/ppermute | solution.py:390
  169.2 11.4 %collective-permute-start.17 = (bf16[136,1536]{1,0:T(8,128)(2,1)S(1)}, bf16[136,1536]{1,0:T(8,128)(2,1)S(1)}, u32[]{:S(2)}, u32[]{:S(2)}) collective-permute-start(bf16[136,1536]{1,0:T(8,128)(2,1)S(1)} %collective-permute-done.16.refs_1_), channel_id=1, source_target_pairs={{0,7},{1,0},{2,1},{3,2},{4,3},{5,4},{6,5},{7,6},{8,15},{9,8},{10,9... | collective-permute-start | bytes 1253384 | tf_op jit(solution)/shard_map/ppermute | solution.py:390
  178.7 12.4 %collective-permute-start.14 = (bf16[136,1536]{1,0:T(8,128)(2,1)S(1)}, bf16[136,1536]{1,0:T(8,128)(2,1)S(1)}, u32[]{:S(2)}, u32[]{:S(2)}) collective-permute-start(bf16[136,1536]{1,0:T(8,128)(2,1)S(1)} %collective-permute-done.13.refs_0_), channel_id=1, source_target_pairs={{0,1},{1,2},{2,3},{3,4},{4,5},{5,6},{6,7},{7,0},{8,9},{9,10},{10,1... | collective-permute-start | bytes 1253384 | tf_op jit(solution)/shard_map/ppermute | solution.py:390
  180.7 11.0 %collective-permute-start.18 = (bf16[136,1536]{1,0:T(8,128)(2,1)S(1)}, bf16[136,1536]{1,0:T(8,128)(2,1)S(1)}, u32[]{:S(2)}, u32[]{:S(2)}) collective-permute-start(bf16[136,1536]{1,0:T(8,128)(2,1)S(1)} %collective-permute-done.17.refs_1_), channel_id=1, source_target_pairs={{0,7},{1,0},{2,1},{3,2},{4,3},{5,4},{6,5},{7,6},{8,15},{9,8},{10,9... | collective-permute-start | bytes 1253384 | tf_op jit(solution)/shard_map/ppermute | solution.py:390
  193.5 21.3 %collective-permute-start.21 = (bf16[8,136,512]{2,1,0:T(8,128)(2,1)S(1)}, bf16[8,136,512]{2,1,0:T(8,128)(2,1)S(1)}, u32[]{:S(2)}, u32[]{:S(2)}) collective-permute-start(bf16[8,136,512]{2,1,0:T(8,128)(2,1)S(1)} %get-tuple-element.61), channel_id=1, source_target_pairs={{0,32},{32,0},{1,33},{33,1},{2,34},{34,2},{3,35},{35,3},{4,36},{36... | collective-permute-start | bytes 3342344 | tf_op jit(solution)/shard_map/ppermute | solution.py:417
  195.5 15.8 %collective-permute-start.19 = (bf16[72,1536]{1,0:T(8,128)(2,1)S(1)}, bf16[72,1536]{1,0:T(8,128)(2,1)S(1)}, u32[]{:S(2)}, u32[]{:S(2)}) collective-permute-start(bf16[72,1536]{1,0:T(8,128)(2,1)S(1)} %slice.21), channel_id=1, source_target_pairs={{0,7},{1,0},{2,1},{3,2},{4,3},{5,4},{6,5},{7,6},{8,15},{9,8},{10,9... | collective-permute-start | bytes 663560 | tf_op jit(solution)/shard_map/ppermute | solution.py:390
  201.1 10.1 %collective-permute-start.15 = (bf16[64,1536]{1,0:T(8,128)(2,1)S(1)}, bf16[64,1536]{1,0:T(8,128)(2,1)S(1)}, u32[]{:S(2)}, u32[]{:S(2)}) collective-permute-start(bf16[64,1536]{1,0:T(8,128)(2,1)S(1)} %slice.20), channel_id=1, source_target_pairs={{0,1},{1,2},{2,3},{3,4},{4,5},{5,6},{6,7},{7,0},{8,9},{9,10},{10,1... | collective-permute-start | bytes 589832 | tf_op jit(solution)/shard_map/ppermute | solution.py:390
  212.9 3.3 %collective-permute-start.20 = (bf16[1,136,512]{2,1,0:T(8,128)(2,1)S(1)}, bf16[1,136,512]{2,1,0:T(8,128)(2,1)S(1)}, u32[]{:S(2)}, u32[]{:S(2)}) collective-permute-start(bf16[1,136,512]{2,1,0:T(8,128)(2,1)S(1)} %get-tuple-element.59), channel_id=1, source_target_pairs={{0,32},{32,0},{1,33},{33,1},{2,34},{34,2},{3,35},{35,3},{4,36},{36... | collective-permute-start | bytes 417800 | tf_op jit(solution)/shard_map/ppermute | solution.py:419
  216.7 1.0 copy-start.2
  217.7 21.5 %all-to-all-start.2 = ((bf16[8,136,512]{2,1,0:T(8,128)(2,1)}), bf16[8,136,512]{2,1,0:T(8,128)(2,1)}, u32[]{:S(2)}, u32[]{:S(2)}) async-start(bf16[8,136,512]{2,1,0:T(8,128)(2,1)} %copy-done.2), calls=%async_computation.2 | async-start | bytes 2228224 | tf_op jit(solution)/shard_map/all_to_all | solution.py:422
  241.3 13.3 %all-to-all-start.3 = ((bf16[8,17,512]{2,1,0:T(8,128)(2,1)}), bf16[8,17,512]{2,1,0:T(8,128)(2,1)S(1)}, u32[]{:S(2)}, u32[]{:S(2)}) async-start(bf16[8,17,512]{2,1,0:T(8,128)(2,1)} %shard_map.126), calls=%async_computation.3 | async-start | bytes 393216 | tf_op jit(solution)/shard_map/all_to_all | solution.py:427
  245.7 8.9 %copy-start.8 = (s32[28,2]{0,1:T(2,128)S(1)}, s32[28,2]{0,1:T(2,128)}, u32[]{:S(2)}) copy-start(s32[28,2]{0,1:T(2,128)} %param.8) | copy-start | bytes 676
  245.7 8.9 %copy-start.9 = (f32[28,2]{0,1:T(2,128)S(1)}, f32[28,2]{0,1:T(2,128)}, u32[]{:S(2)}) copy-start(f32[28,2]{0,1:T(2,128)} %param.9) | copy-start | bytes 676

commit v4 on v3

--- a/solution.py
+++ b/solution.py
@@ -299,41 +299,31 @@
     )(where, *chunks, w, *extra)
 
 
-def join_kernel(keep_ref, got_ref, out_ref):
+def join_kernel(where_ref, keep_ref, got_ref, last_keep_ref, last_got_ref, out_ref):
     out_ref[...] = (keep_ref[...].astype(F32) + got_ref[...].astype(F32)).astype(BF16)
-
-
-def join_last_kernel(where_ref, keep_ref, got_ref, held_ref, out_ref):
-    join_kernel(keep_ref, got_ref, out_ref)
-
-
-def join(keep, got):
-    shape = keep.shape
-    block = pl.BlockSpec((shape[0] // 2, *shape[1:]), lambda i: (i, 0, 0))
+    ring = 2 * pl.num_programs(0)
+    last = (where_ref[0] + 4) & (ring - 1)
+
+    @pl.when(pl.program_id(0) == last >> 1)
+    def _():
+        total = last_keep_ref[...].astype(F32) + last_got_ref[...].astype(F32)
+        out_ref[pl.ds(last & 1, 1)] = total.astype(BF16)
+
+
+def join(where, keep, got, last_keep, last_got):
+    n, height, depth = keep.shape
+    pair = pl.BlockSpec((2, height, depth), lambda i, o: (i, 0, 0))
+    one = pl.BlockSpec((1, height, depth), lambda i, o: (0, 0, 0))
     return call(
         join_kernel,
-        grid=(2,),
-        in_specs=[block, block],
-        out_specs=block,
-        out_shape=jax.ShapeDtypeStruct(shape, BF16),
-    )(keep, got)
-
-
-def join_last(where, steps, keep, got, held):
-    shape = keep.shape
-    chunk = stepper(steps, held.shape[0])
-    flat = pl.BlockSpec(shape, lambda i, o: (0, 0, 0))
-    return call(
-        join_last_kernel,
         grid_spec=pltpu.PrefetchScalarGridSpec(
             num_scalar_prefetch=1,
-            grid=(1,),
-            in_specs=[flat, flat, pl.BlockSpec(memory_space=pl.ANY)],
-            out_specs=pl.BlockSpec(shape, lambda i, o: (chunk(i, o), 0, 0)),
-        ),
-        out_shape=jax.ShapeDtypeStruct(held.shape, BF16),
-        input_output_aliases={3: 0},
-    )(where, keep, got, held)
+            grid=(n // 2,),
+            in_specs=[pair, pair, one, one],
+            out_specs=pair,
+        ),
+        out_shape=pltpu.HBM(keep.shape, BF16),
+    )(where, keep, got, last_keep, last_got)
 
 
 def split_kernel(sums_ref, out_ref):
@@ -391,7 +381,7 @@
 
     where = jnp.stack([here, core]).astype(jnp.int32)
 
-    half = height // 16 * 8
+    half = height // 22 * 8
     far = parts(where, (4,), mine, other, w, (half, height - half))
     got = both(*far)
     near = parts(where, (3, -3), mine, other, w)
@@ -417,8 +407,7 @@
     early = lax.ppermute(held[1], "core", swap)
     keep, send, acts = back(where, (4,), got, w, held, ring, halves=True)
     late = lax.ppermute(send, "core", swap)
-    sums = join(held[0], early)
-    sums = join_last(where, (4,), keep, late, sums)
+    sums = join(where, held[0], early, keep, late)
     sums = lax.all_to_all(sums, ("x", "ylo"), 0, 0, tiled=True)
     own = call(
         split_kernel,

time: 261 us -> 259 us (level)
  no operation moved by 1% of the time
where the time goes in v4:
time: 259 us; the launch traced here: 255 us
  starting transfers between devices  93.3 us (36%)
  waiting for transfers between devices  85.5 us (33%)
  blocking collectives  38 us (15%)
  Pallas kernels  24.2 us (9%)
  matrix products  6.26 us (2%)
  other arithmetic  3.26 us (1%)
  local copies, waits for them, and re-layouts  3.03 us (1%)
    ppermute x8, starting transfers between devices, both(): lax.ppermute(to_left, 'tensor', left)  47.8 us
    ppermute x8, waiting for transfers between devices, both(): lax.ppermute(to_right, 'tensor', right)  34.5 us
    ppermute x3, waiting for transfers between devices, step(): lax.ppermute(pieces[r], 'expert', [(i, (i + r) % experts) for i in range(...  32.8 us
    all_to_all x1, blocking collectives, step(): lax.all_to_all(sent.reshape(lows * 2 * experts, slots, depth), NEAR, 0, 0...  19.5 us
    all_to_all x1, blocking collectives, step(): lax.all_to_all(jnp.broadcast_to(own[None], (n_chips // lows, lows * heigh...  18.5 us
    ppermute x8, starting transfers between devices, both(): lax.ppermute(to_right, 'tensor', right)  15.3 us
    ppermute x3, starting transfers between devices, step(): lax.ppermute(pieces[r], 'expert', [(i, (i + r) % experts) for i in range(...  12.5 us
    all_to_all x1, waiting for transfers between devices, step(): sums = lax.all_to_all(sums, ('x', 'ylo'), 0, 0, tiled=True)  9.19 us
  transfers between devices with their start and end apart: 24, of which 15 were waited for; matrix products, arithmetic and copies ran while one was open for 4% of the time, Pallas kernels for 5%

profile of v4, /device:TPU:6, one launch (start us, length us, event | category | flops | bytes accessed | tf_op | source)
XLA Modules:
  0.0 254.7 jit_solution(6803521882032597049)
XLA Ops:
  0.6 2.3 shard_map.110
  2.9 19.5 %all_to_all.20 = bf16[16,17,512]{2,1,0:T(8,128)(2,1)S(1)} all-to-all(bf16[16,17,512]{2,1,0:T(8,128)(2,1)} %bitcast.31), channel_id=1, replica_groups=mesh['ylo'=2,'x'=4,'core'=2,'expert'=4,'tensor'=8] {'ylo','core','expert'}, dimensions={0} | all-to-all | bytes 557056 | tf_op jit(solution)/shard_map/all_to_all | solution.py:359
  22.6 18.5 %all_to_all.21 = bf16[4,272,512]{2,1,0:T(8,128)(2,1)S(1)} all-to-all(bf16[4,272,512]{2,1,0:T(8,128)(2,1)S(1)} %broadcast_in_dim.17), channel_id=1, replica_groups=mesh['ylo'=2,'x'=4,'core'=2,'expert'=4,'tensor'=8] {'x'}, dimensions={0} | all-to-all | bytes 2228224 | tf_op jit(solution)/shard_map/all_to_all | solution.py:369
  41.2 3.0 %collective-permute-start = (bf16[8,136,512]{2,1,0:T(8,128)(2,1)S(1)}, bf16[8,136,512]{2,1,0:T(8,128)(2,1)S(1)}, u32[]{:S(2)}, u32[]{:S(2)}) collective-permute-start(bf16[8,136,512]{2,1,0:T(8,128)(2,1)S(1)} %bitcast.22), channel_id=1, source_target_pairs={{0,32},{32,0},{1,33},{33,1},{2,34},{34,2},{3,35},{35,3},{4,36},{36... | collective-permute-start | bytes 3342344 | tf_op jit(solution)/shard_map/ppermute | solution.py:373
  47.4 3.8 %collective-permute-start.1 = (bf16[512,384]{1,0:T(8,128)(2,1)}, bf16[512,384]{1,0:T(8,128)(2,1)S(1)}, u32[]{:S(2)}, u32[]{:S(2)}) collective-permute-start(bf16[512,384]{1,0:T(8,128)(2,1)} %get-tuple-element.36), channel_id=1, source_target_pairs={{0,8},{8,16},{16,24},{24,0},{1,9},{9,17},{17,25},{25,1},{2,10},{10... | collective-permute-start | bytes 1179656 | tf_op jit(solution)/shard_map/ppermute | solution.py:365
  51.2 5.2 %collective-permute-start.2 = (bf16[512,384]{1,0:T(8,128)(2,1)}, bf16[512,384]{1,0:T(8,128)(2,1)S(1)}, u32[]{:S(2)}, u32[]{:S(2)}) collective-permute-start(bf16[512,384]{1,0:T(8,128)(2,1)} %get-tuple-element.37), channel_id=1, source_target_pairs={{0,16},{8,24},{16,0},{24,8},{1,17},{9,25},{17,1},{25,9},{2,18},{10... | collective-permute-start | bytes 1179656 | tf_op jit(solution)/shard_map/ppermute | solution.py:365
  56.4 3.5 %collective-permute-start.3 = (bf16[512,384]{1,0:T(8,128)(2,1)}, bf16[512,384]{1,0:T(8,128)(2,1)S(1)}, u32[]{:S(2)}, u32[]{:S(2)}) collective-permute-start(bf16[512,384]{1,0:T(8,128)(2,1)} %get-tuple-element.38), channel_id=1, source_target_pairs={{0,24},{8,0},{16,8},{24,16},{1,25},{9,1},{17,9},{25,17},{2,26},{10... | collective-permute-start | bytes 1179656 | tf_op jit(solution)/shard_map/ppermute | solution.py:365
  60.0 10.5 %collective-permute-done.1.refs_1_ = bf16[512,384]{1,0:T(8,128)(2,1)S(1)} collective-permute-done((bf16[512,384]{1,0:T(8,128)(2,1)}, bf16[512,384]{1,0:T(8,128)(2,1)S(1)}, u32[]{:S(2)}, u32[]{:S(2)}) %collective-permute-start.1) | collective-permute-done | bytes 393248 | tf_op jit(solution)/shard_map/ppermute | solution.py:365
  70.5 17.1 %collective-permute-done.2.refs_2_ = bf16[512,384]{1,0:T(8,128)(2,1)S(1)} collective-permute-done((bf16[512,384]{1,0:T(8,128)(2,1)}, bf16[512,384]{1,0:T(8,128)(2,1)S(1)}, u32[]{:S(2)}, u32[]{:S(2)}) %collective-permute-start.2) | collective-permute-done | bytes 393248 | tf_op jit(solution)/shard_map/ppermute | solution.py:365
  87.6 5.2 %collective-permute-done.3.refs_3_ = bf16[512,384]{1,0:T(8,128)(2,1)S(1)} collective-permute-done((bf16[512,384]{1,0:T(8,128)(2,1)}, bf16[512,384]{1,0:T(8,128)(2,1)S(1)}, u32[]{:S(2)}, u32[]{:S(2)}) %collective-permute-start.3) | collective-permute-done | bytes 393248 | tf_op jit(solution)/shard_map/ppermute | solution.py:365
  95.5 10.7 %collective-permute-start.8 = (bf16[88,1536]{1,0:T(8,128)(2,1)S(1)}, bf16[88,1536]{1,0:T(8,128)(2,1)S(1)}, u32[]{:S(2)}, u32[]{:S(2)}) collective-permute-start(bf16[88,1536]{1,0:T(8,128)(2,1)S(1)} %get-tuple-element.45), channel_id=1, source_target_pairs={{0,7},{1,0},{2,1},{3,2},{4,3},{5,4},{6,5},{7,6},{8,15},{9,8},{10,9... | collective-permute-start | bytes 811016 | tf_op jit(solution)/shard_map/ppermute | solution.py:380
  106.2 1.9 collective-permute-start.4
  109.5 5.2 %collective-permute-done.4.got_ref = bf16[48,1536]{1,0:T(8,128)(2,1)S(1)} collective-permute-done((bf16[48,1536]{1,0:T(8,128)(2,1)S(1)}, bf16[48,1536]{1,0:T(8,128)(2,1)S(1)}, u32[]{:S(2)}, u32[]{:S(2)}) %collective-permute-start.4) | collective-permute-done | bytes 147488 | tf_op jit(solution)/shard_map/ppermute | solution.py:380
  114.8 1.9 collective-permute-start.5
  116.8 5.1 %collective-permute-start.9 = (bf16[136,1536]{1,0:T(8,128)(2,1)S(1)}, bf16[136,1536]{1,0:T(8,128)(2,1)S(1)}, u32[]{:S(2)}, u32[]{:S(2)}) collective-permute-start(bf16[136,1536]{1,0:T(8,128)(2,1)S(1)} %shard_map.117), channel_id=1, source_target_pairs={{0,7},{1,0},{2,1},{3,2},{4,3},{5,4},{6,5},{7,6},{8,15},{9,8},{10,9... | collective-permute-start | bytes 1253384 | tf_op jit(solution)/shard_map/ppermute | solution.py:380
  122.0 2.8 %shard_map.113 = (bf16[136,1536]{1,0:T(8,128)(2,1)S(1)}, bf16[136,1536]{1,0:T(8,128)(2,1)S(1)}, bf16[136,1536]{1,0:T(8,128)(2,1)S(1)}, bf16[136,1536]{1,0:T(8,128)(2,1)S(1)}, bf16[136,1536]{1,0:T(8,128)(2,1)S(1)}) custom-call(s32[2]{0:T(128)S(1)} %pad_add_fusion.order_ref.where_ref, bf16[8,136,512]{2,1,0:T(8,128)(2,1)S(1)} %bitcast.25, ...), custom_call_target="tpu_custom_call" | custom-call | flops 1069547520 | bytes 5054464 | tf_op jit(solution)/shard_map/pallas_call | solution.py:167
  124.8 3.6 %collective-permute-done.5 = bf16[136,1536]{1,0:T(8,128)(2,1)S(1)} collective-permute-done((bf16[136,1536]{1,0:T(8,128)(2,1)S(1)}, bf16[136,1536]{1,0:T(8,128)(2,1)S(1)}, u32[]{:S(2)}, u32[]{:S(2)}) %collective-permute-start.5) | collective-permute-done | bytes 417824 | tf_op jit(solution)/shard_map/ppermute | solution.py:380
  128.5 1.9 collective-permute-start.6
  130.5 5.1 %collective-permute-start.10 = (bf16[136,1536]{1,0:T(8,128)(2,1)S(1)}, bf16[136,1536]{1,0:T(8,128)(2,1)S(1)}, u32[]{:S(2)}, u32[]{:S(2)}) collective-permute-start(bf16[136,1536]{1,0:T(8,128)(2,1)S(1)} %add.14), channel_id=1, source_target_pairs={{0,7},{1,0},{2,1},{3,2},{4,3},{5,4},{6,5},{7,6},{8,15},{9,8},{10,9... | collective-permute-start | bytes 1253384 | tf_op jit(solution)/shard_map/ppermute | solution.py:380
  135.7 5.5 %collective-permute-done.6 = bf16[136,1536]{1,0:T(8,128)(2,1)S(1)} collective-permute-done((bf16[136,1536]{1,0:T(8,128)(2,1)S(1)}, bf16[136,1536]{1,0:T(8,128)(2,1)S(1)}, u32[]{:S(2)}, u32[]{:S(2)}) %collective-permute-start.6) | collective-permute-done | bytes 417824 | tf_op jit(solution)/shard_map/ppermute | solution.py:380
  141.2 1.9 collective-permute-start.7
  143.3 5.1 %collective-permute-start.11 = (bf16[136,1536]{1,0:T(8,128)(2,1)S(1)}, bf16[136,1536]{1,0:T(8,128)(2,1)S(1)}, u32[]{:S(2)}, u32[]{:S(2)}) collective-permute-start(bf16[136,1536]{1,0:T(8,128)(2,1)S(1)} %add.15), channel_id=1, source_target_pairs={{0,7},{1,0},{2,1},{3,2},{4,3},{5,4},{6,5},{7,6},{8,15},{9,8},{10,9... | collective-permute-start | bytes 1253384 | tf_op jit(solution)/shard_map/ppermute | solution.py:380
  148.4 4.6 %collective-permute-done.7.b_ref = bf16[136,1536]{1,0:T(8,128)(2,1)S(1)} collective-permute-done((bf16[136,1536]{1,0:T(8,128)(2,1)S(1)}, bf16[136,1536]{1,0:T(8,128)(2,1)S(1)}, u32[]{:S(2)}, u32[]{:S(2)}) %collective-permute-start.7) | collective-permute-done | bytes 417824 | tf_op jit(solution)/shard_map/ppermute | solution.py:380
  154.6 1.9 collective-permute-start.12
  156.6 5.6 %collective-permute-start.15 = (bf16[136,1536]{1,0:T(8,128)(2,1)S(1)}, bf16[136,1536]{1,0:T(8,128)(2,1)S(1)}, u32[]{:S(2)}, u32[]{:S(2)}) collective-permute-start(bf16[136,1536]{1,0:T(8,128)(2,1)S(1)} %shard_map.118.refs_0_), channel_id=1, source_target_pairs={{0,7},{1,0},{2,1},{3,2},{4,3},{5,4},{6,5},{7,6},{8,15},{9,8},{10,9... | collective-permute-start | bytes 1253384 | tf_op jit(solution)/shard_map/ppermute | solution.py:380
  162.2 4.1 %collective-permute-done.12.refs_0_ = bf16[136,1536]{1,0:T(8,128)(2,1)S(1)} collective-permute-done((bf16[136,1536]{1,0:T(8,128)(2,1)S(1)}, bf16[136,1536]{1,0:T(8,128)(2,1)S(1)}, u32[]{:S(2)}, u32[]{:S(2)}) %collective-permute-start.12) | collective-permute-done | bytes 417824 | tf_op jit(solution)/shard_map/ppermute | solution.py:380
  166.2 1.9 collective-permute-start.13
  168.2 5.1 %collective-permute-start.16 = (bf16[136,1536]{1,0:T(8,128)(2,1)S(1)}, bf16[136,1536]{1,0:T(8,128)(2,1)S(1)}, u32[]{:S(2)}, u32[]{:S(2)}) collective-permute-start(bf16[136,1536]{1,0:T(8,128)(2,1)S(1)} %collective-permute-done.15.refs_1_), channel_id=1, source_target_pairs={{0,7},{1,0},{2,1},{3,2},{4,3},{5,4},{6,5},{7,6},{8,15},{9,8},{10,9... | collective-permute-start | bytes 1253384 | tf_op jit(solution)/shard_map/ppermute | solution.py:380
  173.3 4.4 %collective-permute-done.13.refs_0_ = bf16[136,1536]{1,0:T(8,128)(2,1)S(1)} collective-permute-done((bf16[136,1536]{1,0:T(8,128)(2,1)S(1)}, bf16[136,1536]{1,0:T(8,128)(2,1)S(1)}, u32[]{:S(2)}, u32[]{:S(2)}) %collective-permute-start.13) | collective-permute-done | bytes 417824 | tf_op jit(solution)/shard_map/ppermute | solution.py:380
  177.7 1.9 collective-permute-start.14
  179.6 5.4 %collective-permute-start.17 = (bf16[136,1536]{1,0:T(8,128)(2,1)S(1)}, bf16[136,1536]{1,0:T(8,128)(2,1)S(1)}, u32[]{:S(2)}, u32[]{:S(2)}) collective-permute-start(bf16[136,1536]{1,0:T(8,128)(2,1)S(1)} %collective-permute-done.16.refs_1_), channel_id=1, source_target_pairs={{0,7},{1,0},{2,1},{3,2},{4,3},{5,4},{6,5},{7,6},{8,15},{9,8},{10,9... | collective-permute-start | bytes 1253384 | tf_op jit(solution)/shard_map/ppermute | solution.py:380
  186.2 1.9 shard_map.120
  188.1 1.9 shard_map.121
  190.6 1.9 shard_map.122
  192.5 1.9 collective-permute-start.18
  194.4 5.6 %collective-permute-start.20 = (bf16[88,1536]{1,0:T(8,128)(2,1)S(1)}, bf16[88,1536]{1,0:T(8,128)(2,1)S(1)}, u32[]{:S(2)}, u32[]{:S(2)}) collective-permute-start(bf16[88,1536]{1,0:T(8,128)(2,1)S(1)} %slice.21), channel_id=1, source_target_pairs={{0,7},{1,0},{2,1},{3,2},{4,3},{5,4},{6,5},{7,6},{8,15},{9,8},{10,9... | collective-permute-start | bytes 811016 | tf_op jit(solution)/shard_map/ppermute | solution.py:380
  200.1 1.9 collective-permute-start.19
  202.0 7.1 %collective-permute-done.19.refs_0_ = bf16[48,1536]{1,0:T(8,128)(2,1)S(1)} collective-permute-done((bf16[48,1536]{1,0:T(8,128)(2,1)S(1)}, bf16[48,1536]{1,0:T(8,128)(2,1)S(1)}, u32[]{:S(2)}, u32[]{:S(2)}) %collective-permute-start.19) | collective-permute-done | bytes 147488 | tf_op jit(solution)/shard_map/ppermute | solution.py:380
  210.7 1.9 collective-permute-start.21
  214.0 2.2 shard_map.124
  216.3 6.2 %all-to-all-start.2 = ((bf16[8,136,512]{2,1,0:T(8,128)(2,1)}), bf16[8,136,512]{2,1,0:T(8,128)(2,1)}, u32[]{:S(2)}, u32[]{:S(2)}) async-start(bf16[8,136,512]{2,1,0:T(8,128)(2,1)} %shard_map.124), calls=%async_computation.2 | async-start | bytes 2228224 | tf_op jit(solution)/shard_map/all_to_all | solution.py:411
  222.5 2.7 %broadcast_select_fusion = (bf16[8,136,512]{2,1,0:T(8,128)(2,1)}, bf16[8,136,512]{2,1,0:T(8,128)(2,1)S(1)}) fusion(bf16[8,136,512]{2,1,0:T(8,128)(2,1)} %copy-done.1, bf16[8,136,512]{2,1,0:T(8,128)(2,1)} %bitcast.26, pred[]{:T(512)S(6)} %eq.4), kind=kLoop, calls=%fused_computation.9 | loop fusion | flops 1114112 | bytes 4456449 | tf_op jit(solution)/shard_map/jit(_where)/select_n | solution.py:424
  225.2 1.7 fusion.1
  228.5 9.2 %all-to-all-done.2.sums_ref = bf16[8,136,512]{2,1,0:T(8,128)(2,1)} async-done(((bf16[8,136,512]{2,1,0:T(8,128)(2,1)}), bf16[8,136,512]{2,1,0:T(8,128)(2,1)}, u32[]{:S(2)}, u32[]{:S(2)}) %all-to-all-start.2) | async-done | bytes 1114144 | tf_op jit(solution)/shard_map/all_to_all | solution.py:411
  237.7 2.1 shard_map.125
  239.8 4.5 %all-to-all-start.3 = ((bf16[8,17,512]{2,1,0:T(8,128)(2,1)}), bf16[8,17,512]{2,1,0:T(8,128)(2,1)S(1)}, u32[]{:S(2)}, u32[]{:S(2)}) async-start(bf16[8,17,512]{2,1,0:T(8,128)(2,1)} %shard_map.125), calls=%async_computation.3 | async-start | bytes 393216 | tf_op jit(solution)/shard_map/all_to_all | solution.py:416
  244.3 2.9 %fusion.2 = bf16[1,512,512]{2,1,0:T(8,128)(2,1)} fusion(bf16[1088,512]{1,0:T(8,128)(2,1)} %bitcast.32, bf16[1088,1536]{1,0:T(8,128)(2,1)S(1)} %bitcast.21), kind=kOutput, calls=%fused_computation.5 | convolution fusion | flops 570687488 | bytes 2752512 | tf_op jit(solution)/shard_map/dot_general | solution.py:337
  247.3 5.9 %all-to-all-done.3.back_ref = bf16[8,17,512]{2,1,0:T(8,128)(2,1)S(1)} async-done(((bf16[8,17,512]{2,1,0:T(8,128)(2,1)}), bf16[8,17,512]{2,1,0:T(8,128)(2,1)S(1)}, u32[]{:S(2)}, u32[]{:S(2)}) %all-to-all-start.3) | async-done | bytes 139296 | tf_op jit(solution)/shard_map/all_to_all | solution.py:416
  (50 shorter events, 17.4 us)
Async XLA Ops:
  22.6 21.6 %copy-start.2 = (bf16[4,512,128]{2,1,0:T(8,128)(2,1)S(1)}, bf16[4,512,128]{2,1,0:T(8,128)(2,1)}, u32[]{:S(2)}) copy-start(bf16[4,512,128]{2,1,0:T(8,128)(2,1)} %refs_0_.1) | copy-start | bytes 1572868
  22.6 21.6 %copy-start.3 = (bf16[4,512,128]{2,1,0:T(8,128)(2,1)S(1)}, bf16[4,512,128]{2,1,0:T(8,128)(2,1)}, u32[]{:S(2)}) copy-start(bf16[4,512,128]{2,1,0:T(8,128)(2,1)} %refs_1_.1) | copy-start | bytes 1572868
  41.2 80.8 %copy-start = (bf16[4,272,512]{2,1,0:T(8,128)(2,1)}, bf16[4,272,512]{2,1,0:T(8,128)(2,1)S(1)}, u32[]{:S(2)}) copy-start(bf16[4,272,512]{2,1,0:T(8,128)(2,1)S(1)} %all_to_all.21) | copy-start | bytes 3342340
  41.2 53.3 %collective-permute-start = (bf16[8,136,512]{2,1,0:T(8,128)(2,1)S(1)}, bf16[8,136,512]{2,1,0:T(8,128)(2,1)S(1)}, u32[]{:S(2)}, u32[]{:S(2)}) collective-permute-start(bf16[8,136,512]{2,1,0:T(8,128)(2,1)S(1)} %bitcast.22), channel_id=1, source_target_pairs={{0,32},{32,0},{1,33},{33,1},{2,34},{34,2},{3,35},{35,3},{4,36},{36... | collective-permute-start | bytes 3342344 | tf_op jit(solution)/shard_map/ppermute | solution.py:373
  44.2 1.0 copy-start.4
  46.7 0.7 copy-start.5
  47.4 23.1 %collective-permute-start.1 = (bf16[512,384]{1,0:T(8,128)(2,1)}, bf16[512,384]{1,0:T(8,128)(2,1)S(1)}, u32[]{:S(2)}, u32[]{:S(2)}) collective-permute-start(bf16[512,384]{1,0:T(8,128)(2,1)} %get-tuple-element.36), channel_id=1, source_target_pairs={{0,8},{8,16},{16,24},{24,0},{1,9},{9,17},{17,25},{25,1},{2,10},{10... | collective-permute-start | bytes 1179656 | tf_op jit(solution)/shard_map/ppermute | solution.py:365
  51.2 36.4 %collective-permute-start.2 = (bf16[512,384]{1,0:T(8,128)(2,1)}, bf16[512,384]{1,0:T(8,128)(2,1)S(1)}, u32[]{:S(2)}, u32[]{:S(2)}) collective-permute-start(bf16[512,384]{1,0:T(8,128)(2,1)} %get-tuple-element.37), channel_id=1, source_target_pairs={{0,16},{8,24},{16,0},{24,8},{1,17},{9,25},{17,1},{25,9},{2,18},{10... | collective-permute-start | bytes 1179656 | tf_op jit(solution)/shard_map/ppermute | solution.py:365
  56.4 36.4 %collective-permute-start.3 = (bf16[512,384]{1,0:T(8,128)(2,1)}, bf16[512,384]{1,0:T(8,128)(2,1)S(1)}, u32[]{:S(2)}, u32[]{:S(2)}) collective-permute-start(bf16[512,384]{1,0:T(8,128)(2,1)} %get-tuple-element.38), channel_id=1, source_target_pairs={{0,24},{8,0},{16,8},{24,16},{1,25},{9,1},{17,9},{25,17},{2,26},{10... | collective-permute-start | bytes 1179656 | tf_op jit(solution)/shard_map/ppermute | solution.py:365
  92.8 1.0 copy-start.6
  94.5 27.4 %copy-start.1 = (bf16[8,136,512]{2,1,0:T(8,128)(2,1)}, bf16[8,136,512]{2,1,0:T(8,128)(2,1)S(1)}, u32[]{:S(2)}) copy-start(bf16[8,136,512]{2,1,0:T(8,128)(2,1)S(1)} %collective-permute-done.other_x_ref) | copy-start | bytes 3342340
  95.5 21.3 %collective-permute-start.8 = (bf16[88,1536]{1,0:T(8,128)(2,1)S(1)}, bf16[88,1536]{1,0:T(8,128)(2,1)S(1)}, u32[]{:S(2)}, u32[]{:S(2)}) collective-permute-start(bf16[88,1536]{1,0:T(8,128)(2,1)S(1)} %get-tuple-element.45), channel_id=1, source_target_pairs={{0,7},{1,0},{2,1},{3,2},{4,3},{5,4},{6,5},{7,6},{8,15},{9,8},{10,9... | collective-permute-start | bytes 811016 | tf_op jit(solution)/shard_map/ppermute | solution.py:380
  106.2 8.6 %collective-permute-start.4 = (bf16[48,1536]{1,0:T(8,128)(2,1)S(1)}, bf16[48,1536]{1,0:T(8,128)(2,1)S(1)}, u32[]{:S(2)}, u32[]{:S(2)}) collective-permute-start(bf16[48,1536]{1,0:T(8,128)(2,1)S(1)} %get-tuple-element.41), channel_id=1, source_target_pairs={{0,1},{1,2},{2,3},{3,4},{4,5},{5,6},{6,7},{7,0},{8,9},{9,10},{10,1... | collective-permute-start | bytes 442376 | tf_op jit(solution)/shard_map/ppermute | solution.py:380
  114.8 13.5 %collective-permute-start.5 = (bf16[136,1536]{1,0:T(8,128)(2,1)S(1)}, bf16[136,1536]{1,0:T(8,128)(2,1)S(1)}, u32[]{:S(2)}, u32[]{:S(2)}) collective-permute-start(bf16[136,1536]{1,0:T(8,128)(2,1)S(1)} %shard_map.116), channel_id=1, source_target_pairs={{0,1},{1,2},{2,3},{3,4},{4,5},{5,6},{6,7},{7,0},{8,9},{9,10},{10,1... | collective-permute-start | bytes 1253384 | tf_op jit(solution)/shard_map/ppermute | solution.py:380
  116.8 13.6 %collective-permute-start.9 = (bf16[136,1536]{1,0:T(8,128)(2,1)S(1)}, bf16[136,1536]{1,0:T(8,128)(2,1)S(1)}, u32[]{:S(2)}, u32[]{:S(2)}) collective-permute-start(bf16[136,1536]{1,0:T(8,128)(2,1)S(1)} %shard_map.117), channel_id=1, source_target_pairs={{0,7},{1,0},{2,1},{3,2},{4,3},{5,4},{6,5},{7,6},{8,15},{9,8},{10,9... | collective-permute-start | bytes 1253384 | tf_op jit(solution)/shard_map/ppermute | solution.py:380
  128.5 12.7 %collective-permute-start.6 = (bf16[136,1536]{1,0:T(8,128)(2,1)S(1)}, bf16[136,1536]{1,0:T(8,128)(2,1)S(1)}, u32[]{:S(2)}, u32[]{:S(2)}) collective-permute-start(bf16[136,1536]{1,0:T(8,128)(2,1)S(1)} %add.12), channel_id=1, source_target_pairs={{0,1},{1,2},{2,3},{3,4},{4,5},{5,6},{6,7},{7,0},{8,9},{9,10},{10,1... | collective-permute-start | bytes 1253384 | tf_op jit(solution)/shard_map/ppermute | solution.py:380
  130.5 12.6 %collective-permute-start.10 = (bf16[136,1536]{1,0:T(8,128)(2,1)S(1)}, bf16[136,1536]{1,0:T(8,128)(2,1)S(1)}, u32[]{:S(2)}, u32[]{:S(2)}) collective-permute-start(bf16[136,1536]{1,0:T(8,128)(2,1)S(1)} %add.14), channel_id=1, source_target_pairs={{0,7},{1,0},{2,1},{3,2},{4,3},{5,4},{6,5},{7,6},{8,15},{9,8},{10,9... | collective-permute-start | bytes 1253384 | tf_op jit(solution)/shard_map/ppermute | solution.py:380
  141.2 11.8 %collective-permute-start.7 = (bf16[136,1536]{1,0:T(8,128)(2,1)S(1)}, bf16[136,1536]{1,0:T(8,128)(2,1)S(1)}, u32[]{:S(2)}, u32[]{:S(2)}) collective-permute-start(bf16[136,1536]{1,0:T(8,128)(2,1)S(1)} %add.13), channel_id=1, source_target_pairs={{0,1},{1,2},{2,3},{3,4},{4,5},{5,6},{6,7},{7,0},{8,9},{9,10},{10,1... | collective-permute-start | bytes 1253384 | tf_op jit(solution)/shard_map/ppermute | solution.py:380
  143.3 11.1 %collective-permute-start.11 = (bf16[136,1536]{1,0:T(8,128)(2,1)S(1)}, bf16[136,1536]{1,0:T(8,128)(2,1)S(1)}, u32[]{:S(2)}, u32[]{:S(2)}) collective-permute-start(bf16[136,1536]{1,0:T(8,128)(2,1)S(1)} %add.15), channel_id=1, source_target_pairs={{0,7},{1,0},{2,1},{3,2},{4,3},{5,4},{6,5},{7,6},{8,15},{9,8},{10,9... | collective-permute-start | bytes 1253384 | tf_op jit(solution)/shard_map/ppermute | solution.py:380
  154.6 11.6 %collective-permute-start.12 = (bf16[136,1536]{1,0:T(8,128)(2,1)S(1)}, bf16[136,1536]{1,0:T(8,128)(2,1)S(1)}, u32[]{:S(2)}, u32[]{:S(2)}) collective-permute-start(bf16[136,1536]{1,0:T(8,128)(2,1)S(1)} %shard_map.118.refs_0_), channel_id=1, source_target_pairs={{0,1},{1,2},{2,3},{3,4},{4,5},{5,6},{6,7},{7,0},{8,9},{9,10},{10,1... | collective-permute-start | bytes 1253384 | tf_op jit(solution)/shard_map/ppermute | solution.py:380
  156.6 11.6 %collective-permute-start.15 = (bf16[136,1536]{1,0:T(8,128)(2,1)S(1)}, bf16[136,1536]{1,0:T(8,128)(2,1)S(1)}, u32[]{:S(2)}, u32[]{:S(2)}) collective-permute-start(bf16[136,1536]{1,0:T(8,128)(2,1)S(1)} %shard_map.118.refs_0_), channel_id=1, source_target_pairs={{0,7},{1,0},{2,1},{3,2},{4,3},{5,4},{6,5},{7,6},{8,15},{9,8},{10,9... | collective-permute-start | bytes 1253384 | tf_op jit(solution)/shard_map/ppermute | solution.py:380
  166.2 11.4 %collective-permute-start.13 = (bf16[136,1536]{1,0:T(8,128)(2,1)S(1)}, bf16[136,1536]{1,0:T(8,128)(2,1)S(1)}, u32[]{:S(2)}, u32[]{:S(2)}) collective-permute-start(bf16[136,1536]{1,0:T(8,128)(2,1)S(1)} %collective-permute-done.12.refs_0_), channel_id=1, source_target_pairs={{0,1},{1,2},{2,3},{3,4},{4,5},{5,6},{6,7},{7,0},{8,9},{9,10},{10,1... | collective-permute-start | bytes 1253384 | tf_op jit(solution)/shard_map/ppermute | solution.py:380
  168.2 11.4 %collective-permute-start.16 = (bf16[136,1536]{1,0:T(8,128)(2,1)S(1)}, bf16[136,1536]{1,0:T(8,128)(2,1)S(1)}, u32[]{:S(2)}, u32[]{:S(2)}) collective-permute-start(bf16[136,1536]{1,0:T(8,128)(2,1)S(1)} %collective-permute-done.15.refs_1_), channel_id=1, source_target_pairs={{0,7},{1,0},{2,1},{3,2},{4,3},{5,4},{6,5},{7,6},{8,15},{9,8},{10,9... | collective-permute-start | bytes 1253384 | tf_op jit(solution)/shard_map/ppermute | solution.py:380
  177.7 12.4 %collective-permute-start.14 = (bf16[136,1536]{1,0:T(8,128)(2,1)S(1)}, bf16[136,1536]{1,0:T(8,128)(2,1)S(1)}, u32[]{:S(2)}, u32[]{:S(2)}) collective-permute-start(bf16[136,1536]{1,0:T(8,128)(2,1)S(1)} %collective-permute-done.13.refs_0_), channel_id=1, source_target_pairs={{0,1},{1,2},{2,3},{3,4},{4,5},{5,6},{6,7},{7,0},{8,9},{9,10},{10,1... | collective-permute-start | bytes 1253384 | tf_op jit(solution)/shard_map/ppermute | solution.py:380
  179.6 11.0 %collective-permute-start.17 = (bf16[136,1536]{1,0:T(8,128)(2,1)S(1)}, bf16[136,1536]{1,0:T(8,128)(2,1)S(1)}, u32[]{:S(2)}, u32[]{:S(2)}) collective-permute-start(bf16[136,1536]{1,0:T(8,128)(2,1)S(1)} %collective-permute-done.16.refs_1_), channel_id=1, source_target_pairs={{0,7},{1,0},{2,1},{3,2},{4,3},{5,4},{6,5},{7,6},{8,15},{9,8},{10,9... | collective-permute-start | bytes 1253384 | tf_op jit(solution)/shard_map/ppermute | solution.py:380
  192.5 21.5 %collective-permute-start.18 = (bf16[8,136,512]{2,1,0:T(8,128)(2,1)S(1)}, bf16[8,136,512]{2,1,0:T(8,128)(2,1)S(1)}, u32[]{:S(2)}, u32[]{:S(2)}) collective-permute-start(bf16[8,136,512]{2,1,0:T(8,128)(2,1)S(1)} %get-tuple-element.58), channel_id=1, source_target_pairs={{0,32},{32,0},{1,33},{33,1},{2,34},{34,2},{3,35},{35,3},{4,36},{36... | collective-permute-start | bytes 3342344 | tf_op jit(solution)/shard_map/ppermute | solution.py:407
  194.4 14.7 %collective-permute-start.20 = (bf16[88,1536]{1,0:T(8,128)(2,1)S(1)}, bf16[88,1536]{1,0:T(8,128)(2,1)S(1)}, u32[]{:S(2)}, u32[]{:S(2)}) collective-permute-start(bf16[88,1536]{1,0:T(8,128)(2,1)S(1)} %slice.21), channel_id=1, source_target_pairs={{0,7},{1,0},{2,1},{3,2},{4,3},{5,4},{6,5},{7,6},{8,15},{9,8},{10,9... | collective-permute-start | bytes 811016 | tf_op jit(solution)/shard_map/ppermute | solution.py:380
  200.1 9.1 %collective-permute-start.19 = (bf16[48,1536]{1,0:T(8,128)(2,1)S(1)}, bf16[48,1536]{1,0:T(8,128)(2,1)S(1)}, u32[]{:S(2)}, u32[]{:S(2)}) collective-permute-start(bf16[48,1536]{1,0:T(8,128)(2,1)S(1)} %slice.20), channel_id=1, source_target_pairs={{0,1},{1,2},{2,3},{3,4},{4,5},{5,6},{6,7},{7,0},{8,9},{9,10},{10,1... | collective-permute-start | bytes 442376 | tf_op jit(solution)/shard_map/ppermute | solution.py:380
  210.7 3.3 %collective-permute-start.21 = (bf16[1,136,512]{2,1,0:T(8,128)(2,1)S(1)}, bf16[1,136,512]{2,1,0:T(8,128)(2,1)S(1)}, u32[]{:S(2)}, u32[]{:S(2)}) collective-permute-start(bf16[1,136,512]{2,1,0:T(8,128)(2,1)S(1)} %get-tuple-element.61), channel_id=1, source_target_pairs={{0,32},{32,0},{1,33},{33,1},{2,34},{34,2},{3,35},{35,3},{4,36},{36... | collective-permute-start | bytes 417800 | tf_op jit(solution)/shard_map/ppermute | solution.py:409
  216.3 21.5 %all-to-all-start.2 = ((bf16[8,136,512]{2,1,0:T(8,128)(2,1)}), bf16[8,136,512]{2,1,0:T(8,128)(2,1)}, u32[]{:S(2)}, u32[]{:S(2)}) async-start(bf16[8,136,512]{2,1,0:T(8,128)(2,1)} %shard_map.124), calls=%async_computation.2 | async-start | bytes 2228224 | tf_op jit(solution)/shard_map/all_to_all | solution.py:411
  239.8 13.3 %all-to-all-start.3 = ((bf16[8,17,512]{2,1,0:T(8,128)(2,1)}), bf16[8,17,512]{2,1,0:T(8,128)(2,1)S(1)}, u32[]{:S(2)}, u32[]{:S(2)}) async-start(bf16[8,17,512]{2,1,0:T(8,128)(2,1)} %shard_map.125), calls=%async_computation.3 | async-start | bytes 393216 | tf_op jit(solution)/shard_map/all_to_all | solution.py:416
  244.3 8.9 %copy-start.7 = (s32[28,2]{0,1:T(2,128)S(1)}, s32[28,2]{0,1:T(2,128)}, u32[]{:S(2)}) copy-start(s32[28,2]{0,1:T(2,128)} %param.8) | copy-start | bytes 676
  244.3 8.9 %copy-start.8 = (f32[28,2]{0,1:T(2,128)S(1)}, f32[28,2]{0,1:T(2,128)}, u32[]{:S(2)}) copy-start(f32[28,2]{0,1:T(2,128)} %param.9) | copy-start | bytes 676

commit v5 on v4

--- a/solution.py
+++ b/solution.py
@@ -101,32 +101,36 @@
 
 
 def place_kernel(expert_ref, *refs):
-    pieces, out = refs[:-1], refs[-1]
+    pieces, out = refs[:2], refs[-1]
     width = out.shape[2]
-    for r, piece in enumerate(pieces):
-
-        @pl.when(pl.program_id(0) == r)
+    for i, piece in enumerate(pieces):
+
+        @pl.when(pl.program_id(0) == i)
         def _():
             for a in range(3):
                 out[a] = piece[:, a * width : (a + 1) * width]
 
 
-def place(expert, pieces):
-    n, (depth, width3) = len(pieces), pieces[0].shape
+def place(expert, first, pieces, n, held):
+    depth, width3 = pieces[0].shape
     width = width3 // 3
+    whole = pl.BlockSpec((depth, width3), lambda i, e: (0, 0))
     return call(
         place_kernel,
         grid_spec=pltpu.PrefetchScalarGridSpec(
             num_scalar_prefetch=1,
-            grid=(n,),
-            in_specs=[pl.BlockSpec((depth, width3), lambda i, e: (0, 0))] * n,
-            out_specs=pl.BlockSpec((3, depth, width), lambda i, e: (0, 0, (e[0] - i) & (n - 1))),
+            grid=(2,),
+            in_specs=[whole, whole] + [pl.BlockSpec(memory_space=pl.ANY)] * len(held),
+            out_specs=pl.BlockSpec(
+                (3, depth, width), lambda i, e: (0, 0, (e[0] - first - 2 * i) & (n - 1))
+            ),
         ),
         out_shape=jax.ShapeDtypeStruct((3, depth, n * width), BF16),
+        input_output_aliases={3: 0} if held else {},
         cost_estimate=pl.CostEstimate(
-            flops=0, bytes_accessed=12 * n * depth * width, transcendentals=0
-        ),
-    )(expert.astype(jnp.int32).reshape(1), *pieces)
+            flops=0, bytes_accessed=24 * depth * width, transcendentals=0
+        ),
+    )(expert.astype(jnp.int32).reshape(1), *pieces, *held)
 
 
 def part_kernel(n, order_ref, mine_x_ref, other_x_ref, w_ref, *out_refs):
@@ -365,7 +369,8 @@
         lax.ppermute(pieces[r], "expert", [(i, (i + r) % experts) for i in range(experts)])
         for r in range(1, experts)
     ]
-    w = place(expert, pieces)
+    w = place(expert, 0, pieces[0::2], experts, ())
+    w = place(expert, 1, pieces[1::2], experts, (w,))
     mine = lax.all_to_all(
         jnp.broadcast_to(own[None], (n_chips // lows, lows * height, depth)), "x", 0, 0, tiled=True
     ).reshape(n_chips, height, depth)
@@ -409,8 +414,12 @@
     late = lax.ppermute(send, "core", swap)
     sums = join(where, held[0], early, keep, late)
     sums = lax.all_to_all(sums, ("x", "ylo"), 0, 0, tiled=True)
+    lanes = 128
     own = call(
         split_kernel,
+        grid=(depth // lanes,),
+        in_specs=[pl.BlockSpec((n_chips, height, lanes), lambda i: (0, 0, i))],
+        out_specs=pl.BlockSpec((2 * experts, slots, lanes), lambda i: (0, 0, i)),
         out_shape=jax.ShapeDtypeStruct((2 * experts, slots, depth), BF16),
     )(sums)
     returned = lax.all_to_all(own, ("core", "expert"), 0, 0, tiled=True)

time: 259 us -> 256 us (0.988)
  waiting for transfers between devices: 85.5 us -> 80.7 us
    ppermute x3, waiting for transfers between devices: 32.8 us -> 27.9 us  [step(): lax.ppermute(pieces[r], 'expert', [(i, (i + r) % experts) for i in range(...]
where the time goes in v5:
time: 256 us; the launch traced here: 251 us
  starting transfers between devices  93.5 us (37%)
  waiting for transfers between devices  80.7 us (32%)
  blocking collectives  38 us (15%)
  Pallas kernels  25.4 us (10%)
  matrix products  6.25 us (2%)
  other arithmetic  3.26 us (1%)
  local copies, waits for them, and re-layouts  3.03 us (1%)
    ppermute x8, starting transfers between devices, both(): lax.ppermute(to_left, 'tensor', left)  47.9 us
    ppermute x8, waiting for transfers between devices, both(): lax.ppermute(to_right, 'tensor', right)  34.5 us
    ppermute x3, waiting for transfers between devices, step(): lax.ppermute(pieces[r], 'expert', [(i, (i + r) % experts) for i in range(...  27.9 us
    all_to_all x1, blocking collectives, step(): lax.all_to_all(sent.reshape(lows * 2 * experts, slots, depth), NEAR, 0, 0...  19.5 us
    all_to_all x1, blocking collectives, step(): lax.all_to_all(jnp.broadcast_to(own[None], (n_chips // lows, lows * heigh...  18.5 us
    ppermute x8, starting transfers between devices, both(): lax.ppermute(to_right, 'tensor', right)  15.3 us
    ppermute x3, starting transfers between devices, step(): lax.ppermute(pieces[r], 'expert', [(i, (i + r) % experts) for i in range(...  12.5 us
    all_to_all x1, waiting for transfers between devices, step(): sums = lax.all_to_all(sums, ('x', 'ylo'), 0, 0, tiled=True)  9.19 us
  transfers between devices with their start and end apart: 24, of which 15 were waited for; matrix products, arithmetic and copies ran while one was open for 4% of the time, Pallas kernels for 5%

profile of v5, /device:TPU:6, one launch (start us, length us, event | category | flops | bytes accessed | tf_op | source)
XLA Modules:
  0.0 251.2 jit_solution(14494322481586132199)
XLA Ops:
  0.6 2.3 shard_map.110
  2.9 19.5 %all_to_all.20 = bf16[16,17,512]{2,1,0:T(8,128)(2,1)S(1)} all-to-all(bf16[16,17,512]{2,1,0:T(8,128)(2,1)} %bitcast.31), channel_id=1, replica_groups=mesh['ylo'=2,'x'=4,'core'=2,'expert'=4,'tensor'=8] {'ylo','core','expert'}, dimensions={0} | all-to-all | bytes 557056 | tf_op jit(solution)/shard_map/all_to_all | solution.py:363
  22.6 18.5 %all_to_all.21 = bf16[4,272,512]{2,1,0:T(8,128)(2,1)S(1)} all-to-all(bf16[4,272,512]{2,1,0:T(8,128)(2,1)S(1)} %broadcast_in_dim.17), channel_id=1, replica_groups=mesh['ylo'=2,'x'=4,'core'=2,'expert'=4,'tensor'=8] {'x'}, dimensions={0} | all-to-all | bytes 2228224 | tf_op jit(solution)/shard_map/all_to_all | solution.py:374
  41.2 3.0 %collective-permute-start = (bf16[8,136,512]{2,1,0:T(8,128)(2,1)S(1)}, bf16[8,136,512]{2,1,0:T(8,128)(2,1)S(1)}, u32[]{:S(2)}, u32[]{:S(2)}) collective-permute-start(bf16[8,136,512]{2,1,0:T(8,128)(2,1)S(1)} %bitcast.22), channel_id=1, source_target_pairs={{0,32},{32,0},{1,33},{33,1},{2,34},{34,2},{3,35},{35,3},{4,36},{36... | collective-permute-start | bytes 3342344 | tf_op jit(solution)/shard_map/ppermute | solution.py:378
  47.4 4.6 %collective-permute-start.3 = (bf16[512,384]{1,0:T(8,128)(2,1)}, bf16[512,384]{1,0:T(8,128)(2,1)S(1)}, u32[]{:S(2)}, u32[]{:S(2)}) collective-permute-start(bf16[512,384]{1,0:T(8,128)(2,1)} %get-tuple-element.38), channel_id=1, source_target_pairs={{0,16},{8,24},{16,0},{24,8},{1,17},{9,25},{17,1},{25,9},{2,18},{10... | collective-permute-start | bytes 1179656 | tf_op jit(solution)/shard_map/ppermute | solution.py:369
  52.0 4.4 %collective-permute-start.1 = (bf16[512,384]{1,0:T(8,128)(2,1)}, bf16[512,384]{1,0:T(8,128)(2,1)S(1)}, u32[]{:S(2)}, u32[]{:S(2)}) collective-permute-start(bf16[512,384]{1,0:T(8,128)(2,1)} %get-tuple-element.35), channel_id=1, source_target_pairs={{0,8},{8,16},{16,24},{24,0},{1,9},{9,17},{17,25},{25,1},{2,10},{10... | collective-permute-start | bytes 1179656 | tf_op jit(solution)/shard_map/ppermute | solution.py:369
  56.4 3.5 %collective-permute-start.2 = (bf16[512,384]{1,0:T(8,128)(2,1)}, bf16[512,384]{1,0:T(8,128)(2,1)S(1)}, u32[]{:S(2)}, u32[]{:S(2)}) collective-permute-start(bf16[512,384]{1,0:T(8,128)(2,1)} %get-tuple-element.36), channel_id=1, source_target_pairs={{0,24},{8,0},{16,8},{24,16},{1,25},{9,1},{17,9},{25,17},{2,26},{10... | collective-permute-start | bytes 1179656 | tf_op jit(solution)/shard_map/ppermute | solution.py:369
  60.0 5.7 %collective-permute-done.3.refs_1_ = bf16[512,384]{1,0:T(8,128)(2,1)S(1)} collective-permute-done((bf16[512,384]{1,0:T(8,128)(2,1)}, bf16[512,384]{1,0:T(8,128)(2,1)S(1)}, u32[]{:S(2)}, u32[]{:S(2)}) %collective-permute-start.3) | collective-permute-done | bytes 393248 | tf_op jit(solution)/shard_map/ppermute | solution.py:369
  67.1 14.5 %collective-permute-done.1.refs_0_ = bf16[512,384]{1,0:T(8,128)(2,1)S(1)} collective-permute-done((bf16[512,384]{1,0:T(8,128)(2,1)}, bf16[512,384]{1,0:T(8,128)(2,1)S(1)}, u32[]{:S(2)}, u32[]{:S(2)}) %collective-permute-start.1) | collective-permute-done | bytes 393248 | tf_op jit(solution)/shard_map/ppermute | solution.py:369
  81.6 7.7 %collective-permute-done.2.refs_1_ = bf16[512,384]{1,0:T(8,128)(2,1)S(1)} collective-permute-done((bf16[512,384]{1,0:T(8,128)(2,1)}, bf16[512,384]{1,0:T(8,128)(2,1)S(1)}, u32[]{:S(2)}, u32[]{:S(2)}) %collective-permute-start.2) | collective-permute-done | bytes 393248 | tf_op jit(solution)/shard_map/ppermute | solution.py:369
  90.6 10.8 %collective-permute-start.8 = (bf16[88,1536]{1,0:T(8,128)(2,1)S(1)}, bf16[88,1536]{1,0:T(8,128)(2,1)S(1)}, u32[]{:S(2)}, u32[]{:S(2)}) collective-permute-start(bf16[88,1536]{1,0:T(8,128)(2,1)S(1)} %get-tuple-element.45), channel_id=1, source_target_pairs={{0,7},{1,0},{2,1},{3,2},{4,3},{5,4},{6,5},{7,6},{8,15},{9,8},{10,9... | collective-permute-start | bytes 811016 | tf_op jit(solution)/shard_map/ppermute | solution.py:385
  101.3 1.9 collective-permute-start.4
  104.7 5.2 %collective-permute-done.4.got_ref = bf16[48,1536]{1,0:T(8,128)(2,1)S(1)} collective-permute-done((bf16[48,1536]{1,0:T(8,128)(2,1)S(1)}, bf16[48,1536]{1,0:T(8,128)(2,1)S(1)}, u32[]{:S(2)}, u32[]{:S(2)}) %collective-permute-start.4) | collective-permute-done | bytes 147488 | tf_op jit(solution)/shard_map/ppermute | solution.py:385
  110.0 1.9 collective-permute-start.5
  112.0 5.1 %collective-permute-start.9 = (bf16[136,1536]{1,0:T(8,128)(2,1)S(1)}, bf16[136,1536]{1,0:T(8,128)(2,1)S(1)}, u32[]{:S(2)}, u32[]{:S(2)}) collective-permute-start(bf16[136,1536]{1,0:T(8,128)(2,1)S(1)} %shard_map.118), channel_id=1, source_target_pairs={{0,7},{1,0},{2,1},{3,2},{4,3},{5,4},{6,5},{7,6},{8,15},{9,8},{10,9... | collective-permute-start | bytes 1253384 | tf_op jit(solution)/shard_map/ppermute | solution.py:385
  117.1 2.8 %shard_map.114 = (bf16[136,1536]{1,0:T(8,128)(2,1)S(1)}, bf16[136,1536]{1,0:T(8,128)(2,1)S(1)}, bf16[136,1536]{1,0:T(8,128)(2,1)S(1)}, bf16[136,1536]{1,0:T(8,128)(2,1)S(1)}, bf16[136,1536]{1,0:T(8,128)(2,1)S(1)}) custom-call(s32[2]{0:T(128)S(1)} %pad_add_fusion.order_ref.where_ref, bf16[8,136,512]{2,1,0:T(8,128)(2,1)S(1)} %bitcast.25, ...), custom_call_target="tpu_custom_call" | custom-call | flops 1069547520 | bytes 5054464 | tf_op jit(solution)/shard_map/pallas_call | solution.py:171
  119.9 3.6 %collective-permute-done.5 = bf16[136,1536]{1,0:T(8,128)(2,1)S(1)} collective-permute-done((bf16[136,1536]{1,0:T(8,128)(2,1)S(1)}, bf16[136,1536]{1,0:T(8,128)(2,1)S(1)}, u32[]{:S(2)}, u32[]{:S(2)}) %collective-permute-start.5) | collective-permute-done | bytes 417824 | tf_op jit(solution)/shard_map/ppermute | solution.py:385
  123.7 1.9 collective-permute-start.6
  125.7 5.1 %collective-permute-start.10 = (bf16[136,1536]{1,0:T(8,128)(2,1)S(1)}, bf16[136,1536]{1,0:T(8,128)(2,1)S(1)}, u32[]{:S(2)}, u32[]{:S(2)}) collective-permute-start(bf16[136,1536]{1,0:T(8,128)(2,1)S(1)} %add.14), channel_id=1, source_target_pairs={{0,7},{1,0},{2,1},{3,2},{4,3},{5,4},{6,5},{7,6},{8,15},{9,8},{10,9... | collective-permute-start | bytes 1253384 | tf_op jit(solution)/shard_map/ppermute | solution.py:385
  130.9 5.5 %collective-permute-done.6 = bf16[136,1536]{1,0:T(8,128)(2,1)S(1)} collective-permute-done((bf16[136,1536]{1,0:T(8,128)(2,1)S(1)}, bf16[136,1536]{1,0:T(8,128)(2,1)S(1)}, u32[]{:S(2)}, u32[]{:S(2)}) %collective-permute-start.6) | collective-permute-done | bytes 417824 | tf_op jit(solution)/shard_map/ppermute | solution.py:385
  136.4 1.9 collective-permute-start.7
  138.5 5.1 %collective-permute-start.11 = (bf16[136,1536]{1,0:T(8,128)(2,1)S(1)}, bf16[136,1536]{1,0:T(8,128)(2,1)S(1)}, u32[]{:S(2)}, u32[]{:S(2)}) collective-permute-start(bf16[136,1536]{1,0:T(8,128)(2,1)S(1)} %add.15), channel_id=1, source_target_pairs={{0,7},{1,0},{2,1},{3,2},{4,3},{5,4},{6,5},{7,6},{8,15},{9,8},{10,9... | collective-permute-start | bytes 1253384 | tf_op jit(solution)/shard_map/ppermute | solution.py:385
  143.6 4.6 %collective-permute-done.7.b_ref = bf16[136,1536]{1,0:T(8,128)(2,1)S(1)} collective-permute-done((bf16[136,1536]{1,0:T(8,128)(2,1)S(1)}, bf16[136,1536]{1,0:T(8,128)(2,1)S(1)}, u32[]{:S(2)}, u32[]{:S(2)}) %collective-permute-start.7) | collective-permute-done | bytes 417824 | tf_op jit(solution)/shard_map/ppermute | solution.py:385
  149.8 1.9 collective-permute-start.12
  151.8 5.6 %collective-permute-start.15 = (bf16[136,1536]{1,0:T(8,128)(2,1)S(1)}, bf16[136,1536]{1,0:T(8,128)(2,1)S(1)}, u32[]{:S(2)}, u32[]{:S(2)}) collective-permute-start(bf16[136,1536]{1,0:T(8,128)(2,1)S(1)} %shard_map.119.refs_0_), channel_id=1, source_target_pairs={{0,7},{1,0},{2,1},{3,2},{4,3},{5,4},{6,5},{7,6},{8,15},{9,8},{10,9... | collective-permute-start | bytes 1253384 | tf_op jit(solution)/shard_map/ppermute | solution.py:385
  157.4 4.1 %collective-permute-done.12.refs_0_ = bf16[136,1536]{1,0:T(8,128)(2,1)S(1)} collective-permute-done((bf16[136,1536]{1,0:T(8,128)(2,1)S(1)}, bf16[136,1536]{1,0:T(8,128)(2,1)S(1)}, u32[]{:S(2)}, u32[]{:S(2)}) %collective-permute-start.12) | collective-permute-done | bytes 417824 | tf_op jit(solution)/shard_map/ppermute | solution.py:385
  161.5 1.9 collective-permute-start.13
  163.4 5.1 %collective-permute-start.16 = (bf16[136,1536]{1,0:T(8,128)(2,1)S(1)}, bf16[136,1536]{1,0:T(8,128)(2,1)S(1)}, u32[]{:S(2)}, u32[]{:S(2)}) collective-permute-start(bf16[136,1536]{1,0:T(8,128)(2,1)S(1)} %collective-permute-done.15.refs_1_), channel_id=1, source_target_pairs={{0,7},{1,0},{2,1},{3,2},{4,3},{5,4},{6,5},{7,6},{8,15},{9,8},{10,9... | collective-permute-start | bytes 1253384 | tf_op jit(solution)/shard_map/ppermute | solution.py:385
  168.5 4.3 %collective-permute-done.13.refs_0_ = bf16[136,1536]{1,0:T(8,128)(2,1)S(1)} collective-permute-done((bf16[136,1536]{1,0:T(8,128)(2,1)S(1)}, bf16[136,1536]{1,0:T(8,128)(2,1)S(1)}, u32[]{:S(2)}, u32[]{:S(2)}) %collective-permute-start.13) | collective-permute-done | bytes 417824 | tf_op jit(solution)/shard_map/ppermute | solution.py:385
  172.9 1.9 collective-permute-start.14
  174.8 5.4 %collective-permute-start.17 = (bf16[136,1536]{1,0:T(8,128)(2,1)S(1)}, bf16[136,1536]{1,0:T(8,128)(2,1)S(1)}, u32[]{:S(2)}, u32[]{:S(2)}) collective-permute-start(bf16[136,1536]{1,0:T(8,128)(2,1)S(1)} %collective-permute-done.16.refs_1_), channel_id=1, source_target_pairs={{0,7},{1,0},{2,1},{3,2},{4,3},{5,4},{6,5},{7,6},{8,15},{9,8},{10,9... | collective-permute-start | bytes 1253384 | tf_op jit(solution)/shard_map/ppermute | solution.py:385
  181.4 1.9 shard_map.121
  183.4 1.9 shard_map.122
  185.8 1.9 shard_map.123
  187.7 1.9 collective-permute-start.18
  189.6 5.6 %collective-permute-start.20 = (bf16[88,1536]{1,0:T(8,128)(2,1)S(1)}, bf16[88,1536]{1,0:T(8,128)(2,1)S(1)}, u32[]{:S(2)}, u32[]{:S(2)}) collective-permute-start(bf16[88,1536]{1,0:T(8,128)(2,1)S(1)} %slice.21), channel_id=1, source_target_pairs={{0,7},{1,0},{2,1},{3,2},{4,3},{5,4},{6,5},{7,6},{8,15},{9,8},{10,9... | collective-permute-start | bytes 811016 | tf_op jit(solution)/shard_map/ppermute | solution.py:385
  195.3 1.9 collective-permute-start.19
  197.2 7.1 %collective-permute-done.19.refs_0_ = bf16[48,1536]{1,0:T(8,128)(2,1)S(1)} collective-permute-done((bf16[48,1536]{1,0:T(8,128)(2,1)S(1)}, bf16[48,1536]{1,0:T(8,128)(2,1)S(1)}, u32[]{:S(2)}, u32[]{:S(2)}) %collective-permute-start.19) | collective-permute-done | bytes 147488 | tf_op jit(solution)/shard_map/ppermute | solution.py:385
  205.9 1.9 collective-permute-start.21
  209.2 2.2 shard_map.125
  211.5 6.2 %all-to-all-start.2 = ((bf16[8,136,512]{2,1,0:T(8,128)(2,1)}), bf16[8,136,512]{2,1,0:T(8,128)(2,1)}, u32[]{:S(2)}, u32[]{:S(2)}) async-start(bf16[8,136,512]{2,1,0:T(8,128)(2,1)} %shard_map.125), calls=%async_computation.2 | async-start | bytes 2228224 | tf_op jit(solution)/shard_map/all_to_all | solution.py:416
  217.7 2.7 %broadcast_select_fusion = (bf16[8,136,512]{2,1,0:T(8,128)(2,1)}, bf16[8,136,512]{2,1,0:T(8,128)(2,1)S(1)}) fusion(bf16[8,136,512]{2,1,0:T(8,128)(2,1)} %copy-done.1, bf16[8,136,512]{2,1,0:T(8,128)(2,1)} %bitcast.26, pred[]{:T(512)S(6)} %eq.4), kind=kLoop, calls=%fused_computation.9 | loop fusion | flops 1114112 | bytes 4456449 | tf_op jit(solution)/shard_map/jit(_where)/select_n | solution.py:433
  220.4 1.7 fusion.1
  223.7 9.2 %all-to-all-done.2.sums_ref = bf16[8,136,512]{2,1,0:T(8,128)(2,1)} async-done(((bf16[8,136,512]{2,1,0:T(8,128)(2,1)}), bf16[8,136,512]{2,1,0:T(8,128)(2,1)}, u32[]{:S(2)}, u32[]{:S(2)}) %all-to-all-start.2) | async-done | bytes 1114144 | tf_op jit(solution)/shard_map/all_to_all | solution.py:416
  232.9 3.3 %shard_map.126 = bf16[8,17,512]{2,1,0:T(8,128)(2,1)} custom-call(bf16[8,136,512]{2,1,0:T(8,128)(2,1)} %all-to-all-done.2.sums_ref), custom_call_target="tpu_custom_call" | custom-call | tf_op jit(solution)/shard_map/pallas_call | solution.py:418
  236.2 4.6 %all-to-all-start.3 = ((bf16[8,17,512]{2,1,0:T(8,128)(2,1)}), bf16[8,17,512]{2,1,0:T(8,128)(2,1)S(1)}, u32[]{:S(2)}, u32[]{:S(2)}) async-start(bf16[8,17,512]{2,1,0:T(8,128)(2,1)} %shard_map.126), calls=%async_computation.3 | async-start | bytes 393216 | tf_op jit(solution)/shard_map/all_to_all | solution.py:425
  240.8 2.9 %fusion.2 = bf16[1,512,512]{2,1,0:T(8,128)(2,1)} fusion(bf16[1088,512]{1,0:T(8,128)(2,1)} %bitcast.32, bf16[1088,1536]{1,0:T(8,128)(2,1)S(1)} %bitcast.21), kind=kOutput, calls=%fused_computation.5 | convolution fusion | flops 570687488 | bytes 2752512 | tf_op jit(solution)/shard_map/dot_general | solution.py:341
  243.7 5.9 %all-to-all-done.3.back_ref = bf16[8,17,512]{2,1,0:T(8,128)(2,1)S(1)} async-done(((bf16[8,17,512]{2,1,0:T(8,128)(2,1)}), bf16[8,17,512]{2,1,0:T(8,128)(2,1)S(1)}, u32[]{:S(2)}, u32[]{:S(2)}) %all-to-all-start.3) | async-done | bytes 139296 | tf_op jit(solution)/shard_map/all_to_all | solution.py:425
  (51 shorter events, 17.4 us)
Async XLA Ops:
  22.6 21.6 %copy-start.2 = (bf16[4,512,128]{2,1,0:T(8,128)(2,1)S(1)}, bf16[4,512,128]{2,1,0:T(8,128)(2,1)}, u32[]{:S(2)}) copy-start(bf16[4,512,128]{2,1,0:T(8,128)(2,1)} %refs_0_.1) | copy-start | bytes 1572868
  22.6 21.6 %copy-start.3 = (bf16[4,512,128]{2,1,0:T(8,128)(2,1)S(1)}, bf16[4,512,128]{2,1,0:T(8,128)(2,1)}, u32[]{:S(2)}) copy-start(bf16[4,512,128]{2,1,0:T(8,128)(2,1)} %refs_1_.1) | copy-start | bytes 1572868
  41.2 76.0 %copy-start = (bf16[4,272,512]{2,1,0:T(8,128)(2,1)}, bf16[4,272,512]{2,1,0:T(8,128)(2,1)S(1)}, u32[]{:S(2)}) copy-start(bf16[4,272,512]{2,1,0:T(8,128)(2,1)S(1)} %all_to_all.21) | copy-start | bytes 3342340
  41.2 48.4 %collective-permute-start = (bf16[8,136,512]{2,1,0:T(8,128)(2,1)S(1)}, bf16[8,136,512]{2,1,0:T(8,128)(2,1)S(1)}, u32[]{:S(2)}, u32[]{:S(2)}) collective-permute-start(bf16[8,136,512]{2,1,0:T(8,128)(2,1)S(1)} %bitcast.22), channel_id=1, source_target_pairs={{0,32},{32,0},{1,33},{33,1},{2,34},{34,2},{3,35},{35,3},{4,36},{36... | collective-permute-start | bytes 3342344 | tf_op jit(solution)/shard_map/ppermute | solution.py:378
  44.2 1.0 copy-start.4
  46.7 0.7 copy-start.5
  47.4 18.4 %collective-permute-start.3 = (bf16[512,384]{1,0:T(8,128)(2,1)}, bf16[512,384]{1,0:T(8,128)(2,1)S(1)}, u32[]{:S(2)}, u32[]{:S(2)}) collective-permute-start(bf16[512,384]{1,0:T(8,128)(2,1)} %get-tuple-element.38), channel_id=1, source_target_pairs={{0,16},{8,24},{16,0},{24,8},{1,17},{9,25},{17,1},{25,9},{2,18},{10... | collective-permute-start | bytes 1179656 | tf_op jit(solution)/shard_map/ppermute | solution.py:369
  52.0 29.6 %collective-permute-start.1 = (bf16[512,384]{1,0:T(8,128)(2,1)}, bf16[512,384]{1,0:T(8,128)(2,1)S(1)}, u32[]{:S(2)}, u32[]{:S(2)}) collective-permute-start(bf16[512,384]{1,0:T(8,128)(2,1)} %get-tuple-element.35), channel_id=1, source_target_pairs={{0,8},{8,16},{16,24},{24,0},{1,9},{9,17},{17,25},{25,1},{2,10},{10... | collective-permute-start | bytes 1179656 | tf_op jit(solution)/shard_map/ppermute | solution.py:369
  56.4 32.9 %collective-permute-start.2 = (bf16[512,384]{1,0:T(8,128)(2,1)}, bf16[512,384]{1,0:T(8,128)(2,1)S(1)}, u32[]{:S(2)}, u32[]{:S(2)}) collective-permute-start(bf16[512,384]{1,0:T(8,128)(2,1)} %get-tuple-element.36), channel_id=1, source_target_pairs={{0,24},{8,0},{16,8},{24,16},{1,25},{9,1},{17,9},{25,17},{2,26},{10... | collective-permute-start | bytes 1179656 | tf_op jit(solution)/shard_map/ppermute | solution.py:369
  65.8 1.0 copy-start.6
  89.6 27.5 %copy-start.1 = (bf16[8,136,512]{2,1,0:T(8,128)(2,1)}, bf16[8,136,512]{2,1,0:T(8,128)(2,1)S(1)}, u32[]{:S(2)}) copy-start(bf16[8,136,512]{2,1,0:T(8,128)(2,1)S(1)} %collective-permute-done.other_x_ref) | copy-start | bytes 3342340
  90.6 21.4 %collective-permute-start.8 = (bf16[88,1536]{1,0:T(8,128)(2,1)S(1)}, bf16[88,1536]{1,0:T(8,128)(2,1)S(1)}, u32[]{:S(2)}, u32[]{:S(2)}) collective-permute-start(bf16[88,1536]{1,0:T(8,128)(2,1)S(1)} %get-tuple-element.45), channel_id=1, source_target_pairs={{0,7},{1,0},{2,1},{3,2},{4,3},{5,4},{6,5},{7,6},{8,15},{9,8},{10,9... | collective-permute-start | bytes 811016 | tf_op jit(solution)/shard_map/ppermute | solution.py:385
  101.3 8.6 %collective-permute-start.4 = (bf16[48,1536]{1,0:T(8,128)(2,1)S(1)}, bf16[48,1536]{1,0:T(8,128)(2,1)S(1)}, u32[]{:S(2)}, u32[]{:S(2)}) collective-permute-start(bf16[48,1536]{1,0:T(8,128)(2,1)S(1)} %get-tuple-element.41), channel_id=1, source_target_pairs={{0,1},{1,2},{2,3},{3,4},{4,5},{5,6},{6,7},{7,0},{8,9},{9,10},{10,1... | collective-permute-start | bytes 442376 | tf_op jit(solution)/shard_map/ppermute | solution.py:385
  110.0 13.5 %collective-permute-start.5 = (bf16[136,1536]{1,0:T(8,128)(2,1)S(1)}, bf16[136,1536]{1,0:T(8,128)(2,1)S(1)}, u32[]{:S(2)}, u32[]{:S(2)}) collective-permute-start(bf16[136,1536]{1,0:T(8,128)(2,1)S(1)} %shard_map.117), channel_id=1, source_target_pairs={{0,1},{1,2},{2,3},{3,4},{4,5},{5,6},{6,7},{7,0},{8,9},{9,10},{10,1... | collective-permute-start | bytes 1253384 | tf_op jit(solution)/shard_map/ppermute | solution.py:385
  112.0 13.6 %collective-permute-start.9 = (bf16[136,1536]{1,0:T(8,128)(2,1)S(1)}, bf16[136,1536]{1,0:T(8,128)(2,1)S(1)}, u32[]{:S(2)}, u32[]{:S(2)}) collective-permute-start(bf16[136,1536]{1,0:T(8,128)(2,1)S(1)} %shard_map.118), channel_id=1, source_target_pairs={{0,7},{1,0},{2,1},{3,2},{4,3},{5,4},{6,5},{7,6},{8,15},{9,8},{10,9... | collective-permute-start | bytes 1253384 | tf_op jit(solution)/shard_map/ppermute | solution.py:385
  123.7 12.7 %collective-permute-start.6 = (bf16[136,1536]{1,0:T(8,128)(2,1)S(1)}, bf16[136,1536]{1,0:T(8,128)(2,1)S(1)}, u32[]{:S(2)}, u32[]{:S(2)}) collective-permute-start(bf16[136,1536]{1,0:T(8,128)(2,1)S(1)} %add.12), channel_id=1, source_target_pairs={{0,1},{1,2},{2,3},{3,4},{4,5},{5,6},{6,7},{7,0},{8,9},{9,10},{10,1... | collective-permute-start | bytes 1253384 | tf_op jit(solution)/shard_map/ppermute | solution.py:385
  125.7 12.7 %collective-permute-start.10 = (bf16[136,1536]{1,0:T(8,128)(2,1)S(1)}, bf16[136,1536]{1,0:T(8,128)(2,1)S(1)}, u32[]{:S(2)}, u32[]{:S(2)}) collective-permute-start(bf16[136,1536]{1,0:T(8,128)(2,1)S(1)} %add.14), channel_id=1, source_target_pairs={{0,7},{1,0},{2,1},{3,2},{4,3},{5,4},{6,5},{7,6},{8,15},{9,8},{10,9... | collective-permute-start | bytes 1253384 | tf_op jit(solution)/shard_map/ppermute | solution.py:385
  136.4 11.8 %collective-permute-start.7 = (bf16[136,1536]{1,0:T(8,128)(2,1)S(1)}, bf16[136,1536]{1,0:T(8,128)(2,1)S(1)}, u32[]{:S(2)}, u32[]{:S(2)}) collective-permute-start(bf16[136,1536]{1,0:T(8,128)(2,1)S(1)} %add.13), channel_id=1, source_target_pairs={{0,1},{1,2},{2,3},{3,4},{4,5},{5,6},{6,7},{7,0},{8,9},{9,10},{10,1... | collective-permute-start | bytes 1253384 | tf_op jit(solution)/shard_map/ppermute | solution.py:385
  138.5 11.1 %collective-permute-start.11 = (bf16[136,1536]{1,0:T(8,128)(2,1)S(1)}, bf16[136,1536]{1,0:T(8,128)(2,1)S(1)}, u32[]{:S(2)}, u32[]{:S(2)}) collective-permute-start(bf16[136,1536]{1,0:T(8,128)(2,1)S(1)} %add.15), channel_id=1, source_target_pairs={{0,7},{1,0},{2,1},{3,2},{4,3},{5,4},{6,5},{7,6},{8,15},{9,8},{10,9... | collective-permute-start | bytes 1253384 | tf_op jit(solution)/shard_map/ppermute | solution.py:385
  149.8 11.6 %collective-permute-start.12 = (bf16[136,1536]{1,0:T(8,128)(2,1)S(1)}, bf16[136,1536]{1,0:T(8,128)(2,1)S(1)}, u32[]{:S(2)}, u32[]{:S(2)}) collective-permute-start(bf16[136,1536]{1,0:T(8,128)(2,1)S(1)} %shard_map.119.refs_0_), channel_id=1, source_target_pairs={{0,1},{1,2},{2,3},{3,4},{4,5},{5,6},{6,7},{7,0},{8,9},{9,10},{10,1... | collective-permute-start | bytes 1253384 | tf_op jit(solution)/shard_map/ppermute | solution.py:385
  151.8 11.6 %collective-permute-start.15 = (bf16[136,1536]{1,0:T(8,128)(2,1)S(1)}, bf16[136,1536]{1,0:T(8,128)(2,1)S(1)}, u32[]{:S(2)}, u32[]{:S(2)}) collective-permute-start(bf16[136,1536]{1,0:T(8,128)(2,1)S(1)} %shard_map.119.refs_0_), channel_id=1, source_target_pairs={{0,7},{1,0},{2,1},{3,2},{4,3},{5,4},{6,5},{7,6},{8,15},{9,8},{10,9... | collective-permute-start | bytes 1253384 | tf_op jit(solution)/shard_map/ppermute | solution.py:385
  161.5 11.4 %collective-permute-start.13 = (bf16[136,1536]{1,0:T(8,128)(2,1)S(1)}, bf16[136,1536]{1,0:T(8,128)(2,1)S(1)}, u32[]{:S(2)}, u32[]{:S(2)}) collective-permute-start(bf16[136,1536]{1,0:T(8,128)(2,1)S(1)} %collective-permute-done.12.refs_0_), channel_id=1, source_target_pairs={{0,1},{1,2},{2,3},{3,4},{4,5},{5,6},{6,7},{7,0},{8,9},{9,10},{10,1... | collective-permute-start | bytes 1253384 | tf_op jit(solution)/shard_map/ppermute | solution.py:385
  163.4 11.4 %collective-permute-start.16 = (bf16[136,1536]{1,0:T(8,128)(2,1)S(1)}, bf16[136,1536]{1,0:T(8,128)(2,1)S(1)}, u32[]{:S(2)}, u32[]{:S(2)}) collective-permute-start(bf16[136,1536]{1,0:T(8,128)(2,1)S(1)} %collective-permute-done.15.refs_1_), channel_id=1, source_target_pairs={{0,7},{1,0},{2,1},{3,2},{4,3},{5,4},{6,5},{7,6},{8,15},{9,8},{10,9... | collective-permute-start | bytes 1253384 | tf_op jit(solution)/shard_map/ppermute | solution.py:385
  172.9 12.4 %collective-permute-start.14 = (bf16[136,1536]{1,0:T(8,128)(2,1)S(1)}, bf16[136,1536]{1,0:T(8,128)(2,1)S(1)}, u32[]{:S(2)}, u32[]{:S(2)}) collective-permute-start(bf16[136,1536]{1,0:T(8,128)(2,1)S(1)} %collective-permute-done.13.refs_0_), channel_id=1, source_target_pairs={{0,1},{1,2},{2,3},{3,4},{4,5},{5,6},{6,7},{7,0},{8,9},{9,10},{10,1... | collective-permute-start | bytes 1253384 | tf_op jit(solution)/shard_map/ppermute | solution.py:385
  174.8 11.0 %collective-permute-start.17 = (bf16[136,1536]{1,0:T(8,128)(2,1)S(1)}, bf16[136,1536]{1,0:T(8,128)(2,1)S(1)}, u32[]{:S(2)}, u32[]{:S(2)}) collective-permute-start(bf16[136,1536]{1,0:T(8,128)(2,1)S(1)} %collective-permute-done.16.refs_1_), channel_id=1, source_target_pairs={{0,7},{1,0},{2,1},{3,2},{4,3},{5,4},{6,5},{7,6},{8,15},{9,8},{10,9... | collective-permute-start | bytes 1253384 | tf_op jit(solution)/shard_map/ppermute | solution.py:385
  187.7 21.5 %collective-permute-start.18 = (bf16[8,136,512]{2,1,0:T(8,128)(2,1)S(1)}, bf16[8,136,512]{2,1,0:T(8,128)(2,1)S(1)}, u32[]{:S(2)}, u32[]{:S(2)}) collective-permute-start(bf16[8,136,512]{2,1,0:T(8,128)(2,1)S(1)} %get-tuple-element.58), channel_id=1, source_target_pairs={{0,32},{32,0},{1,33},{33,1},{2,34},{34,2},{3,35},{35,3},{4,36},{36... | collective-permute-start | bytes 3342344 | tf_op jit(solution)/shard_map/ppermute | solution.py:412
  189.6 14.7 %collective-permute-start.20 = (bf16[88,1536]{1,0:T(8,128)(2,1)S(1)}, bf16[88,1536]{1,0:T(8,128)(2,1)S(1)}, u32[]{:S(2)}, u32[]{:S(2)}) collective-permute-start(bf16[88,1536]{1,0:T(8,128)(2,1)S(1)} %slice.21), channel_id=1, source_target_pairs={{0,7},{1,0},{2,1},{3,2},{4,3},{5,4},{6,5},{7,6},{8,15},{9,8},{10,9... | collective-permute-start | bytes 811016 | tf_op jit(solution)/shard_map/ppermute | solution.py:385
  195.3 9.1 %collective-permute-start.19 = (bf16[48,1536]{1,0:T(8,128)(2,1)S(1)}, bf16[48,1536]{1,0:T(8,128)(2,1)S(1)}, u32[]{:S(2)}, u32[]{:S(2)}) collective-permute-start(bf16[48,1536]{1,0:T(8,128)(2,1)S(1)} %slice.20), channel_id=1, source_target_pairs={{0,1},{1,2},{2,3},{3,4},{4,5},{5,6},{6,7},{7,0},{8,9},{9,10},{10,1... | collective-permute-start | bytes 442376 | tf_op jit(solution)/shard_map/ppermute | solution.py:385
  205.9 3.3 %collective-permute-start.21 = (bf16[1,136,512]{2,1,0:T(8,128)(2,1)S(1)}, bf16[1,136,512]{2,1,0:T(8,128)(2,1)S(1)}, u32[]{:S(2)}, u32[]{:S(2)}) collective-permute-start(bf16[1,136,512]{2,1,0:T(8,128)(2,1)S(1)} %get-tuple-element.61), channel_id=1, source_target_pairs={{0,32},{32,0},{1,33},{33,1},{2,34},{34,2},{3,35},{35,3},{4,36},{36... | collective-permute-start | bytes 417800 | tf_op jit(solution)/shard_map/ppermute | solution.py:414
  211.5 21.4 %all-to-all-start.2 = ((bf16[8,136,512]{2,1,0:T(8,128)(2,1)}), bf16[8,136,512]{2,1,0:T(8,128)(2,1)}, u32[]{:S(2)}, u32[]{:S(2)}) async-start(bf16[8,136,512]{2,1,0:T(8,128)(2,1)} %shard_map.125), calls=%async_computation.2 | async-start | bytes 2228224 | tf_op jit(solution)/shard_map/all_to_all | solution.py:416
  236.2 13.5 %all-to-all-start.3 = ((bf16[8,17,512]{2,1,0:T(8,128)(2,1)}), bf16[8,17,512]{2,1,0:T(8,128)(2,1)S(1)}, u32[]{:S(2)}, u32[]{:S(2)}) async-start(bf16[8,17,512]{2,1,0:T(8,128)(2,1)} %shard_map.126), calls=%async_computation.3 | async-start | bytes 393216 | tf_op jit(solution)/shard_map/all_to_all | solution.py:425
  240.8 8.9 %copy-start.7 = (s32[28,2]{0,1:T(2,128)S(1)}, s32[28,2]{0,1:T(2,128)}, u32[]{:S(2)}) copy-start(s32[28,2]{0,1:T(2,128)} %param.8) | copy-start | bytes 676
  240.8 8.9 %copy-start.8 = (f32[28,2]{0,1:T(2,128)S(1)}, f32[28,2]{0,1:T(2,128)}, u32[]{:S(2)}) copy-start(f32[28,2]{0,1:T(2,128)} %param.9) | copy-start | bytes 676
